TPU v7x, 32 devices: a whole 2x2x4 slice. The times are simulated.
32 devices in a mesh: group: 2 (over y), seq: 16 (over z, x, core).
Axes of the slice: x: 2, y: 2, z: 4, core: 2. Of those that a mesh axis runs over, the one named last changes fastest.
Arguments:
- coarse_query: bfloat16 [1024, 3072], P(('group', 'seq')), parts along dimension 0, may hold values from -96 to 96
- coarse_key: bfloat16 [1024, 3072], P(('group', 'seq')), parts along dimension 0, may hold values from -12 to 12
- coarse_value: bfloat16 [1024, 3072], P(('group', 'seq')), parts along dimension 0, may hold values from -6 to 6
- fine_query: bfloat16 [4096, 3072], P(('group', 'seq')), parts along dimension 0, may hold values from -108 to 108
- fine_key: bfloat16 [4096, 3072], P(('group', 'seq')), parts along dimension 0, may hold values from -9 to 9
- fine_value: bfloat16 [4096, 3072], P(('group', 'seq')), parts along dimension 0, may hold values from -6 to 6
- head_reach: int32 [24], replicated, may hold values from 1 to 2, as said below
Outputs:
- fine_result: bfloat16 [4096, 3072], P(('group', 'seq')), parts along dimension 0
- cross_result: bfloat16 [4096, 3072], P(('group', 'seq')), parts along dimension 0
There are 2 independent parts, one for each index of `group`. A program takes and returns all parts, laid end to end along the dimension named above; an argument that names none is the same for every part. Nothing has to cross between parts.
Inputs may be any that keep to these rules, and one draw needn't show every extreme that they name: `head_reach`: each head reaches at least one frame; some head reaches 2 frames.
All inputs are finite; a program needn't handle non-finite values.
Results may differ from a plain program's by a relative error of at most 0.0054.
Values may be sent and summed in bfloat16 or wider, within the bound.
No kernel may reach another device: no remote copies, remote signals or barrier semaphores. Data moves between devices by JAX's collectives and lax.ppermute only.
A program may use at most 128 MiB of HBM per device.

v0:
```python
import math

import jax
import jax.numpy as jnp
from jax import lax
from jax.sharding import PartitionSpec as P

HD = 128
TT = 4
TH = 4
TW = 8
NT = 8
HALO_F = 2


masked_score = -1e30


def from_behind(value, axis, steps):
    count = lax.axis_size(axis)
    initial, last = (max(0, -steps), min(count, count - steps))
    return lax.ppermute(value, axis, [(source, source + steps) for source in range(initial, last)])


def softmax_rows(scores):
    largest = jnp.max(scores, axis=-1, keepdims=True)
    exponent = jnp.exp(scores - largest)
    return (exponent / jnp.sum(exponent, axis=-1, keepdims=True)).astype(jnp.bfloat16)


def attend_heads(query_rows, key_rows, value_rows, head_size, allowed, exactness):
    head_total = query_rows.shape[1] // head_size
    query_heads = query_rows.reshape(query_rows.shape[0], head_total, head_size)
    key_heads = key_rows.reshape(key_rows.shape[0], head_total, head_size)
    value_heads = value_rows.reshape(value_rows.shape[0], head_total, head_size)
    scores = jnp.einsum(
        "qhd,khd->hqk",
        query_heads,
        key_heads,
        preferred_element_type=jnp.float32,
        precision=exactness,
    ) * head_size ** (-0.5)
    if allowed is not None:
        scores = jnp.where(allowed, scores, masked_score)
    weights = softmax_rows(scores)
    blended = jnp.einsum(
        "hqk,khd->qhd",
        weights,
        value_heads,
        preferred_element_type=jnp.float32,
        precision=exactness,
    )
    return blended.reshape(query_rows.shape[0], head_total * head_size)


def into_slots(local_rows, blocks, groups):
    row_count, full_width = local_rows.shape
    shaped = local_rows.reshape(blocks, row_count // blocks, groups, full_width // groups)
    return shaped.transpose(0, 2, 1, 3).reshape(
        blocks * groups, row_count // blocks, full_width // groups
    )


def from_slots(slot_array, blocks, groups):
    row_count = slot_array.shape[1]
    group_width = slot_array.shape[2]
    shaped = slot_array.reshape(blocks, groups, row_count, group_width)
    return shaped.transpose(0, 2, 1, 3).reshape(blocks * row_count, groups * group_width)


def replicate_groups(local_rows, blocks, groups):
    row_count, full_width = local_rows.shape
    shaped = local_rows.reshape(row_count, groups, full_width // groups).transpose(1, 0, 2)
    widened = jnp.broadcast_to(shaped[None], (blocks, groups, row_count, full_width // groups))
    return widened.reshape(blocks * groups, row_count, full_width // groups)


def pool_frames(coarse_rows, group_cells):
    summed = jnp.sum(
        coarse_rows.reshape(-1, group_cells, coarse_rows.shape[1]).astype(jnp.float32), axis=1
    )
    return summed * group_cells ** (-0.5)


def group_attention(query_rows, key_rows, value_rows):
    pieces = []
    for head_index in range(query_rows.shape[1] // HD):
        lower = head_index * HD
        upper = lower + HD
        mixed_piece = attend_heads(
            query_rows[:, lower:upper],
            key_rows[:, lower:upper],
            value_rows[:, lower:upper],
            HD,
            None,
            None,
        )
        pieces.append(mixed_piece.astype(jnp.bfloat16))
    return jnp.concatenate(pieces, axis=1)


def shards(coarse_query, coarse_key, coarse_value, fine_query, fine_key, fine_value, head_reach):
    devices = lax.axis_size("seq")
    position = lax.axis_index("seq")
    model_width = coarse_query.shape[1]
    head_count = model_width // HD
    groups = math.gcd(head_count, devices)
    blocks = devices // groups
    group_width = model_width // groups
    fine_rows = fine_query.shape[0]
    plane_cells = TH * TW
    tiles_across = devices // NT
    time_tile = position // tiles_across
    group_cells = TH // 2 * (TW // 2)
    halo_rows = HALO_F * plane_cells
    exact = lax.Precision.HIGHEST
    query_send = into_slots(coarse_query, blocks, groups)
    key_send = replicate_groups(coarse_key, blocks, groups)
    value_send = replicate_groups(coarse_value, blocks, groups)
    fine_send = into_slots(fine_query, blocks, groups)
    query_slots, key_slots, value_slots, fine_slots = (
        lax.all_to_all(query_send, "seq", split_axis=0, concat_axis=0, tiled=True),
        lax.all_to_all(key_send, "seq", split_axis=0, concat_axis=0, tiled=True),
        lax.all_to_all(value_send, "seq", split_axis=0, concat_axis=0, tiled=True),
        lax.all_to_all(fine_send, "seq", split_axis=0, concat_axis=0, tiled=True),
    )
    key_flat = key_slots.reshape(-1, group_width)
    value_flat = value_slots.reshape(-1, group_width)
    attended = group_attention(query_slots.reshape(-1, group_width), key_flat, value_flat)
    pooled_key = pool_frames(key_flat, group_cells)
    pooled_value = pool_frames(value_flat, group_cells)
    crossed = attend_heads(
        fine_slots.reshape(-1, group_width), pooled_key, pooled_value, HD, None, exact
    ).astype(jnp.bfloat16)
    returned, cross_slots = (
        lax.all_to_all(
            attended.reshape(devices, -1, group_width),
            "seq",
            split_axis=0,
            concat_axis=0,
            tiled=True,
        ),
        lax.all_to_all(
            crossed.reshape(devices, -1, group_width),
            "seq",
            split_axis=0,
            concat_axis=0,
            tiled=True,
        ),
    )
    coarse_attention = from_slots(returned, blocks, groups)
    cross_result = from_slots(cross_slots, blocks, groups)
    before_key, before_value = from_behind(
        (fine_key[fine_rows - halo_rows :], fine_value[fine_rows - halo_rows :]),
        "seq",
        tiles_across,
    )
    after_key, after_value = from_behind(
        (fine_key[:halo_rows], fine_value[:halo_rows]), "seq", -tiles_across
    )
    window_key = jnp.concatenate([before_key, fine_key, after_key], axis=0)
    window_value = jnp.concatenate([before_value, fine_value, after_value], axis=0)
    query_frame = time_tile * TT + jnp.arange(fine_rows, dtype=jnp.int32) // plane_cells
    key_frame = (
        time_tile * TT
        - HALO_F
        + jnp.arange(fine_rows + 2 * halo_rows, dtype=jnp.int32) // plane_cells
    )
    distance = jnp.abs(query_frame[:, None] - key_frame[None, :])
    inside = (key_frame >= 0) & (key_frame < NT * TT)
    allowed = (distance[None, :, :] <= head_reach[:, None, None]) & inside[None, None, :]
    window_attention = attend_heads(fine_query, window_key, window_value, HD, allowed, None)
    half_height = TH // 2
    half_width = TW // 2
    spread = coarse_attention.reshape(TT, half_height, 1, half_width, 1, model_width)
    upsampled = jnp.broadcast_to(spread, (TT, half_height, 2, half_width, 2, model_width)).reshape(
        fine_rows, model_width
    )
    fine_result = (window_attention + upsampled.astype(jnp.float32)).astype(jnp.bfloat16)
    return (fine_result, cross_result)


def solution(mesh):
    in_specs = (
        P(("group", "seq"), None),
        P(("group", "seq"), None),
        P(("group", "seq"), None),
        P(("group", "seq"), None),
        P(("group", "seq"), None),
        P(("group", "seq"), None),
        P(),
    )
    out_specs = (P(("group", "seq"), None), P(("group", "seq"), None))
    return jax.shard_map(shards, mesh=mesh, in_specs=in_specs, out_specs=out_specs, check_vma=False)
```

profile of v0, /device:TPU:11, one launch (start us, length us, event | category | flops | bytes accessed | tf_op | source)
XLA Modules:
  0.0 147.0 jit_solution(1412274654744890279)
XLA Ops:
  0.6 2.1 %fusion.44 = (bf16[64,3072]{1,0:T(8,128)(2,1)}, bf16[64,3072]{1,0:T(8,128)(2,1)}) fusion(bf16[128,3072]{1,0:T(8,128)(2,1)} %param.11), kind=kLoop, calls=%fused_computation.77 | loop fusion | bytes 1572864 | tf_op jit(solution)/shard_map/slice | solution.py:154
  2.8 3.2 %collective-permute-start.2 = (bf16[64,3072]{1,0:T(8,128)(2,1)}, bf16[64,3072]{1,0:T(8,128)(2,1)}, u32[]{:S(2)}, u32[]{:S(2)}) collective-permute-start(bf16[64,3072]{1,0:T(8,128)(2,1)} %get-tuple-element.2), channel_id=1, source_target_pairs={{0,2},{1,3},{2,4},{3,5},{4,6},{5,7},{6,8},{7,9},{8,10},{9,11},{10,... | collective-permute-start | bytes 1179656 | tf_op jit(solution)/shard_map/ppermute | solution.py:22
  6.0 2.2 %collective-permute-start.3 = (bf16[64,3072]{1,0:T(8,128)(2,1)}, bf16[64,3072]{1,0:T(8,128)(2,1)}, u32[]{:S(2)}, u32[]{:S(2)}) collective-permute-start(bf16[64,3072]{1,0:T(8,128)(2,1)} %get-tuple-element.3), channel_id=1, source_target_pairs={{2,0},{3,1},{4,2},{5,3},{6,4},{7,5},{8,6},{9,7},{10,8},{11,9},{12,... | collective-permute-start | bytes 1179656 | tf_op jit(solution)/shard_map/ppermute | solution.py:22
  8.2 0.9 fusion.45
  9.1 4.1 %collective-permute-start = (bf16[64,3072]{1,0:T(8,128)(2,1)}, bf16[64,3072]{1,0:T(8,128)(2,1)}, u32[]{:S(2)}, u32[]{:S(2)}) collective-permute-start(bf16[64,3072]{1,0:T(8,128)(2,1)} %get-tuple-element.4), channel_id=1, source_target_pairs={{0,2},{1,3},{2,4},{3,5},{4,6},{5,7},{6,8},{7,9},{8,10},{9,11},{10,... | collective-permute-start | bytes 1179656 | tf_op jit(solution)/shard_map/ppermute | solution.py:22
  13.2 1.9 %collective-permute-start.1 = (bf16[64,3072]{1,0:T(8,128)(2,1)}, bf16[64,3072]{1,0:T(8,128)(2,1)}, u32[]{:S(2)}, u32[]{:S(2)}) collective-permute-start(bf16[64,3072]{1,0:T(8,128)(2,1)} %get-tuple-element.5), channel_id=1, source_target_pairs={{2,0},{3,1},{4,2},{5,3},{6,4},{7,5},{8,6},{9,7},{10,8},{11,9},{12,... | collective-permute-start | bytes 1179656 | tf_op jit(solution)/shard_map/ppermute | solution.py:22
  15.2 0.7 copy.74
  15.9 8.4 %all-to-all-start = ((bf16[16,16,384]{2,1,0:T(8,128)(2,1)}), bf16[16,16,384]{2,1,0:T(8,128)(2,1)}, u32[]{:S(2)}, u32[]{:S(2)}) async-start(bf16[16,16,384]{2,1,0:T(8,128)(2,1)} %bitcast.6), calls=%async_computation | async-start | bytes 393216 | tf_op jit(solution)/shard_map/all_to_all | solution.py:122
  24.4 0.8 subtract_abs_fusion
  25.4 0.9 copy-done
  26.2 0.4 copy.69
  26.7 1.0 copy.92
  27.7 1.0 copy.79
  28.7 13.1 %collective-permute-done = bf16[64,3072]{1,0:T(8,128)(2,1)} collective-permute-done((bf16[64,3072]{1,0:T(8,128)(2,1)}, bf16[64,3072]{1,0:T(8,128)(2,1)}, u32[]{:S(2)}, u32[]{:S(2)}) %collective-permute-start) | collective-permute-done | bytes 393248 | tf_op jit(solution)/shard_map/ppermute | solution.py:22
  41.8 1.2 pad_maximum_fusion
  43.1 1.6 %copy.67 = bf16[256,3072]{0,1:T(8,128)(2,1)} copy(bf16[256,3072]{1,0:T(8,128)(2,1)S(1)} %pad_maximum_fusion) | data formatting | bytes 3145728 | tf_op jit(solution)/shard_map/concatenate | solution.py:162
  44.6 1.4 copy.68
  46.0 1.4 copy.70
  47.4 0.8 broadcast_in_dim.10
  48.2 7.4 %all-to-all-start.1 = ((bf16[16,32,384]{2,1,0:T(8,128)(2,1)}), bf16[16,32,384]{2,1,0:T(8,128)(2,1)S(1)}, u32[]{:S(2)}, u32[]{:S(2)}) async-start(bf16[16,32,384]{2,1,0:T(8,128)(2,1)} %bitcast.9), calls=%async_computation.1 | async-start | bytes 786432 | tf_op jit(solution)/shard_map/all_to_all | solution.py:123
  55.6 2.1 %pad_maximum_fusion.1 = bf16[256,3072]{0,1:T(8,128)(2,1)} fusion(bf16[64,3072]{0,1:T(8,128)(2,1)S(1)} %copy.70, bf16[128,3072]{0,1:T(8,128)(2,1)S(1)} %copy.69, bf16[64,3072]{0,1:T(8,128)(2,1)S(1)} %copy.68), kind=kLoop, calls=%fused_computation.7 | loop fusion | flops 4718592 | bytes 3145728 | tf_op jit(solution)/shard_map/concatenate | solution.py:161
  57.7 5.0 %fusion.46 = (f32[24,128]{1,0:T(8,128)S(1)}, f32[24,128,256]{1,2,0:T(8,128)}) fusion(s32[128,256]{0,1:T(8,128)S(1)} %copy-done.6, s32[24]{0:T(128)S(1)} %copy-done.7, pred[256]{0:T(512)(128)(4,1)S(1)} %compare_and_fusion, bf16[256,24,128]{0,2,1:T(8,128)(2,1)} %bitcast.127, bf16[128,3072]{1,0:T(8,128)(2,1)} %param.10), kind=kOutput, calls=%fused_computation.79 | convolution fusion | flops 206045440 | bytes 5648736 | tf_op jit(solution)/shard_map/sub | solution.py:27
  62.7 3.7 %all-to-all-done.1 = bf16[16,32,384]{2,1,0:T(8,128)(2,1)S(1)} async-done(((bf16[16,32,384]{2,1,0:T(8,128)(2,1)}), bf16[16,32,384]{2,1,0:T(8,128)(2,1)S(1)}, u32[]{:S(2)}, u32[]{:S(2)}) %all-to-all-start.1) | async-done | bytes 393248 | tf_op jit(solution)/shard_map/all_to_all | solution.py:123
  66.4 0.8 broadcast_in_dim.11
  67.2 4.9 %all-to-all-start.2 = ((bf16[16,32,384]{2,1,0:T(8,128)(2,1)}), bf16[16,32,384]{2,1,0:T(8,128)(2,1)S(1)}, u32[]{:S(2)}, u32[]{:S(2)}) async-start(bf16[16,32,384]{2,1,0:T(8,128)(2,1)} %bitcast.12), calls=%async_computation.2 | async-start | bytes 786432 | tf_op jit(solution)/shard_map/all_to_all | solution.py:124
  72.1 1.1 fusion.51
  73.4 1.2 fusion.50
  74.8 8.0 %all-to-all-done.2 = bf16[16,32,384]{2,1,0:T(8,128)(2,1)S(1)} async-done(((bf16[16,32,384]{2,1,0:T(8,128)(2,1)}), bf16[16,32,384]{2,1,0:T(8,128)(2,1)S(1)}, u32[]{:S(2)}, u32[]{:S(2)}) %all-to-all-start.2) | async-done | bytes 393248 | tf_op jit(solution)/shard_map/all_to_all | solution.py:124
  82.8 5.0 %all-to-all-start.4 = ((bf16[16,64,384]{2,1,0:T(8,128)(2,1)}), bf16[16,64,384]{2,1,0:T(8,128)(2,1)S(1)}, u32[]{:S(2)}, u32[]{:S(2)}) async-start(bf16[16,64,384]{2,1,0:T(8,128)(2,1)} %bitcast.31), calls=%async_computation.4 | async-start | bytes 1572864 | tf_op jit(solution)/shard_map/all_to_all | solution.py:125
  87.8 1.1 fusion.49
  90.1 0.7 pad_maximum_fusion.2
  91.3 15.7 %all-to-all-done.4 = bf16[16,64,384]{2,1,0:T(8,128)(2,1)S(1)} async-done(((bf16[16,64,384]{2,1,0:T(8,128)(2,1)}), bf16[16,64,384]{2,1,0:T(8,128)(2,1)S(1)}, u32[]{:S(2)}, u32[]{:S(2)}) %all-to-all-start.4) | async-done | bytes 786464 | tf_op jit(solution)/shard_map/all_to_all | solution.py:125
  107.1 4.8 %all-to-all-start.3 = ((bf16[16,16,384]{2,1,0:T(8,128)(2,1)}), bf16[16,16,384]{2,1,0:T(8,128)(2,1)S(1)}, u32[]{:S(2)}, u32[]{:S(2)}) async-start(bf16[16,16,384]{2,1,0:T(8,128)(2,1)} %pad_maximum_fusion.2), calls=%async_computation.3 | async-start | bytes 393216 | tf_op jit(solution)/shard_map/all_to_all | solution.py:136
  112.1 0.9 fusion.10
  113.1 1.2 fusion.52
  114.3 0.8 fusion.12
  115.1 0.7 copy.83
  115.9 1.4 convert_element_type.139
  117.3 1.1 all-to-all-done.3
  118.4 6.6 %all-to-all-start.5 = ((bf16[16,64,384]{2,1,0:T(8,128)(2,1)}), bf16[16,64,384]{2,1,0:T(8,128)(2,1)}, u32[]{:S(2)}, u32[]{:S(2)}) async-start(bf16[16,64,384]{2,1,0:T(8,128)(2,1)} %convert_element_type.139), calls=%async_computation.5 | async-start | bytes 1572864 | tf_op jit(solution)/shard_map/all_to_all | solution.py:143
  125.0 2.5 %fusion.7 = f32[24,128,128]{2,1,0:T(8,128)S(1)} fusion(bf16[256,24,128]{0,2,1:T(8,128)(2,1)S(1)} %bitcast.121, f32[24,128,256]{1,2,0:T(8,128)} %get-tuple-element.7, f32[24,128]{1,0:T(8,128)S(1)} %get-tuple-element.6), kind=kOutput, calls=%fused_computation.13 | convolution fusion | flops 202899456 | bytes 6303744 | tf_op jit(solution)/shard_map/hqk,khd->qhd/dot_general | solution.py:46
  127.5 0.5 copy.78
  128.2 1.8 %broadcast_in_dim.12 = f32[4,2,2,4,2,3072]{5,4,3,2,1,0:T(2,128)} broadcast(f32[4,2,4,3072]{3,2,1,0:T(4,128)S(1)} %reshape.276), dimensions={0,1,3,5} | broadcast | bytes 1966080 | tf_op jit(solution)/shard_map/broadcast_in_dim | solution.py:176
  130.0 2.4 %convert_element_type.130 = f32[128,3072]{1,0:T(8,128)S(1)} reshape(f32[4,2,2,4,2,3072]{5,4,3,2,1,0:T(2,128)} %broadcast_in_dim.12) | data formatting | bytes 3145728 | tf_op jit(solution)/shard_map/convert_element_type | solution.py:179
  132.4 1.0 add_convert_fusion
  133.4 10.9 %all-to-all-done.5 = bf16[16,64,384]{2,1,0:T(8,128)(2,1)} async-done(((bf16[16,64,384]{2,1,0:T(8,128)(2,1)}), bf16[16,64,384]{2,1,0:T(8,128)(2,1)}, u32[]{:S(2)}, u32[]{:S(2)}) %all-to-all-start.5) | async-done | bytes 786464 | tf_op jit(solution)/shard_map/all_to_all | solution.py:143
  144.4 1.6 %copy.84 = bf16[2,64,8,384]{3,2,1,0:T(8,128)(2,1)S(1)} copy(bf16[2,64,8,384]{3,1,2,0:T(8,128)(2,1)} %bitcast.35) | data formatting | bytes 1572864 | tf_op jit(solution)/shard_map/transpose | solution.py:68
  145.9 1.0 copy.94
  (41 shorter events, 3.0 us)
Async XLA Ops:
  0.6 7.6 %copy-start.1 = (bf16[128,3072]{1,0:T(8,128)(2,1)S(1)}, bf16[128,3072]{1,0:T(8,128)(2,1)}, u32[]{:S(2)}) copy-start(bf16[128,3072]{1,0:T(8,128)(2,1)} %param.12) | copy-start | bytes 2359300
  0.6 14.5 %copy-start.4 = (bf16[32,3072]{1,0:T(8,128)(2,1)S(1)}, bf16[32,3072]{1,0:T(8,128)(2,1)}, u32[]{:S(2)}) copy-start(bf16[32,3072]{1,0:T(8,128)(2,1)} %param.7) | copy-start | bytes 589828
  2.8 41.9 %collective-permute-start.2 = (bf16[64,3072]{1,0:T(8,128)(2,1)}, bf16[64,3072]{1,0:T(8,128)(2,1)}, u32[]{:S(2)}, u32[]{:S(2)}) collective-permute-start(bf16[64,3072]{1,0:T(8,128)(2,1)} %get-tuple-element.2), channel_id=1, source_target_pairs={{0,2},{1,3},{2,4},{3,5},{4,6},{5,7},{6,8},{7,9},{8,10},{9,11},{10,... | collective-permute-start | bytes 1179656 | tf_op jit(solution)/shard_map/ppermute | solution.py:22
  6.0 19.2 %copy-start.3 = (bf16[128,3072]{1,0:T(8,128)(2,1)S(1)}, bf16[128,3072]{1,0:T(8,128)(2,1)}, u32[]{:S(2)}) copy-start(bf16[128,3072]{1,0:T(8,128)(2,1)} %param.10) | copy-start | bytes 2359300
  6.0 40.0 %collective-permute-start.3 = (bf16[64,3072]{1,0:T(8,128)(2,1)}, bf16[64,3072]{1,0:T(8,128)(2,1)}, u32[]{:S(2)}, u32[]{:S(2)}) collective-permute-start(bf16[64,3072]{1,0:T(8,128)(2,1)} %get-tuple-element.3), channel_id=1, source_target_pairs={{2,0},{3,1},{4,2},{5,3},{6,4},{7,5},{8,6},{9,7},{10,8},{11,9},{12,... | collective-permute-start | bytes 1179656 | tf_op jit(solution)/shard_map/ppermute | solution.py:22
  9.1 32.7 %collective-permute-start = (bf16[64,3072]{1,0:T(8,128)(2,1)}, bf16[64,3072]{1,0:T(8,128)(2,1)}, u32[]{:S(2)}, u32[]{:S(2)}) collective-permute-start(bf16[64,3072]{1,0:T(8,128)(2,1)} %get-tuple-element.4), channel_id=1, source_target_pairs={{0,2},{1,3},{2,4},{3,5},{4,6},{5,7},{6,8},{7,9},{8,10},{9,11},{10,... | collective-permute-start | bytes 1179656 | tf_op jit(solution)/shard_map/ppermute | solution.py:22
  13.2 28.6 %collective-permute-start.1 = (bf16[64,3072]{1,0:T(8,128)(2,1)}, bf16[64,3072]{1,0:T(8,128)(2,1)}, u32[]{:S(2)}, u32[]{:S(2)}) collective-permute-start(bf16[64,3072]{1,0:T(8,128)(2,1)} %get-tuple-element.5), channel_id=1, source_target_pairs={{2,0},{3,1},{4,2},{5,3},{6,4},{7,5},{8,6},{9,7},{10,8},{11,9},{12,... | collective-permute-start | bytes 1179656 | tf_op jit(solution)/shard_map/ppermute | solution.py:22
  15.9 31.5 %all-to-all-start = ((bf16[16,16,384]{2,1,0:T(8,128)(2,1)}), bf16[16,16,384]{2,1,0:T(8,128)(2,1)}, u32[]{:S(2)}, u32[]{:S(2)}) async-start(bf16[16,16,384]{2,1,0:T(8,128)(2,1)} %bitcast.6), calls=%async_computation | async-start | bytes 393216 | tf_op jit(solution)/shard_map/all_to_all | solution.py:122
  25.1 1.1 copy-start
  25.3 1.4 copy-start.5
  48.2 18.2 %all-to-all-start.1 = ((bf16[16,32,384]{2,1,0:T(8,128)(2,1)}), bf16[16,32,384]{2,1,0:T(8,128)(2,1)S(1)}, u32[]{:S(2)}, u32[]{:S(2)}) async-start(bf16[16,32,384]{2,1,0:T(8,128)(2,1)} %bitcast.9), calls=%async_computation.1 | async-start | bytes 786432 | tf_op jit(solution)/shard_map/all_to_all | solution.py:123
  55.6 2.1 %copy-start.6 = (s32[128,256]{0,1:T(8,128)S(1)}, s32[128,256]{0,1:T(8,128)}, u32[]{:S(2)}) copy-start(s32[128,256]{0,1:T(8,128)} %subtract_abs_fusion) | copy-start | bytes 393220
  55.6 2.1 %copy-start.7 = (s32[24]{0:T(128)S(1)}, s32[24]{0:T(128)}, u32[]{:S(2)}) copy-start(s32[24]{0:T(128)} %param.13) | copy-start | bytes 292
  67.2 15.7 %all-to-all-start.2 = ((bf16[16,32,384]{2,1,0:T(8,128)(2,1)}), bf16[16,32,384]{2,1,0:T(8,128)(2,1)S(1)}, u32[]{:S(2)}, u32[]{:S(2)}) async-start(bf16[16,32,384]{2,1,0:T(8,128)(2,1)} %bitcast.12), calls=%async_computation.2 | async-start | bytes 786432 | tf_op jit(solution)/shard_map/all_to_all | solution.py:124
  82.8 24.2 %all-to-all-start.4 = ((bf16[16,64,384]{2,1,0:T(8,128)(2,1)}), bf16[16,64,384]{2,1,0:T(8,128)(2,1)S(1)}, u32[]{:S(2)}, u32[]{:S(2)}) async-start(bf16[16,64,384]{2,1,0:T(8,128)(2,1)} %bitcast.31), calls=%async_computation.4 | async-start | bytes 1572864 | tf_op jit(solution)/shard_map/all_to_all | solution.py:125
  107.1 11.4 %all-to-all-start.3 = ((bf16[16,16,384]{2,1,0:T(8,128)(2,1)}), bf16[16,16,384]{2,1,0:T(8,128)(2,1)S(1)}, u32[]{:S(2)}, u32[]{:S(2)}) async-start(bf16[16,16,384]{2,1,0:T(8,128)(2,1)} %pad_maximum_fusion.2), calls=%async_computation.3 | async-start | bytes 393216 | tf_op jit(solution)/shard_map/all_to_all | solution.py:136
  115.9 9.1 %copy-start.2 = (bf16[256,3072]{0,1:T(8,128)(2,1)S(1)}, bf16[256,3072]{0,1:T(8,128)(2,1)}, u32[]{:S(2)}) copy-start(bf16[256,3072]{0,1:T(8,128)(2,1)} %copy.67) | copy-start | bytes 4718596
  118.4 25.9 %all-to-all-start.5 = ((bf16[16,64,384]{2,1,0:T(8,128)(2,1)}), bf16[16,64,384]{2,1,0:T(8,128)(2,1)}, u32[]{:S(2)}, u32[]{:S(2)}) async-start(bf16[16,64,384]{2,1,0:T(8,128)(2,1)} %convert_element_type.139), calls=%async_computation.5 | async-start | bytes 1572864 | tf_op jit(solution)/shard_map/all_to_all | solution.py:143
where the time goes:
time: 149 us; the launch traced here: 147 us
  waiting for transfers between devices  52.6 us (35%)
  starting transfers between devices  48.5 us (33%)
  local copies, waits for them, and re-layouts  23.1 us (16%)
  matrix products  13.6 us (9%)
  other arithmetic  8.25 us (6%)
    all_to_all x1, waiting for transfers between devices, shards(): lax.all_to_all(fine_send, 'seq', split_axis=0, concat_axis=0, tiled=True)  15.7 us
    ppermute x4, waiting for transfers between devices, from_behind(): lax.ppermute(value, axis, [(source, source + steps) for source in range(i...  13.1 us
    ppermute x4, starting transfers between devices, from_behind(): lax.ppermute(value, axis, [(source, source + steps) for source in range(i...  11.4 us
    all_to_all x1, waiting for transfers between devices, shards(): lax.all_to_all(crossed.reshape(devices, -1, group_width), 'seq', split_ax...  10.9 us
    all_to_all x1, starting transfers between devices, shards(): lax.all_to_all(query_send, 'seq', split_axis=0, concat_axis=0, tiled=True)  8.42 us
    all_to_all x1, waiting for transfers between devices, shards(): lax.all_to_all(value_send, 'seq', split_axis=0, concat_axis=0, tiled=True)  8.02 us
    all_to_all x1, starting transfers between devices, shards(): lax.all_to_all(key_send, 'seq', split_axis=0, concat_axis=0, tiled=True)  7.44 us
    all_to_all x1, starting transfers between devices, shards(): lax.all_to_all(crossed.reshape(devices, -1, group_width), 'seq', split_ax...  6.57 us
  transfers between devices with their start and end apart: 10, of which 6 were waited for; matrix products, arithmetic and copies ran while one was open for 26% of the time, Pallas kernels for 0%

commit v1 on v0

v1 whole, which is shorter than its diff:
```python
import functools
import math

import jax
import jax.numpy as jnp
from jax import lax
from jax.experimental import pallas as pl
from jax.experimental.pallas import tpu as pltpu
from jax.sharding import PartitionSpec as P

HD = 128
TT = 4
TH = 4
TW = 8
NT = 8
HALO_F = 2

PLANE = TH * TW
CELLS = (TH // 2) * (TW // 2)
SCALE = HD**-0.5
MASKED = -1e30
FAR = 1 << 20

VMEM = pl.BlockSpec(memory_space=pltpu.VMEM)
SMEM = pl.BlockSpec(memory_space=pltpu.SMEM)


def softmax_rows(scores):
    exponent = jnp.exp(scores - jnp.max(scores, axis=-1, keepdims=True))
    return (exponent / jnp.sum(exponent, axis=-1, keepdims=True)).astype(jnp.bfloat16)


def dot_rows(left, right):
    return lax.dot_general(left, right, (((1,), (1,)), ((), ())), preferred_element_type=jnp.float32)


def dot_plain(left, right):
    return lax.dot_general(left, right, (((1,), (0,)), ((), ())), preferred_element_type=jnp.float32)


def halo_kernel(place, key_ref, value_ref, out_ref):
    rows = key_ref.shape[0]
    out_ref[:rows] = key_ref[...]
    out_ref[rows:] = value_ref[...]


def pack_halo(place, fine_key, fine_value, which):
    rows, width = fine_key.shape
    edge = HALO_F * PLANE
    half = rows // edge - 1
    columns = 768
    edge_spec = pl.BlockSpec((edge, columns), lambda c, p: (p[which] * half, c))
    return pl.pallas_call(
        halo_kernel,
        out_shape=jax.ShapeDtypeStruct((2 * edge, width), fine_key.dtype),
        grid_spec=pltpu.PrefetchScalarGridSpec(
            num_scalar_prefetch=1,
            grid=(width // columns,),
            in_specs=[edge_spec, edge_spec],
            out_specs=pl.BlockSpec((2 * edge, columns), lambda c, p: (0, c)),
        ),
        name="pack_halo",
    )(place, fine_key, fine_value)


def pool_rows(rows):
    cells = rows.astype(jnp.float32).reshape(-1, CELLS, rows.shape[1])
    return jnp.sum(cells, axis=1) * CELLS**-0.5


def coarse_pack_kernel(query_ref, key_ref, value_ref, out_ref, pooled_ref):
    rows = query_ref.shape[0]
    for index, ref in enumerate((query_ref, key_ref, value_ref)):
        out_ref[0, index * rows : (index + 1) * rows] = ref[...]
    pooled_ref[:TT] = pool_rows(key_ref[...])
    pooled_ref[TT:] = pool_rows(value_ref[...])


def pack_coarse(coarse_query, coarse_key, coarse_value, groups):
    rows, width = coarse_query.shape
    group_width = width // groups
    column = pl.BlockSpec((rows, group_width), lambda g: (0, g))
    return pl.pallas_call(
        coarse_pack_kernel,
        out_shape=(
            jax.ShapeDtypeStruct((groups, 3 * rows, group_width), coarse_query.dtype),
            jax.ShapeDtypeStruct((2 * TT, width), jnp.float32),
        ),
        grid=(groups,),
        in_specs=[column, column, column],
        out_specs=(
            pl.BlockSpec((1, 3 * rows, group_width), lambda g: (g, 0, 0)),
            pl.BlockSpec((2 * TT, group_width), lambda g: (0, g)),
        ),
        name="pack_coarse",
    )(coarse_query, coarse_key, coarse_value)


def split_pooled_kernel(*refs):
    *in_refs, out_ref = refs
    keys = jnp.concatenate([ref[:TT] for ref in in_refs], axis=0)
    values = jnp.concatenate([ref[TT:] for ref in in_refs], axis=0)
    count = keys.shape[0]
    high = keys.astype(jnp.bfloat16).astype(jnp.float32)
    low = keys - high
    out_ref[...] = jnp.concatenate([high, low, values], axis=0).astype(jnp.bfloat16)


def split_pooled(pieces):
    width = pieces[0].shape[1]
    return pl.pallas_call(
        split_pooled_kernel,
        out_shape=jax.ShapeDtypeStruct((3 * TT * len(pieces), width), jnp.bfloat16),
        in_specs=[VMEM] * len(pieces),
        out_specs=VMEM,
        name="split_pooled",
    )(*pieces)


def coarse_kernel(own_ref, *refs):
    *other_refs, out_ref = refs
    members, packed, _ = own_ref.shape
    rows = packed // 3

    def flat(ref, start):
        piece = ref[:, start : start + rows]
        return piece.reshape(members * rows, HD)

    query = flat(own_ref, 0)
    keys = jnp.concatenate([flat(own_ref, rows)] + [flat(r, 0) for r in other_refs], axis=0)
    values = jnp.concatenate([flat(own_ref, 2 * rows)] + [flat(r, rows) for r in other_refs], axis=0)
    weights = softmax_rows(dot_rows(query, keys) * SCALE)
    mixed = dot_plain(weights, values)
    out_ref[...] = mixed.astype(out_ref.dtype).reshape(members, rows, HD)


def attend_coarse(own, others):
    members, packed, group_width = own.shape
    rows = packed // 3
    return pl.pallas_call(
        coarse_kernel,
        out_shape=jax.ShapeDtypeStruct((members, rows, group_width), own.dtype),
        grid=(group_width // HD,),
        in_specs=[pl.BlockSpec((members, packed, HD), lambda h: (0, 0, h))]
        + [pl.BlockSpec((members, 2 * rows, HD), lambda h: (0, 0, h)) for _ in others],
        out_specs=pl.BlockSpec((members, rows, HD), lambda h: (0, 0, h)),
        name="attend_coarse",
    )(own, *others)


def cross_kernel(chunk, query_ref, *refs):
    *token_refs, out_ref = refs
    third = chunk // 3
    high, low, values = [], [], []
    for ref in token_refs:
        rows = ref[...].astype(jnp.float32)
        for start in range(0, rows.shape[0], chunk):
            high.append(rows[start : start + third])
            low.append(rows[start + third : start + 2 * third])
            values.append(rows[start + 2 * third : start + chunk])
    high = jnp.concatenate(high, axis=0).astype(jnp.bfloat16)
    low = jnp.concatenate(low, axis=0).astype(jnp.bfloat16)
    values = jnp.concatenate(values, axis=0).astype(jnp.bfloat16)
    for head in range(query_ref.shape[1] // HD):
        cut = slice(head * HD, (head + 1) * HD)
        query = query_ref[:, cut]
        scores = dot_rows(
            jnp.concatenate([query, query], axis=1),
            jnp.concatenate([high[:, cut], low[:, cut]], axis=1),
        )
        weights = softmax_rows(scores * SCALE)
        out_ref[:, cut] = dot_plain(weights, values[:, cut]).astype(out_ref.dtype)


def attend_cross(fine_query, tokens, chunk, heads_at_once):
    rows, width = fine_query.shape
    columns = heads_at_once * HD
    return pl.pallas_call(
        functools.partial(cross_kernel, chunk),
        out_shape=jax.ShapeDtypeStruct((rows, width), jnp.bfloat16),
        grid=(width // columns,),
        in_specs=[pl.BlockSpec((rows, columns), lambda c: (0, c))]
        + [pl.BlockSpec((t.shape[0], columns), lambda c: (0, c)) for t in tokens],
        out_specs=pl.BlockSpec((rows, columns), lambda c: (0, c)),
        name="attend_cross",
    )(fine_query, *tokens)


def window_kernel(place, reach, query_ref, key_ref, value_ref, pair_ref, next_ref, out_ref):
    rows, columns = query_ref.shape
    edge = HALO_F * PLANE
    total = rows + 2 * edge
    time_tile = place[2]
    later = time_tile % 2 == 0
    row_frame = lax.broadcasted_iota(jnp.int32, (rows, total), 0) // PLANE
    column = lax.broadcasted_iota(jnp.int32, (rows, total), 1)
    own_frame = column // PLANE
    pair_frame = (column - rows) // PLANE + jnp.where(later, TT, -HALO_F)
    next_frame = (column - rows - edge) // PLANE + jnp.where(later, -HALO_F, TT)
    key_frame = jnp.where(column < rows, own_frame, jnp.where(column < rows + edge, pair_frame, next_frame))
    distance = jnp.abs(row_frame - key_frame)
    absolute = key_frame + time_tile * TT
    distance = jnp.where((absolute >= 0) & (absolute < NT * TT), distance, FAR)
    first_head = pl.program_id(0) * (columns // HD)
    for head in range(columns // HD):
        cut = slice(head * HD, (head + 1) * HD)
        keys = jnp.concatenate([key_ref[:, cut], pair_ref[:edge, cut], next_ref[:edge, cut]], axis=0)
        values = jnp.concatenate([value_ref[:, cut], pair_ref[edge:, cut], next_ref[edge:, cut]], axis=0)
        scores = dot_rows(query_ref[:, cut], keys) * SCALE
        scores = jnp.where(distance <= reach[first_head + head], scores, MASKED)
        out_ref[:, cut] = dot_plain(softmax_rows(scores), values)


def attend_window(place, head_reach, fine_query, fine_key, fine_value, pair, beyond, heads_at_once):
    rows, width = fine_query.shape
    columns = heads_at_once * HD
    block = pl.BlockSpec((rows, columns), lambda c, p, r: (0, c))
    halo = pl.BlockSpec((pair.shape[0], columns), lambda c, p, r: (0, c))
    return pl.pallas_call(
        window_kernel,
        out_shape=jax.ShapeDtypeStruct((rows, width), jnp.float32),
        grid_spec=pltpu.PrefetchScalarGridSpec(
            num_scalar_prefetch=2,
            grid=(width // columns,),
            in_specs=[block, block, block, halo, halo],
            out_specs=block,
        ),
        name="attend_window",
    )(place, head_reach, fine_query, fine_key, fine_value, pair, beyond)


def finish_kernel(window_ref, coarse_ref, out_ref):
    rows = window_ref.shape[0]
    coarse_rows = coarse_ref.shape[1]
    row = lax.broadcasted_iota(jnp.int32, (rows, coarse_rows), 0)
    column = lax.broadcasted_iota(jnp.int32, (rows, coarse_rows), 1)
    frame, y, x = row // PLANE, (row % PLANE) // TW, row % TW
    source = frame * CELLS + (y // 2) * (TW // 2) + x // 2
    pick = (source == column).astype(jnp.bfloat16)
    upsampled = dot_plain(pick, coarse_ref[0])
    out_ref[...] = (window_ref[...] + upsampled).astype(out_ref.dtype)


def finish(window, returned):
    rows, width = window.shape
    groups, coarse_rows, group_width = returned.shape
    block = pl.BlockSpec((rows, group_width), lambda g: (0, g))
    return pl.pallas_call(
        finish_kernel,
        out_shape=jax.ShapeDtypeStruct((rows, width), jnp.bfloat16),
        grid=(groups,),
        in_specs=[block, pl.BlockSpec((1, coarse_rows, group_width), lambda g: (g, 0, 0))],
        out_specs=block,
        name="finish",
    )(window, returned)


def shards(coarse_query, coarse_key, coarse_value, fine_query, fine_key, fine_value, head_reach):
    devices = lax.axis_size("seq")
    position = lax.axis_index("seq")
    head_count = coarse_query.shape[1] // HD
    groups = math.gcd(head_count, devices)
    blocks = devices // groups
    inner = math.gcd(2, groups)
    outer = groups // inner
    tiles_across = devices // NT
    time_tile = position // tiles_across

    def seat(o, b, c):
        return (o * blocks + b) * inner + c

    def around(value, extent, move):
        moved = []
        for step in range(1, extent):
            links = [
                (seat(o, b, c), seat(*move(o, b, c, step)))
                for o in range(outer)
                for b in range(blocks)
                for c in range(inner)
            ]
            moved.append(lax.ppermute(value, "seq", links))
        return moved

    over_blocks = functools.partial(around, extent=blocks, move=lambda o, b, c, s: (o, (b + s) % blocks, c))
    over_outer = functools.partial(around, extent=outer, move=lambda o, b, c, s: ((o + s) % outer, b, c))
    over_inner = functools.partial(around, extent=inner, move=lambda o, b, c, s: (o, b, (c + s) % inner))
    same_block = [[seat(o, b, c) for o in range(outer) for c in range(inner)] for b in range(blocks)]

    def exchange(slots):
        return lax.all_to_all(slots, "seq", 0, 0, tiled=True, axis_index_groups=same_block)

    odd = time_tile % 2
    place = jnp.stack([1 - odd, odd, time_tile]).astype(jnp.int32)
    pairs = [(j, j + tiles_across) for j in range(devices - tiles_across)]
    early = [(a, b) for a, b in pairs if (a // tiles_across) % 2 == 0]
    late = [(a, b) for a, b in pairs if (a // tiles_across) % 2 == 1]

    def swap(value, links):
        return lax.ppermute(value, "seq", links + [(b, a) for a, b in links])

    pair = swap(pack_halo(place, fine_key, fine_value, 0), early)
    slots, pooled = pack_coarse(coarse_query, coarse_key, coarse_value, groups)
    received = exchange(slots)
    beyond = swap(pack_halo(place, fine_key, fine_value, 1), late)
    token_part = split_pooled([pooled] + over_blocks(pooled))
    tokens = jnp.concatenate([token_part] + over_outer(token_part), axis=0)
    all_tokens = [tokens] + over_inner(tokens)
    coarse_rows = coarse_query.shape[0]
    attended = attend_coarse(received, over_blocks(received[:, coarse_rows:]))
    returned = exchange(attended)
    cross_result = attend_cross(fine_query, all_tokens, token_part.shape[0], 4)
    window = attend_window(place, head_reach, fine_query, fine_key, fine_value, pair, beyond, 4)
    fine_result = finish(window, returned)
    return (fine_result, cross_result)


def solution(mesh):
    rows = P(("group", "seq"), None)
    return jax.shard_map(
        shards, mesh=mesh, in_specs=(rows,) * 6 + (P(),), out_specs=(rows, rows), check_vma=False
    )
```

time: 149 us -> 107 us (0.72)
  Pallas kernels: 0 us -> 40.9 us
  starting transfers between devices: 48.5 us -> 21.7 us
  local copies, waits for them, and re-layouts: 23.1 us -> 3.92 us
  waiting for transfers between devices: 52.6 us -> 37.4 us
  matrix products: 13.6 us -> 0 us
  other arithmetic: 8.25 us -> 0.69 us
    pallas_call x0 -> x8, Pallas kernels: none -> 40.9 us  [the longest x1 8.69 us: attend_window(): pl.pallas_call(window_kernel, out_shape=jax.ShapeDtypeStruct((rows, width...]
    all_to_all x6 -> x2, waiting for transfers between devices: 39.5 us -> 0.01 us  [exchange(): lax.all_to_all(slots, 'seq', 0, 0, tiled=True, axis_index_groups=same_block)]
    ppermute x4 -> x8, waiting for transfers between devices: 13.1 us -> 37.4 us  [the longest x6 37.4 us: around(): moved.append(lax.ppermute(value, 'seq', links))]
    all_to_all x6 -> x2, starting transfers between devices: 37.1 us -> 13.1 us  [exchange(): lax.all_to_all(slots, 'seq', 0, 0, tiled=True, axis_index_groups=same_block)]
    dot_general x9 -> x0, matrix products: 8.58 us -> none  [the longest x4 4.39 us: attend_heads(): jnp.einsum('qhd,khd->hqk', query_heads, key_heads, preferred_element_type...]
    sub x1 -> x0, matrix products: 5 us -> none  [softmax_rows(): exponent = jnp.exp(scores - largest)]
    convert_element_type x5 -> x0, local copies, waits for them, and re-layouts: 4.8 us -> none  [the longest x3 2.63 us: shards(): upsampled.astype(jnp.float32)]
    concatenate x3 -> x1, other arithmetic: 3.98 us -> 0.04 us  [shards(): tokens = jnp.concatenate([token_part] + over_outer(token_part), axis=0)]
  transfers between devices with their start and end apart: 10 -> 10, of which waited for: 6 -> 5; matrix products, arithmetic and copies ran while one was open for 26% -> 1% of each run, Pallas kernels for 0% -> 29%
where the time goes in v1:
time: 107 us; the launch traced here: 105 us
  Pallas kernels  40.9 us (38%)
  waiting for transfers between devices  37.4 us (35%)
  starting transfers between devices  21.7 us (20%)
  local copies, waits for them, and re-layouts  3.92 us (4%)
    ppermute x6, waiting for transfers between devices, around(): moved.append(lax.ppermute(value, 'seq', links))  37.4 us
    all_to_all x2, starting transfers between devices, exchange(): lax.all_to_all(slots, 'seq', 0, 0, tiled=True, axis_index_groups=same_block)  13.1 us
    pallas_call x1, Pallas kernels, attend_window(): pl.pallas_call(window_kernel, out_shape=jax.ShapeDtypeStruct((rows, width...  8.69 us
    pallas_call x1, Pallas kernels, attend_cross(): pl.pallas_call(functools.partial(cross_kernel, chunk), out_shape=jax.Shap...  8.42 us
    pallas_call x2, Pallas kernels, pack_halo(): pl.pallas_call(halo_kernel, out_shape=jax.ShapeDtypeStruct((2 * edge, wid...  7.92 us
    pallas_call x1, Pallas kernels, finish(): pl.pallas_call(finish_kernel, out_shape=jax.ShapeDtypeStruct((rows, width...  5.9 us
    ppermute x6, starting transfers between devices, around(): moved.append(lax.ppermute(value, 'seq', links))  5.12 us
    pallas_call x1, Pallas kernels, pack_coarse(): pl.pallas_call(coarse_pack_kernel, out_shape=(jax.ShapeDtypeStruct((group...  4.53 us
  transfers between devices with their start and end apart: 10, of which 5 were waited for; matrix products, arithmetic and copies ran while one was open for 1% of the time, Pallas kernels for 29%

profile of v1, /device:TPU:11, one launch (start us, length us, event | category | flops | bytes accessed | tf_op | source)
XLA Modules:
  0.0 105.3 jit_solution(15762350228182754267)
XLA Ops:
  0.6 4.5 %pack_coarse.1 = (bf16[8,96,384]{2,1,0:T(8,128)(2,1)}, f32[8,3072]{1,0:T(8,128)}) custom-call(bf16[32,3072]{1,0:T(8,128)(2,1)} %query_ref.4, bf16[32,3072]{1,0:T(8,128)(2,1)} %key_ref.7, bf16[32,3072]{1,0:T(8,128)(2,1)} %value_ref.7), custom_call_target="tpu_custom_call" | custom-call | tf_op jit(solution)/shard_map/pack_coarse/pallas_call | solution.py:83
  5.2 0.0 copy-start.7
  5.2 5.7 %all-to-all-start = ((bf16[8,96,384]{2,1,0:T(8,128)(2,1)}), bf16[8,96,384]{2,1,0:T(8,128)(2,1)S(1)}, u32[]{:S(2)}, u32[]{:S(2)}) async-start(bf16[8,96,384]{2,1,0:T(8,128)(2,1)} %get-tuple-element.4), calls=%async_computation | async-start | bytes 1179648 | tf_op jit(solution)/shard_map/all_to_all | solution.py:290
  10.9 0.0 copy-done.7
  10.9 0.3 collective-permute-start.3
  11.2 3.7 %collective-permute-done.3.refs_1_ = f32[8,3072]{1,0:T(8,128)S(1)} collective-permute-done((f32[8,3072]{1,0:T(8,128)S(1)}, f32[8,3072]{1,0:T(8,128)S(1)}, u32[]{:S(2)}, u32[]{:S(2)}) %collective-permute-start.3) | collective-permute-done | bytes 98336 | tf_op jit(solution)/shard_map/ppermute | solution.py:281
  14.9 0.0 copy-start.8
  14.9 0.6 copy-done.8
  15.5 1.6 %split_pooled.1 = bf16[24,3072]{1,0:T(8,128)(2,1)} custom-call(f32[8,3072]{1,0:T(8,128)} %get-tuple-element.5.refs_0_, f32[8,3072]{1,0:T(8,128)} %copy-done.8), custom_call_target="tpu_custom_call" | custom-call | tf_op jit(solution)/shard_map/split_pooled/pallas_call | solution.py:111
  17.1 1.2 %collective-permute-start.4 = (bf16[24,3072]{1,0:T(8,128)(2,1)}, bf16[24,3072]{1,0:T(8,128)(2,1)S(1)}, u32[]{:S(2)}, u32[]{:S(2)}) collective-permute-start(bf16[24,3072]{1,0:T(8,128)(2,1)} %split_pooled.1), channel_id=1, source_target_pairs={{0,4},{1,5},{2,6},{3,7},{4,8},{5,9},{6,10},{7,11},{8,12},{9,13},{1... | collective-permute-start | bytes 442376 | tf_op jit(solution)/shard_map/ppermute | solution.py:281
  18.3 1.3 %collective-permute-start.5 = (bf16[24,3072]{1,0:T(8,128)(2,1)}, bf16[24,3072]{1,0:T(8,128)(2,1)S(1)}, u32[]{:S(2)}, u32[]{:S(2)}) collective-permute-start(bf16[24,3072]{1,0:T(8,128)(2,1)} %split_pooled.1), channel_id=1, source_target_pairs={{0,8},{1,9},{2,10},{3,11},{4,12},{5,13},{6,14},{7,15},{8,0},{9,1},... | collective-permute-start | bytes 442376 | tf_op jit(solution)/shard_map/ppermute | solution.py:281
  19.7 1.0 collective-permute-start.6
  20.7 0.7 pad_add_fusion.place
  21.3 4.0 %pack_halo.2 = bf16[128,3072]{1,0:T(8,128)(2,1)} custom-call(s32[3]{0:T(128)} %pad_add_fusion.place, bf16[128,3072]{1,0:T(8,128)(2,1)} %key_ref.6, bf16[128,3072]{1,0:T(8,128)(2,1)} %value_ref.6), custom_call_target="tpu_custom_call" | custom-call | tf_op jit(solution)/shard_map/pack_halo/pallas_call | solution.py:53
  25.3 0.0 copy-start.5
  25.3 0.3 collective-permute-start
  25.6 4.0 %pack_halo.3 = bf16[128,3072]{1,0:T(8,128)(2,1)} custom-call(s32[3]{0:T(128)} %pad_add_fusion.place, bf16[128,3072]{1,0:T(8,128)(2,1)} %key_ref.6, bf16[128,3072]{1,0:T(8,128)(2,1)} %value_ref.6), custom_call_target="tpu_custom_call" | custom-call | tf_op jit(solution)/shard_map/pack_halo/pallas_call | solution.py:53
  29.5 3.3 %collective-permute-start.1 = (bf16[128,3072]{1,0:T(8,128)(2,1)}, bf16[128,3072]{1,0:T(8,128)(2,1)S(1)}, u32[]{:S(2)}, u32[]{:S(2)}) collective-permute-start(bf16[128,3072]{1,0:T(8,128)(2,1)} %pack_halo.3), channel_id=1, source_target_pairs={{2,4},{3,5},{6,8},{7,9},{10,12},{11,13},{4,2},{5,3},{8,6},{9,7},{1... | collective-permute-start | bytes 2359304 | tf_op jit(solution)/shard_map/ppermute | solution.py:299
  32.8 0.0 all-to-all-done.own_ref
  32.8 0.0 copy-start
  32.8 0.8 collective-permute-done.4
  33.7 0.3 collective-permute-start.2
  33.9 2.9 %collective-permute-done.5 = bf16[24,3072]{1,0:T(8,128)(2,1)S(1)} collective-permute-done((bf16[24,3072]{1,0:T(8,128)(2,1)}, bf16[24,3072]{1,0:T(8,128)(2,1)S(1)}, u32[]{:S(2)}, u32[]{:S(2)}) %collective-permute-start.5) | collective-permute-done | bytes 147488 | tf_op jit(solution)/shard_map/ppermute | solution.py:281
  36.9 1.4 %collective-permute-done.6 = bf16[24,3072]{1,0:T(8,128)(2,1)S(1)} collective-permute-done((bf16[24,3072]{1,0:T(8,128)(2,1)}, bf16[24,3072]{1,0:T(8,128)(2,1)S(1)}, u32[]{:S(2)}, u32[]{:S(2)}) %collective-permute-start.6) | collective-permute-done | bytes 147488 | tf_op jit(solution)/shard_map/ppermute | solution.py:281
  38.3 0.0 copy-done.5
  38.3 0.0 copy-start.1
  38.3 1.0 collective-permute-start.7
  39.4 28.5 %collective-permute-done.2.refs_0_ = bf16[8,64,384]{2,1,0:T(8,128)(2,1)} collective-permute-done((bf16[8,64,384]{2,1,0:T(8,128)(2,1)S(1)}, bf16[8,64,384]{2,1,0:T(8,128)(2,1)}, u32[]{:S(2)}, u32[]{:S(2)}) %collective-permute-start.2) | collective-permute-done | bytes 393248 | tf_op jit(solution)/shard_map/ppermute | solution.py:281
  67.9 0.0 copy-done
  67.9 3.8 %attend_coarse.1 = bf16[8,32,384]{2,1,0:T(8,128)(2,1)} custom-call(bf16[8,96,384]{2,1,0:T(8,128)(2,1)} %copy-done, bf16[8,64,384]{2,1,0:T(8,128)(2,1)} %collective-permute-done.2.refs_0_), custom_call_target="tpu_custom_call" | custom-call | tf_op jit(solution)/shard_map/attend_coarse/pallas_call | solution.py:140
  71.7 7.3 %all-to-all-start.1 = ((bf16[8,32,384]{2,1,0:T(8,128)(2,1)}), bf16[8,32,384]{2,1,0:T(8,128)(2,1)S(1)}, u32[]{:S(2)}, u32[]{:S(2)}) async-start(bf16[8,32,384]{2,1,0:T(8,128)(2,1)} %attend_coarse.1), calls=%async_computation.1 | async-start | bytes 393216 | tf_op jit(solution)/shard_map/all_to_all | solution.py:290
  79.0 0.0 collective-permute-done.pair_ref
  79.0 0.0 copy-start.3
  79.0 0.0 collective-permute-done.1.next_ref
  79.1 0.9 copy-done.3
  79.9 0.0 copy-start.4
  79.9 0.9 copy-done.4
  80.8 8.7 %attend_window.1.window_ref = f32[128,3072]{1,0:T(8,128)} custom-call(s32[3]{0:T(128)} %pad_add_fusion.place, s32[24]{0:T(128)} %reach.1, bf16[128,3072]{1,0:T(8,128)(2,1)} %query_ref.5, bf16[128,3072]{1,0:T(8,128)(2,1)} %key_ref.6, bf16[128,3072]{1,0:T(8,128)(2,1)} %value_ref.6, bf16[128,3072]{1,0:T(8,128)(2,1)} %copy-done.3, bf16[128,3072]{1,0:T(8,128)(2,1)} %copy-done.4), custom_call_target="tpu_custom_call" | custom-call | tf_op jit(solution)/shard_map/attend_window/pallas_call | solution.py:219
  89.5 0.0 copy-done.1
  89.5 0.0 collective-permute-done.7.refs_1_
  89.5 0.0 copy-start.6
  89.5 0.8 copy-done.6
  90.3 8.4 %attend_cross.1 = bf16[128,3072]{1,0:T(8,128)(2,1)} custom-call(bf16[128,3072]{1,0:T(8,128)(2,1)} %query_ref.5, bf16[96,3072]{1,0:T(8,128)(2,1)} %copy-done.1, bf16[96,3072]{1,0:T(8,128)(2,1)} %copy-done.6), custom_call_target="tpu_custom_call" | custom-call | tf_op jit(solution)/shard_map/attend_cross/pallas_call | solution.py:178
  98.7 0.0 all-to-all-done.1.coarse_ref
  98.7 0.0 copy-start.2
  98.7 0.7 copy-done.2
  99.4 5.9 %finish.1 = bf16[128,3072]{1,0:T(8,128)(2,1)} custom-call(f32[128,3072]{1,0:T(8,128)} %attend_window.1.window_ref, bf16[8,32,384]{2,1,0:T(8,128)(2,1)} %copy-done.2), custom_call_target="tpu_custom_call" | custom-call | tf_op jit(solution)/shard_map/finish/pallas_call | solution.py:248
  (2 shorter events, 0.1 us)
Async XLA Ops:
  5.2 5.7 %copy-start.7 = (f32[8,3072]{1,0:T(8,128)S(1)}, f32[8,3072]{1,0:T(8,128)}, u32[]{:S(2)}) copy-start(f32[8,3072]{1,0:T(8,128)} %get-tuple-element.5.refs_0_) | copy-start | bytes 294916
  5.2 27.6 %all-to-all-start = ((bf16[8,96,384]{2,1,0:T(8,128)(2,1)}), bf16[8,96,384]{2,1,0:T(8,128)(2,1)S(1)}, u32[]{:S(2)}, u32[]{:S(2)}) async-start(bf16[8,96,384]{2,1,0:T(8,128)(2,1)} %get-tuple-element.4), calls=%async_computation | async-start | bytes 1179648 | tf_op jit(solution)/shard_map/all_to_all | solution.py:290
  10.9 4.0 %collective-permute-start.3 = (f32[8,3072]{1,0:T(8,128)S(1)}, f32[8,3072]{1,0:T(8,128)S(1)}, u32[]{:S(2)}, u32[]{:S(2)}) collective-permute-start(f32[8,3072]{1,0:T(8,128)S(1)} %copy-done.7), channel_id=1, source_target_pairs={{0,2},{1,3},{2,0},{3,1},{4,6},{5,7},{6,4},{7,5},{8,10},{9,11},{10,... | collective-permute-start | bytes 294920 | tf_op jit(solution)/shard_map/ppermute | solution.py:281
  14.9 0.6 copy-start.8
  17.1 16.5 %collective-permute-start.4 = (bf16[24,3072]{1,0:T(8,128)(2,1)}, bf16[24,3072]{1,0:T(8,128)(2,1)S(1)}, u32[]{:S(2)}, u32[]{:S(2)}) collective-permute-start(bf16[24,3072]{1,0:T(8,128)(2,1)} %split_pooled.1), channel_id=1, source_target_pairs={{0,4},{1,5},{2,6},{3,7},{4,8},{5,9},{6,10},{7,11},{8,12},{9,13},{1... | collective-permute-start | bytes 442376 | tf_op jit(solution)/shard_map/ppermute | solution.py:281
  18.3 18.5 %collective-permute-start.5 = (bf16[24,3072]{1,0:T(8,128)(2,1)}, bf16[24,3072]{1,0:T(8,128)(2,1)S(1)}, u32[]{:S(2)}, u32[]{:S(2)}) collective-permute-start(bf16[24,3072]{1,0:T(8,128)(2,1)} %split_pooled.1), channel_id=1, source_target_pairs={{0,8},{1,9},{2,10},{3,11},{4,12},{5,13},{6,14},{7,15},{8,0},{9,1},... | collective-permute-start | bytes 442376 | tf_op jit(solution)/shard_map/ppermute | solution.py:281
  19.7 18.6 %collective-permute-start.6 = (bf16[24,3072]{1,0:T(8,128)(2,1)}, bf16[24,3072]{1,0:T(8,128)(2,1)S(1)}, u32[]{:S(2)}, u32[]{:S(2)}) collective-permute-start(bf16[24,3072]{1,0:T(8,128)(2,1)} %split_pooled.1), channel_id=1, source_target_pairs={{0,12},{1,13},{2,14},{3,15},{4,0},{5,1},{6,2},{7,3},{8,4},{9,5},{1... | collective-permute-start | bytes 442376 | tf_op jit(solution)/shard_map/ppermute | solution.py:281
  25.3 13.0 %copy-start.5 = (bf16[24,3072]{1,0:T(8,128)(2,1)S(1)}, bf16[24,3072]{1,0:T(8,128)(2,1)}, u32[]{:S(2)}) copy-start(bf16[24,3072]{1,0:T(8,128)(2,1)} %split_pooled.1) | copy-start | bytes 442372
  25.3 53.7 %collective-permute-start = (bf16[128,3072]{1,0:T(8,128)(2,1)}, bf16[128,3072]{1,0:T(8,128)(2,1)S(1)}, u32[]{:S(2)}, u32[]{:S(2)}) collective-permute-start(bf16[128,3072]{1,0:T(8,128)(2,1)} %pack_halo.2), channel_id=1, source_target_pairs={{0,2},{1,3},{4,6},{5,7},{8,10},{9,11},{12,14},{13,15},{2,0},{3,1},... | collective-permute-start | bytes 2359304 | tf_op jit(solution)/shard_map/ppermute | solution.py:299
  29.5 49.5 %collective-permute-start.1 = (bf16[128,3072]{1,0:T(8,128)(2,1)}, bf16[128,3072]{1,0:T(8,128)(2,1)S(1)}, u32[]{:S(2)}, u32[]{:S(2)}) collective-permute-start(bf16[128,3072]{1,0:T(8,128)(2,1)} %pack_halo.3), channel_id=1, source_target_pairs={{2,4},{3,5},{6,8},{7,9},{10,12},{11,13},{4,2},{5,3},{8,6},{9,7},{1... | collective-permute-start | bytes 2359304 | tf_op jit(solution)/shard_map/ppermute | solution.py:299
  32.8 35.1 %copy-start = (bf16[8,96,384]{2,1,0:T(8,128)(2,1)}, bf16[8,96,384]{2,1,0:T(8,128)(2,1)S(1)}, u32[]{:S(2)}) copy-start(bf16[8,96,384]{2,1,0:T(8,128)(2,1)S(1)} %all-to-all-done.own_ref) | copy-start | bytes 1769476
  33.7 34.3 %collective-permute-start.2 = (bf16[8,64,384]{2,1,0:T(8,128)(2,1)S(1)}, bf16[8,64,384]{2,1,0:T(8,128)(2,1)}, u32[]{:S(2)}, u32[]{:S(2)}) collective-permute-start(bf16[8,64,384]{2,1,0:T(8,128)(2,1)S(1)} %slice.4), channel_id=1, source_target_pairs={{0,2},{1,3},{2,0},{3,1},{4,6},{5,7},{6,4},{7,5},{8,10},{9,11},{10,... | collective-permute-start | bytes 1179656 | tf_op jit(solution)/shard_map/ppermute | solution.py:281
  38.3 51.2 %copy-start.1 = (bf16[96,3072]{1,0:T(8,128)(2,1)}, bf16[96,3072]{1,0:T(8,128)(2,1)S(1)}, u32[]{:S(2)}) copy-start(bf16[96,3072]{1,0:T(8,128)(2,1)S(1)} %pad_maximum_fusion.refs_0_) | copy-start | bytes 1769476
  38.3 51.2 %collective-permute-start.7 = (bf16[96,3072]{1,0:T(8,128)(2,1)S(1)}, bf16[96,3072]{1,0:T(8,128)(2,1)S(1)}, u32[]{:S(2)}, u32[]{:S(2)}) collective-permute-start(bf16[96,3072]{1,0:T(8,128)(2,1)S(1)} %pad_maximum_fusion.refs_0_), channel_id=1, source_target_pairs={{0,1},{1,0},{2,3},{3,2},{4,5},{5,4},{6,7},{7,6},{8,9},{9,8},{10,11... | collective-permute-start | bytes 1769480 | tf_op jit(solution)/shard_map/ppermute | solution.py:281
  71.7 27.0 %all-to-all-start.1 = ((bf16[8,32,384]{2,1,0:T(8,128)(2,1)}), bf16[8,32,384]{2,1,0:T(8,128)(2,1)S(1)}, u32[]{:S(2)}, u32[]{:S(2)}) async-start(bf16[8,32,384]{2,1,0:T(8,128)(2,1)} %attend_coarse.1), calls=%async_computation.1 | async-start | bytes 393216 | tf_op jit(solution)/shard_map/all_to_all | solution.py:290
  79.0 0.9 copy-start.3
  79.9 0.9 copy-start.4
  89.5 0.8 copy-start.6
  98.7 0.7 copy-start.2

commit v2 on v1

v2 whole, which is shorter than its diff:
```python
import functools
import math

import jax
import jax.numpy as jnp
from jax import lax
from jax.experimental import pallas as pl
from jax.experimental.pallas import tpu as pltpu
from jax.sharding import PartitionSpec as P


HD = 128
TT = 4
TH = 4
TW = 8
NT = 8
HALO_F = 2

PLANE = TH * TW
CELLS = (TH // 2) * (TW // 2)
SCALE = HD**-0.5
MASKED = -1e30
FAR = 1 << 20
GRANT = pltpu.CompilerParams(vmem_limit_bytes=20 << 20)

VMEM = pl.BlockSpec(memory_space=pltpu.VMEM)
SMEM = pl.BlockSpec(memory_space=pltpu.SMEM)
HBM = pl.BlockSpec(memory_space=pltpu.HBM)


def streamed(value):
    return pltpu.with_memory_space_constraint(value, pltpu.HBM)


def dot_rows(left, right):
    return lax.dot_general(left, right, (((1,), (1,)), ((), ())), preferred_element_type=jnp.float32)


def dot_plain(left, right):
    return lax.dot_general(left, right, (((1,), (0,)), ((), ())), preferred_element_type=jnp.float32)


def blend(scores, values):
    exponent = jnp.exp(scores - jnp.max(scores, axis=-1, keepdims=True)).astype(jnp.bfloat16)
    ones = jnp.ones((values.shape[0], HD), values.dtype)
    sums = dot_plain(exponent, jnp.concatenate([values, ones], axis=1))
    return sums[:, :HD] * (1.0 / sums[:, HD:])


def head_cut(head):
    return slice(head * HD, (head + 1) * HD)


def pool_rows(rows):
    cells = rows.astype(jnp.float32).reshape(-1, CELLS, rows.shape[1])
    return jnp.sum(cells, axis=1) * CELLS**-0.5


def pack_kernel(
    tiles_across,
    query_hbm,
    key_hbm,
    value_hbm,
    fine_key_hbm,
    fine_value_hbm,
    slots_hbm,
    pooled_ref,
    pair_hbm,
    far_hbm,
    coarse_buf,
    fine_buf,
    in_sem,
    slot_sem,
    edge_sem,
):
    groups = slots_hbm.shape[0]
    rows, width = query_hbm.shape
    fine_rows = fine_key_hbm.shape[0]
    group_width = width // groups
    edge = HALO_F * PLANE
    odd = (lax.axis_index("seq") // tiles_across) % 2
    loads = []
    for index, source in enumerate((fine_key_hbm, fine_value_hbm)):
        loads.append(pltpu.make_async_copy(source, fine_buf.at[index], in_sem.at[index]))
    for index, source in enumerate((query_hbm, key_hbm, value_hbm)):
        loads.append(pltpu.make_async_copy(source, coarse_buf.at[index], in_sem.at[2 + index]))
    for load in loads:
        load.start()
    stores = []
    for index in range(2):
        loads[index].wait()
        for side, (target, last) in enumerate(((pair_hbm, 1 - odd), (far_hbm, odd))):
            start = pl.multiple_of(last * (fine_rows - edge), edge)
            stores.append(
                pltpu.make_async_copy(
                    fine_buf.at[index, pl.ds(start, edge)],
                    target.at[pl.ds(index * edge, edge)],
                    edge_sem.at[index, side],
                )
            )
            stores[-1].start()
    for index in range(3):
        loads[2 + index].wait()
        for group in range(groups):
            stores.append(
                pltpu.make_async_copy(
                    coarse_buf.at[index, :, pl.ds(group * group_width, group_width)],
                    slots_hbm.at[group, pl.ds(index * rows, rows)],
                    slot_sem.at[index, group],
                )
            )
            stores[-1].start()
    pooled_ref[:TT] = pool_rows(coarse_buf[1])
    pooled_ref[TT:] = pool_rows(coarse_buf[2])
    for store in stores:
        store.wait()


def pack(coarse_query, coarse_key, coarse_value, fine_key, fine_value, groups, tiles_across):
    rows, width = coarse_query.shape
    kind = coarse_query.dtype
    halo = pltpu.HBM((2 * HALO_F * PLANE, width), kind)
    return pl.pallas_call(
        functools.partial(pack_kernel, tiles_across),
        out_shape=(
            pltpu.HBM((groups, 3 * rows, width // groups), kind),
            jax.ShapeDtypeStruct((2 * TT, width), jnp.float32),
            halo,
            halo,
        ),
        in_specs=[HBM] * 5,
        out_specs=(HBM, VMEM, HBM, HBM),
        scratch_shapes=[
            pltpu.VMEM((3, rows, width), kind),
            pltpu.VMEM((2,) + fine_key.shape, kind),
            pltpu.SemaphoreType.DMA((5,)),
            pltpu.SemaphoreType.DMA((3, groups)),
            pltpu.SemaphoreType.DMA((2, 2)),
        ],
        compiler_params=GRANT,
        name="pack",
    )(*map(streamed, (coarse_query, coarse_key, coarse_value, fine_key, fine_value)))


def split_pooled_kernel(*refs):
    *in_refs, out_ref = refs
    keys = jnp.concatenate([ref[:TT] for ref in in_refs], axis=0)
    values = jnp.concatenate([ref[TT:] for ref in in_refs], axis=0)
    high = keys.astype(jnp.bfloat16).astype(jnp.float32)
    out_ref[...] = jnp.concatenate([high, keys - high, values], axis=0).astype(jnp.bfloat16)


def split_pooled(pieces):
    width = pieces[0].shape[1]
    return pl.pallas_call(
        split_pooled_kernel,
        out_shape=jax.ShapeDtypeStruct((3 * TT * len(pieces), width), jnp.bfloat16),
        in_specs=[VMEM] * len(pieces),
        out_specs=VMEM,
        compiler_params=GRANT,
        name="split_pooled",
    )(*pieces)


def coarse_kernel(own_ref, *refs):
    *other_refs, out_ref = refs
    members, packed, group_width = own_ref.shape
    rows = packed // 3
    for head in range(group_width // HD):
        cut = head_cut(head)

        def flat(ref, start):
            return ref[:, start : start + rows, cut].reshape(members * rows, HD)

        query = flat(own_ref, 0)
        keys = jnp.concatenate([flat(own_ref, rows)] + [flat(r, 0) for r in other_refs], axis=0)
        values = jnp.concatenate([flat(own_ref, 2 * rows)] + [flat(r, rows) for r in other_refs], axis=0)
        mixed = blend(dot_rows(query, keys) * SCALE, values)
        out_ref[:, :, cut] = mixed.astype(out_ref.dtype).reshape(members, rows, HD)


def attend_coarse(own, others):
    members, packed, group_width = own.shape
    return pl.pallas_call(
        coarse_kernel,
        out_shape=jax.ShapeDtypeStruct((members, packed // 3, group_width), own.dtype),
        in_specs=[VMEM] * (1 + len(others)),
        out_specs=VMEM,
        compiler_params=GRANT,
        name="attend_coarse",
    )(own, *others)


def cross_kernel(chunk, query_ref, *refs):
    *token_refs, out_ref = refs
    third = chunk // 3
    for head in range(query_ref.shape[1] // HD):
        cut = head_cut(head)
        high, low, values = [], [], []
        for ref in token_refs:
            rows = ref[:, cut].astype(jnp.float32)
            for start in range(0, rows.shape[0], chunk):
                high.append(rows[start : start + third])
                low.append(rows[start + third : start + 2 * third])
                values.append(rows[start + 2 * third : start + chunk])
        high, low, values = (jnp.concatenate(p, axis=0).astype(jnp.bfloat16) for p in (high, low, values))
        query = query_ref[:, cut]
        scores = dot_rows(jnp.concatenate([query, query], axis=1), jnp.concatenate([high, low], axis=1))
        out_ref[:, cut] = blend(scores * SCALE, values).astype(out_ref.dtype)


def attend_cross(fine_query, tokens, chunk):
    return pl.pallas_call(
        functools.partial(cross_kernel, chunk),
        out_shape=jax.ShapeDtypeStruct(fine_query.shape, jnp.bfloat16),
        in_specs=[VMEM] * (1 + len(tokens)),
        out_specs=VMEM,
        compiler_params=GRANT,
        name="attend_cross",
    )(fine_query, *tokens)


def window_kernel(tiles_across, reach, query_ref, key_ref, value_ref, pair_ref, far_ref, out_ref, bias):
    rows, width = query_ref.shape
    edge = HALO_F * PLANE
    total = rows + 2 * edge
    time_tile = lax.axis_index("seq") // tiles_across
    later = time_tile % 2 == 0
    row_frame = lax.broadcasted_iota(jnp.int32, (rows, total), 0) // PLANE
    column = lax.broadcasted_iota(jnp.int32, (rows, total), 1)
    pair_frame = (column - rows) // PLANE + jnp.where(later, TT, -HALO_F)
    far_frame = (column - rows - edge) // PLANE + jnp.where(later, -HALO_F, TT)
    key_frame = jnp.where(column < rows, column // PLANE, jnp.where(column < rows + edge, pair_frame, far_frame))
    absolute = key_frame + time_tile * TT
    distance = jnp.where((absolute >= 0) & (absolute < NT * TT), jnp.abs(row_frame - key_frame), FAR)
    for limit in range(HALO_F):
        bias[limit] = jnp.where(distance <= limit + 1, 0.0, MASKED)
    for head in range(width // HD):
        cut = head_cut(head)
        keys = jnp.concatenate([key_ref[:, cut], pair_ref[:edge, cut], far_ref[:edge, cut]], axis=0)
        values = jnp.concatenate([value_ref[:, cut], pair_ref[edge:, cut], far_ref[edge:, cut]], axis=0)
        scores = dot_rows(query_ref[:, cut], keys) * SCALE + bias[reach[head] - 1]
        out_ref[:, cut] = blend(scores, values)


def attend_window(head_reach, fine_query, fine_key, fine_value, pair, far, tiles_across):
    rows, width = fine_query.shape
    return pl.pallas_call(
        functools.partial(window_kernel, tiles_across),
        out_shape=jax.ShapeDtypeStruct((rows, width), jnp.float32),
        in_specs=[SMEM] + [VMEM] * 5,
        out_specs=VMEM,
        scratch_shapes=[pltpu.VMEM((HALO_F, rows, 2 * rows), jnp.float32)],
        compiler_params=GRANT,
        name="attend_window",
    )(head_reach, fine_query, fine_key, fine_value, pair, far)


def finish_kernel(window_ref, coarse_ref, out_ref):
    rows = window_ref.shape[0]
    groups, coarse_rows, group_width = coarse_ref.shape
    row = lax.broadcasted_iota(jnp.int32, (rows, coarse_rows), 0)
    column = lax.broadcasted_iota(jnp.int32, (rows, coarse_rows), 1)
    frame, y, x = row // PLANE, (row % PLANE) // TW, row % TW
    source = frame * CELLS + (y // 2) * (TW // 2) + x // 2
    pick = (source == column).astype(jnp.bfloat16)
    for group in range(groups):
        cut = slice(group * group_width, (group + 1) * group_width)
        out_ref[:, cut] = (window_ref[:, cut] + dot_plain(pick, coarse_ref[group])).astype(out_ref.dtype)


def finish(window, returned):
    return pl.pallas_call(
        finish_kernel,
        out_shape=jax.ShapeDtypeStruct(window.shape, jnp.bfloat16),
        in_specs=[VMEM, VMEM],
        out_specs=VMEM,
        compiler_params=GRANT,
        name="finish",
    )(window, returned)


def shards(coarse_query, coarse_key, coarse_value, fine_query, fine_key, fine_value, head_reach):
    devices = lax.axis_size("seq")
    head_count = coarse_query.shape[1] // HD
    groups = math.gcd(head_count, devices)
    blocks = devices // groups
    inner = math.gcd(2, groups)
    outer = groups // inner
    tiles_across = devices // NT

    def seat(o, b, c):
        return (o * blocks + b) * inner + c

    def around(value, extent, move):
        moved = []
        for step in range(1, extent):
            links = [
                (seat(o, b, c), seat(*move(o, b, c, step)))
                for o in range(outer)
                for b in range(blocks)
                for c in range(inner)
            ]
            moved.append(lax.ppermute(value, "seq", links))
        return moved

    over_blocks = functools.partial(around, extent=blocks, move=lambda o, b, c, s: (o, (b + s) % blocks, c))
    over_outer = functools.partial(around, extent=outer, move=lambda o, b, c, s: ((o + s) % outer, b, c))
    over_inner = functools.partial(around, extent=inner, move=lambda o, b, c, s: (o, b, (c + s) % inner))
    same_block = [[seat(o, b, c) for o in range(outer) for c in range(inner)] for b in range(blocks)]

    def exchange(slots):
        return lax.all_to_all(slots, "seq", 0, 0, tiled=True, axis_index_groups=same_block)

    edges = [(j, j + tiles_across) for j in range(devices - tiles_across)]
    early = [(a, b) for a, b in edges if (a // tiles_across) % 2 == 0]
    late = [(a, b) for a, b in edges if (a // tiles_across) % 2 == 1]

    def swap(value, links):
        return lax.ppermute(value, "seq", links + [(b, a) for a, b in links])

    slots, pooled, pair_edge, far_edge = pack(
        coarse_query, coarse_key, coarse_value, fine_key, fine_value, groups, tiles_across
    )
    pair = swap(pair_edge, early)
    received = exchange(slots)
    pieces = [pooled] + over_blocks(pooled)
    token_part = split_pooled(pieces)
    pieces = [token_part] + over_outer(token_part)
    tokens = jnp.concatenate(pieces, axis=0)
    all_tokens = [tokens] + over_inner(tokens)
    coarse_rows = coarse_query.shape[0]
    coarse_keys = received[:, coarse_rows:]
    others = over_blocks(coarse_keys)
    far = swap(far_edge, late)
    cross_result = attend_cross(fine_query, all_tokens, token_part.shape[0])
    attended = attend_coarse(received, others)
    returned = exchange(attended)
    window = attend_window(head_reach, fine_query, fine_key, fine_value, pair, far, tiles_across)
    fine_result = finish(window, returned)
    return (fine_result, cross_result)


def solution(mesh):
    rows = P(("group", "seq"), None)
    return jax.shard_map(
        shards, mesh=mesh, in_specs=(rows,) * 6 + (P(),), out_specs=(rows, rows), check_vma=False
    )
```

time: 107 us -> 79.8 us (0.75)
  the two profiles are of different devices: /device:TPU:11 before, /device:TPU:1 now
where the time goes in v2:
time: 79.8 us; the launch traced here: 79.3 us
  waiting for transfers between devices  37.2 us (47%)
  starting transfers between devices  24.7 us (31%)
  Pallas kernels  11.7 us (15%)
  local copies, waits for them, and re-layouts  3.2 us (4%)
  other arithmetic  1.78 us (2%)
    ppermute x6, waiting for transfers between devices, around(): moved.append(lax.ppermute(value, 'seq', links))  32 us
    all_to_all x2, starting transfers between devices, exchange(): lax.all_to_all(slots, 'seq', 0, 0, tiled=True, axis_index_groups=same_block)  14.6 us
    ppermute x6, starting transfers between devices, around(): moved.append(lax.ppermute(value, 'seq', links))  7.37 us
    all_to_all x2, waiting for transfers between devices, exchange(): lax.all_to_all(slots, 'seq', 0, 0, tiled=True, axis_index_groups=same_block)  5.29 us
    pallas_call x1, Pallas kernels, attend_cross(): pl.pallas_call(functools.partial(cross_kernel, chunk), out_shape=jax.Shap...  3.49 us
    unnamed x14, local copies, waits for them, and re-layouts  3.16 us
    ppermute x2, starting transfers between devices, swap(): return lax.ppermute(value, 'seq', links + [(b, a) for a, b in links])  2.76 us
    pallas_call x1, Pallas kernels, pack(): pl.pallas_call(functools.partial(pack_kernel, tiles_across), out_shape=(p...  2.73 us
  transfers between devices with their start and end apart: 10, of which 4 were waited for; matrix products, arithmetic and copies ran while one was open for 2% of the time, Pallas kernels for 10%

profile of v2, /device:TPU:1, one launch (start us, length us, event | category | flops | bytes accessed | tf_op | source)
XLA Modules:
  0.0 79.3 jit_solution(139115698157971901)
XLA Ops:
  0.6 2.7 %pack.1 = (bf16[8,96,384]{2,1,0:T(8,128)(2,1)}, f32[8,3072]{1,0:T(8,128)S(1)}, bf16[128,3072]{1,0:T(8,128)(2,1)}, bf16[128,3072]{1,0:T(8,128)(2,1)}) custom-call(bf16[32,3072]{1,0:T(8,128)(2,1)} %query_hbm.1, bf16[32,3072]{1,0:T(8,128)(2,1)} %key_hbm.1, bf16[32,3072]{1,0:T(8,128)(2,1)} %value_hbm.1, bf16[128,3072]{1,0:T(8,128)(2,1)} %key_ref.1, ...), custom_call_target="tpu_custom_call" | custom-call | tf_op jit(solution)/shard_map/pack/pallas_call | solution.py:123
  3.4 6.4 %all-to-all-start = ((bf16[8,96,384]{2,1,0:T(8,128)(2,1)}), bf16[8,96,384]{2,1,0:T(8,128)(2,1)S(1)}, u32[]{:S(2)}, u32[]{:S(2)}) async-start(bf16[8,96,384]{2,1,0:T(8,128)(2,1)} %get-tuple-element.8), calls=%async_computation | async-start | bytes 1179648 | tf_op jit(solution)/shard_map/all_to_all | solution.py:313
  9.7 1.2 %collective-permute-start.3 = (f32[8,3072]{1,0:T(8,128)S(1)}, f32[8,3072]{1,0:T(8,128)S(1)}, u32[]{:S(2)}, u32[]{:S(2)}) collective-permute-start(f32[8,3072]{1,0:T(8,128)S(1)} %get-tuple-element.9.refs_0_), channel_id=1, source_target_pairs={{0,2},{1,3},{2,0},{3,1},{4,6},{5,7},{6,4},{7,5},{8,10},{9,11},{10,... | collective-permute-start | bytes 294920 | tf_op jit(solution)/shard_map/ppermute | solution.py:304
  11.0 3.1 %collective-permute-done.3.refs_1_ = f32[8,3072]{1,0:T(8,128)S(1)} collective-permute-done((f32[8,3072]{1,0:T(8,128)S(1)}, f32[8,3072]{1,0:T(8,128)S(1)}, u32[]{:S(2)}, u32[]{:S(2)}) %collective-permute-start.3) | collective-permute-done | bytes 98336 | tf_op jit(solution)/shard_map/ppermute | solution.py:304
  14.1 2.8 %collective-permute-start.6 = (bf16[24,3072]{1,0:T(8,128)(2,1)S(1)}, bf16[24,3072]{1,0:T(8,128)(2,1)S(1)}, u32[]{:S(2)}, u32[]{:S(2)}) collective-permute-start(bf16[24,3072]{1,0:T(8,128)(2,1)S(1)} %split_pooled.1), channel_id=1, source_target_pairs={{0,12},{1,13},{2,14},{3,15},{4,0},{5,1},{6,2},{7,3},{8,4},{9,5},{1... | collective-permute-start | bytes 442376 | tf_op jit(solution)/shard_map/ppermute | solution.py:304
  16.9 0.0 collective-permute-start.5
  16.9 0.6 collective-permute-start.4
  17.5 1.2 %collective-permute-start = (bf16[128,3072]{1,0:T(8,128)(2,1)}, bf16[128,3072]{1,0:T(8,128)(2,1)S(1)}, u32[]{:S(2)}, u32[]{:S(2)}) collective-permute-start(bf16[128,3072]{1,0:T(8,128)(2,1)} %get-tuple-element.6), channel_id=1, source_target_pairs={{0,2},{1,3},{4,6},{5,7},{8,10},{9,11},{12,14},{13,15},{2,0},{3,1},... | collective-permute-start | bytes 2359304 | tf_op jit(solution)/shard_map/ppermute | solution.py:320
  18.7 1.5 %collective-permute-start.1 = (bf16[128,3072]{1,0:T(8,128)(2,1)}, bf16[128,3072]{1,0:T(8,128)(2,1)}, u32[]{:S(2)}, u32[]{:S(2)}) collective-permute-start(bf16[128,3072]{1,0:T(8,128)(2,1)} %get-tuple-element.7), channel_id=1, source_target_pairs={{2,4},{3,5},{6,8},{7,9},{10,12},{11,13},{4,2},{5,3},{8,6},{9,7},{1... | collective-permute-start | bytes 2359304 | tf_op jit(solution)/shard_map/ppermute | solution.py:320
  20.3 5.3 %all-to-all-done.own_ref = bf16[8,96,384]{2,1,0:T(8,128)(2,1)S(1)} async-done(((bf16[8,96,384]{2,1,0:T(8,128)(2,1)}), bf16[8,96,384]{2,1,0:T(8,128)(2,1)S(1)}, u32[]{:S(2)}, u32[]{:S(2)}) %all-to-all-start) | async-done | bytes 589856 | tf_op jit(solution)/shard_map/all_to_all | solution.py:313
  25.6 0.0 copy-start
  25.6 0.0 copy-start.1
  25.6 0.0 copy-start.6
  25.6 0.0 collective-permute-done.6
  25.6 1.2 %collective-permute-start.2 = (bf16[8,64,384]{2,1,0:T(8,128)(2,1)S(1)}, bf16[8,64,384]{2,1,0:T(8,128)(2,1)S(1)}, u32[]{:S(2)}, u32[]{:S(2)}) collective-permute-start(bf16[8,64,384]{2,1,0:T(8,128)(2,1)S(1)} %slice.4), channel_id=1, source_target_pairs={{0,2},{1,3},{2,0},{3,1},{4,6},{5,7},{6,4},{7,5},{8,10},{9,11},{10,... | collective-permute-start | bytes 1179656 | tf_op jit(solution)/shard_map/ppermute | solution.py:304
  26.9 11.3 %collective-permute-done.5 = bf16[24,3072]{1,0:T(8,128)(2,1)S(1)} collective-permute-done((bf16[24,3072]{1,0:T(8,128)(2,1)S(1)}, bf16[24,3072]{1,0:T(8,128)(2,1)S(1)}, u32[]{:S(2)}, u32[]{:S(2)}) %collective-permute-start.5) | collective-permute-done | bytes 147488 | tf_op jit(solution)/shard_map/ppermute | solution.py:304
  38.2 0.0 collective-permute-done.4
  38.2 1.8 %pad_maximum_fusion.refs_0_ = bf16[96,3072]{1,0:T(8,128)(2,1)} fusion(bf16[24,3072]{1,0:T(8,128)(2,1)S(1)} %collective-permute-done.6, bf16[24,3072]{1,0:T(8,128)(2,1)S(1)} %collective-permute-done.5, bf16[24,3072]{1,0:T(8,128)(2,1)} %collective-permute-done.4, bf16[24,3072]{1,0:T(8,128)(2,1)S(1)} %split_pooled.1), kind=kLoop, calls=%fused_computation | loop fusion | flops 2359296 | bytes 1179648 | tf_op jit(solution)/shard_map/concatenate | solution.py:330
  40.0 1.5 %collective-permute-start.7 = (bf16[96,3072]{1,0:T(8,128)(2,1)}, bf16[96,3072]{1,0:T(8,128)(2,1)}, u32[]{:S(2)}, u32[]{:S(2)}) collective-permute-start(bf16[96,3072]{1,0:T(8,128)(2,1)} %pad_maximum_fusion.refs_0_), channel_id=1, source_target_pairs={{0,1},{1,0},{2,3},{3,2},{4,5},{5,4},{6,7},{7,6},{8,9},{9,8},{10,11... | collective-permute-start | bytes 1769480 | tf_op jit(solution)/shard_map/ppermute | solution.py:304
  41.5 17.5 %collective-permute-done.2.refs_0_ = bf16[8,64,384]{2,1,0:T(8,128)(2,1)S(1)} collective-permute-done((bf16[8,64,384]{2,1,0:T(8,128)(2,1)S(1)}, bf16[8,64,384]{2,1,0:T(8,128)(2,1)S(1)}, u32[]{:S(2)}, u32[]{:S(2)}) %collective-permute-start.2) | collective-permute-done | bytes 393248 | tf_op jit(solution)/shard_map/ppermute | solution.py:304
  59.0 1.5 %attend_coarse.1 = bf16[8,32,384]{2,1,0:T(8,128)(2,1)} custom-call(bf16[8,96,384]{2,1,0:T(8,128)(2,1)S(1)} %all-to-all-done.own_ref, bf16[8,64,384]{2,1,0:T(8,128)(2,1)S(1)} %collective-permute-done.2.refs_0_), custom_call_target="tpu_custom_call" | custom-call | tf_op jit(solution)/shard_map/attend_coarse/pallas_call | solution.py:184
  60.6 8.2 %all-to-all-start.1 = ((bf16[8,32,384]{2,1,0:T(8,128)(2,1)}), bf16[8,32,384]{2,1,0:T(8,128)(2,1)S(1)}, u32[]{:S(2)}, u32[]{:S(2)}) async-start(bf16[8,32,384]{2,1,0:T(8,128)(2,1)} %attend_coarse.1), calls=%async_computation.1 | async-start | bytes 393216 | tf_op jit(solution)/shard_map/all_to_all | solution.py:313
  68.8 0.0 collective-permute-done.pair_ref
  68.8 0.0 copy-start.4
  68.8 0.9 %copy-done.4 = bf16[128,3072]{1,0:T(8,128)(2,1)} copy-done((bf16[128,3072]{1,0:T(8,128)(2,1)}, bf16[128,3072]{1,0:T(8,128)(2,1)S(1)}, u32[]{:S(2)}) %copy-start.4) | copy-done | bytes 786456
  69.6 0.0 collective-permute-done.1.far_ref
  69.6 0.0 copy-done
  69.6 0.0 copy-done.1
  69.6 0.0 copy-done.6
  69.7 0.0 copy-start.2
  69.7 1.1 %copy-done.2 = bf16[128,3072]{1,0:T(8,128)(2,1)S(1)} copy-done((bf16[128,3072]{1,0:T(8,128)(2,1)S(1)}, bf16[128,3072]{1,0:T(8,128)(2,1)}, u32[]{:S(2)}) %copy-start.2) | copy-done | bytes 786456
  70.8 0.0 copy-start.5
  70.8 1.1 %copy-done.5 = bf16[128,3072]{1,0:T(8,128)(2,1)S(1)} copy-done((bf16[128,3072]{1,0:T(8,128)(2,1)S(1)}, bf16[128,3072]{1,0:T(8,128)(2,1)}, u32[]{:S(2)}) %copy-start.5) | copy-done | bytes 786456
  71.9 0.0 copy-start.3
  71.9 2.6 %attend_window.1.window_ref = f32[128,3072]{1,0:T(8,128)S(1)} custom-call(s32[24]{0:T(128)S(1)} %copy-done.6, bf16[128,3072]{1,0:T(8,128)(2,1)S(1)} %copy-done.2, bf16[128,3072]{1,0:T(8,128)(2,1)S(1)} %copy-done, bf16[128,3072]{1,0:T(8,128)(2,1)S(1)} %copy-done.1, bf16[128,3072]{1,0:T(8,128)(2,1)S(1)} %copy-done.5, ...), custom_call_target="tpu_custom_call" | custom-call | tf_op jit(solution)/shard_map/attend_window/pallas_call | solution.py:248
  74.5 0.0 collective-permute-done.7.refs_1_
  74.6 0.0 copy-done.3
  74.6 3.5 %attend_cross.1 = bf16[128,3072]{1,0:T(8,128)(2,1)} custom-call(bf16[128,3072]{1,0:T(8,128)(2,1)S(1)} %copy-done.3, bf16[96,3072]{1,0:T(8,128)(2,1)} %pad_maximum_fusion.refs_0_, bf16[96,3072]{1,0:T(8,128)(2,1)} %collective-permute-done.7.refs_1_), custom_call_target="tpu_custom_call" | custom-call | tf_op jit(solution)/shard_map/attend_cross/pallas_call | solution.py:213
  78.1 0.0 all-to-all-done.1.coarse_ref
  78.1 1.2 %finish.1 = bf16[128,3072]{1,0:T(8,128)(2,1)} custom-call(f32[128,3072]{1,0:T(8,128)S(1)} %attend_window.1.window_ref, bf16[8,32,384]{2,1,0:T(8,128)(2,1)S(1)} %all-to-all-done.1.coarse_ref), custom_call_target="tpu_custom_call" | custom-call | tf_op jit(solution)/shard_map/finish/pallas_call | solution.py:273
  (2 shorter events, 0.1 us)
Async XLA Ops:
  3.4 22.2 %all-to-all-start = ((bf16[8,96,384]{2,1,0:T(8,128)(2,1)}), bf16[8,96,384]{2,1,0:T(8,128)(2,1)S(1)}, u32[]{:S(2)}, u32[]{:S(2)}) async-start(bf16[8,96,384]{2,1,0:T(8,128)(2,1)} %get-tuple-element.8), calls=%async_computation | async-start | bytes 1179648 | tf_op jit(solution)/shard_map/all_to_all | solution.py:313
  9.7 4.3 %collective-permute-start.3 = (f32[8,3072]{1,0:T(8,128)S(1)}, f32[8,3072]{1,0:T(8,128)S(1)}, u32[]{:S(2)}, u32[]{:S(2)}) collective-permute-start(f32[8,3072]{1,0:T(8,128)S(1)} %get-tuple-element.9.refs_0_), channel_id=1, source_target_pairs={{0,2},{1,3},{2,0},{3,1},{4,6},{5,7},{6,4},{7,5},{8,10},{9,11},{10,... | collective-permute-start | bytes 294920 | tf_op jit(solution)/shard_map/ppermute | solution.py:304
  14.1 11.5 %collective-permute-start.6 = (bf16[24,3072]{1,0:T(8,128)(2,1)S(1)}, bf16[24,3072]{1,0:T(8,128)(2,1)S(1)}, u32[]{:S(2)}, u32[]{:S(2)}) collective-permute-start(bf16[24,3072]{1,0:T(8,128)(2,1)S(1)} %split_pooled.1), channel_id=1, source_target_pairs={{0,12},{1,13},{2,14},{3,15},{4,0},{5,1},{6,2},{7,3},{8,4},{9,5},{1... | collective-permute-start | bytes 442376 | tf_op jit(solution)/shard_map/ppermute | solution.py:304
  16.9 21.2 %collective-permute-start.5 = (bf16[24,3072]{1,0:T(8,128)(2,1)S(1)}, bf16[24,3072]{1,0:T(8,128)(2,1)S(1)}, u32[]{:S(2)}, u32[]{:S(2)}) collective-permute-start(bf16[24,3072]{1,0:T(8,128)(2,1)S(1)} %split_pooled.1), channel_id=1, source_target_pairs={{0,8},{1,9},{2,10},{3,11},{4,12},{5,13},{6,14},{7,15},{8,0},{9,1},... | collective-permute-start | bytes 442376 | tf_op jit(solution)/shard_map/ppermute | solution.py:304
  16.9 21.2 %collective-permute-start.4 = (bf16[24,3072]{1,0:T(8,128)(2,1)S(1)}, bf16[24,3072]{1,0:T(8,128)(2,1)}, u32[]{:S(2)}, u32[]{:S(2)}) collective-permute-start(bf16[24,3072]{1,0:T(8,128)(2,1)S(1)} %split_pooled.1), channel_id=1, source_target_pairs={{0,4},{1,5},{2,6},{3,7},{4,8},{5,9},{6,10},{7,11},{8,12},{9,13},{1... | collective-permute-start | bytes 442376 | tf_op jit(solution)/shard_map/ppermute | solution.py:304
  17.5 51.2 %collective-permute-start = (bf16[128,3072]{1,0:T(8,128)(2,1)}, bf16[128,3072]{1,0:T(8,128)(2,1)S(1)}, u32[]{:S(2)}, u32[]{:S(2)}) collective-permute-start(bf16[128,3072]{1,0:T(8,128)(2,1)} %get-tuple-element.6), channel_id=1, source_target_pairs={{0,2},{1,3},{4,6},{5,7},{8,10},{9,11},{12,14},{13,15},{2,0},{3,1},... | collective-permute-start | bytes 2359304 | tf_op jit(solution)/shard_map/ppermute | solution.py:320
  18.7 50.9 %collective-permute-start.1 = (bf16[128,3072]{1,0:T(8,128)(2,1)}, bf16[128,3072]{1,0:T(8,128)(2,1)}, u32[]{:S(2)}, u32[]{:S(2)}) collective-permute-start(bf16[128,3072]{1,0:T(8,128)(2,1)} %get-tuple-element.7), channel_id=1, source_target_pairs={{2,4},{3,5},{6,8},{7,9},{10,12},{11,13},{4,2},{5,3},{8,6},{9,7},{1... | collective-permute-start | bytes 2359304 | tf_op jit(solution)/shard_map/ppermute | solution.py:320
  25.6 44.0 %copy-start = (bf16[128,3072]{1,0:T(8,128)(2,1)S(1)}, bf16[128,3072]{1,0:T(8,128)(2,1)}, u32[]{:S(2)}) copy-start(bf16[128,3072]{1,0:T(8,128)(2,1)} %key_ref.1) | copy-start | bytes 2359300
  25.6 44.0 %copy-start.1 = (bf16[128,3072]{1,0:T(8,128)(2,1)S(1)}, bf16[128,3072]{1,0:T(8,128)(2,1)}, u32[]{:S(2)}) copy-start(bf16[128,3072]{1,0:T(8,128)(2,1)} %value_ref.1) | copy-start | bytes 2359300
  25.6 44.0 %copy-start.6 = (s32[24]{0:T(128)S(1)}, s32[24]{0:T(128)}, u32[]{:S(2)}) copy-start(s32[24]{0:T(128)} %reach.1) | copy-start | bytes 292
  25.6 33.4 %collective-permute-start.2 = (bf16[8,64,384]{2,1,0:T(8,128)(2,1)S(1)}, bf16[8,64,384]{2,1,0:T(8,128)(2,1)S(1)}, u32[]{:S(2)}, u32[]{:S(2)}) collective-permute-start(bf16[8,64,384]{2,1,0:T(8,128)(2,1)S(1)} %slice.4), channel_id=1, source_target_pairs={{0,2},{1,3},{2,0},{3,1},{4,6},{5,7},{6,4},{7,5},{8,10},{9,11},{10,... | collective-permute-start | bytes 1179656 | tf_op jit(solution)/shard_map/ppermute | solution.py:304
  40.0 34.6 %collective-permute-start.7 = (bf16[96,3072]{1,0:T(8,128)(2,1)}, bf16[96,3072]{1,0:T(8,128)(2,1)}, u32[]{:S(2)}, u32[]{:S(2)}) collective-permute-start(bf16[96,3072]{1,0:T(8,128)(2,1)} %pad_maximum_fusion.refs_0_), channel_id=1, source_target_pairs={{0,1},{1,0},{2,3},{3,2},{4,5},{5,4},{6,7},{7,6},{8,9},{9,8},{10,11... | collective-permute-start | bytes 1769480 | tf_op jit(solution)/shard_map/ppermute | solution.py:304
  60.6 17.5 %all-to-all-start.1 = ((bf16[8,32,384]{2,1,0:T(8,128)(2,1)}), bf16[8,32,384]{2,1,0:T(8,128)(2,1)S(1)}, u32[]{:S(2)}, u32[]{:S(2)}) async-start(bf16[8,32,384]{2,1,0:T(8,128)(2,1)} %attend_coarse.1), calls=%async_computation.1 | async-start | bytes 393216 | tf_op jit(solution)/shard_map/all_to_all | solution.py:313
  68.8 0.9 %copy-start.4 = (bf16[128,3072]{1,0:T(8,128)(2,1)}, bf16[128,3072]{1,0:T(8,128)(2,1)S(1)}, u32[]{:S(2)}) copy-start(bf16[128,3072]{1,0:T(8,128)(2,1)S(1)} %collective-permute-done.pair_ref) | copy-start | bytes 2359300
  69.7 1.1 %copy-start.2 = (bf16[128,3072]{1,0:T(8,128)(2,1)S(1)}, bf16[128,3072]{1,0:T(8,128)(2,1)}, u32[]{:S(2)}) copy-start(bf16[128,3072]{1,0:T(8,128)(2,1)} %query_ref.3) | copy-start | bytes 2359300
  70.8 1.1 %copy-start.5 = (bf16[128,3072]{1,0:T(8,128)(2,1)S(1)}, bf16[128,3072]{1,0:T(8,128)(2,1)}, u32[]{:S(2)}) copy-start(bf16[128,3072]{1,0:T(8,128)(2,1)} %copy-done.4) | copy-start | bytes 2359300
  71.9 2.6 %copy-start.3 = (bf16[128,3072]{1,0:T(8,128)(2,1)S(1)}, bf16[128,3072]{1,0:T(8,128)(2,1)}, u32[]{:S(2)}) copy-start(bf16[128,3072]{1,0:T(8,128)(2,1)} %query_ref.3) | copy-start | bytes 2359300

commit v3 on v2

--- a/solution.py
+++ b/solution.py
@@ -21,15 +21,21 @@
 SCALE = HD**-0.5
 MASKED = -1e30
 FAR = 1 << 20
-GRANT = pltpu.CompilerParams(vmem_limit_bytes=20 << 20)
+GRANT = pltpu.CompilerParams(vmem_limit_bytes=12 << 20)
+
 
 VMEM = pl.BlockSpec(memory_space=pltpu.VMEM)
 SMEM = pl.BlockSpec(memory_space=pltpu.SMEM)
 HBM = pl.BlockSpec(memory_space=pltpu.HBM)
+ANY = pl.BlockSpec(memory_space=pl.ANY)
 
 
 def streamed(value):
     return pltpu.with_memory_space_constraint(value, pltpu.HBM)
+
+
+def resident(value):
+    return pltpu.with_memory_space_constraint(value, pltpu.VMEM)
 
 
 def dot_rows(left, right):
@@ -65,8 +71,10 @@
     fine_value_hbm,
     slots_hbm,
     pooled_ref,
-    pair_hbm,
-    far_hbm,
+    pair_key_hbm,
+    pair_value_hbm,
+    far_key_hbm,
+    far_value_hbm,
     coarse_buf,
     fine_buf,
     in_sem,
@@ -89,13 +97,12 @@
     stores = []
     for index in range(2):
         loads[index].wait()
+        pair_hbm, far_hbm = ((pair_key_hbm, far_key_hbm), (pair_value_hbm, far_value_hbm))[index]
         for side, (target, last) in enumerate(((pair_hbm, 1 - odd), (far_hbm, odd))):
             start = pl.multiple_of(last * (fine_rows - edge), edge)
             stores.append(
                 pltpu.make_async_copy(
-                    fine_buf.at[index, pl.ds(start, edge)],
-                    target.at[pl.ds(index * edge, edge)],
-                    edge_sem.at[index, side],
+                    fine_buf.at[index, pl.ds(start, edge)], target, edge_sem.at[index, side]
                 )
             )
             stores[-1].start()
@@ -119,7 +126,7 @@
 def pack(coarse_query, coarse_key, coarse_value, fine_key, fine_value, groups, tiles_across):
     rows, width = coarse_query.shape
     kind = coarse_query.dtype
-    halo = pltpu.HBM((2 * HALO_F * PLANE, width), kind)
+    halo = pltpu.HBM((HALO_F * PLANE, width), kind)
     return pl.pallas_call(
         functools.partial(pack_kernel, tiles_across),
         out_shape=(
@@ -127,9 +134,11 @@
             jax.ShapeDtypeStruct((2 * TT, width), jnp.float32),
             halo,
             halo,
+            halo,
+            halo,
         ),
         in_specs=[HBM] * 5,
-        out_specs=(HBM, VMEM, HBM, HBM),
+        out_specs=(HBM, VMEM, HBM, HBM, HBM, HBM),
         scratch_shapes=[
             pltpu.VMEM((3, rows, width), kind),
             pltpu.VMEM((2,) + fine_key.shape, kind),
@@ -210,19 +219,31 @@
 
 
 def attend_cross(fine_query, tokens, chunk):
+    rows, width = fine_query.shape
+    columns = width // 2 if width % (2 * HD) == 0 else width
     return pl.pallas_call(
         functools.partial(cross_kernel, chunk),
         out_shape=jax.ShapeDtypeStruct(fine_query.shape, jnp.bfloat16),
-        in_specs=[VMEM] * (1 + len(tokens)),
-        out_specs=VMEM,
+        grid=(width // columns,),
+        in_specs=[pl.BlockSpec((t.shape[0], columns), lambda c: (0, c)) for t in (fine_query, *tokens)],
+        out_specs=pl.BlockSpec((rows, columns), lambda c: (0, c)),
         compiler_params=GRANT,
         name="attend_cross",
-    )(fine_query, *tokens)
-
-
-def window_kernel(tiles_across, reach, query_ref, key_ref, value_ref, pair_ref, far_ref, out_ref, bias):
-    rows, width = query_ref.shape
-    edge = HALO_F * PLANE
+    )(streamed(fine_query), *tokens)
+
+
+def window_kernel(tiles_across, reach, *refs):
+    *sources, out_ref, held, edges, bias, sem = refs
+    rows, width = out_ref.shape
+    parts, columns = sem.shape[1], width // sem.shape[1]
+    edge = edges.shape[1]
+    loads = []
+    for part in range(parts):
+        span = pl.ds(part * columns, columns)
+        for index, source in enumerate(sources):
+            target = held.at[index] if index < 3 else edges.at[index - 3]
+            loads.append(pltpu.make_async_copy(source.at[:, span], target.at[:, span], sem.at[index, part]))
+            loads[-1].start()
     total = rows + 2 * edge
     time_tile = lax.axis_index("seq") // tiles_across
     later = time_tile % 2 == 0
@@ -235,25 +256,37 @@
     distance = jnp.where((absolute >= 0) & (absolute < NT * TT), jnp.abs(row_frame - key_frame), FAR)
     for limit in range(HALO_F):
         bias[limit] = jnp.where(distance <= limit + 1, 0.0, MASKED)
+    heads = columns // HD
     for head in range(width // HD):
+        if head % heads == 0:
+            for load in loads[head // heads * len(sources) : (head // heads + 1) * len(sources)]:
+                load.wait()
         cut = head_cut(head)
-        keys = jnp.concatenate([key_ref[:, cut], pair_ref[:edge, cut], far_ref[:edge, cut]], axis=0)
-        values = jnp.concatenate([value_ref[:, cut], pair_ref[edge:, cut], far_ref[edge:, cut]], axis=0)
-        scores = dot_rows(query_ref[:, cut], keys) * SCALE + bias[reach[head] - 1]
+        keys = jnp.concatenate([held[1, :, cut], edges[0, :, cut], edges[2, :, cut]], axis=0)
+        values = jnp.concatenate([held[2, :, cut], edges[1, :, cut], edges[3, :, cut]], axis=0)
+        scores = dot_rows(held[0, :, cut], keys) * SCALE + bias[reach[head] - 1]
         out_ref[:, cut] = blend(scores, values)
 
 
-def attend_window(head_reach, fine_query, fine_key, fine_value, pair, far, tiles_across):
+def attend_window(head_reach, fine_query, fine_key, fine_value, halo, tiles_across):
     rows, width = fine_query.shape
+    kind = fine_query.dtype
+    sources = (fine_query, fine_key, fine_value, *halo)
+    parts = 4 if width % (4 * HD) == 0 else 1
     return pl.pallas_call(
         functools.partial(window_kernel, tiles_across),
         out_shape=jax.ShapeDtypeStruct((rows, width), jnp.float32),
-        in_specs=[SMEM] + [VMEM] * 5,
+        in_specs=[SMEM] + [HBM] * 3 + [ANY] * len(halo),
         out_specs=VMEM,
-        scratch_shapes=[pltpu.VMEM((HALO_F, rows, 2 * rows), jnp.float32)],
+        scratch_shapes=[
+            pltpu.VMEM((3, rows, width), kind),
+            pltpu.VMEM((4,) + halo[0].shape, kind),
+            pltpu.VMEM((HALO_F, rows, 2 * rows), jnp.float32),
+            pltpu.SemaphoreType.DMA((len(sources), parts)),
+        ],
         compiler_params=GRANT,
         name="attend_window",
-    )(head_reach, fine_query, fine_key, fine_value, pair, far)
+    )(head_reach, *map(streamed, sources[:3]), *halo)
 
 
 def finish_kernel(window_ref, coarse_ref, out_ref):
@@ -277,7 +310,7 @@
         out_specs=VMEM,
         compiler_params=GRANT,
         name="finish",
-    )(window, returned)
+    )(resident(window), resident(returned))
 
 
 def shards(coarse_query, coarse_key, coarse_value, fine_query, fine_key, fine_value, head_reach):
@@ -312,19 +345,32 @@
     def exchange(slots):
         return lax.all_to_all(slots, "seq", 0, 0, tiled=True, axis_index_groups=same_block)
 
-    edges = [(j, j + tiles_across) for j in range(devices - tiles_across)]
-    early = [(a, b) for a, b in edges if (a // tiles_across) % 2 == 0]
-    late = [(a, b) for a, b in edges if (a // tiles_across) % 2 == 1]
-
-    def swap(value, links):
-        return lax.ppermute(value, "seq", links + [(b, a) for a, b in links])
-
-    slots, pooled, pair_edge, far_edge = pack(
+    def between_tiles(value, move):
+        ends = [(t, t + move(t)) for t in range(NT)]
+        links = [
+            (a * tiles_across + r, b * tiles_across + r)
+            for a, b in ends
+            if 0 <= b < NT
+            for r in range(tiles_across)
+        ]
+        return lax.ppermute(value, "seq", links)
+
+    def to_pair(value):
+        return between_tiles(value, lambda t: 1 - 2 * (t % 2))
+
+    def to_far(value):
+        return between_tiles(value, lambda t: 2 * (t % 2) - 1)
+
+    def to_next_pair(value):
+        return between_tiles(value, lambda t: 2 - 4 * (t % 2))
+
+    slots, pooled, pair_key, pair_value, far_key, far_value = pack(
         coarse_query, coarse_key, coarse_value, fine_key, fine_value, groups, tiles_across
     )
-    pair = swap(pair_edge, early)
+    pieces = [pooled] + over_blocks(pooled)
+    far_value = to_pair(far_value)
+    pair_key = to_pair(pair_key)
     received = exchange(slots)
-    pieces = [pooled] + over_blocks(pooled)
     token_part = split_pooled(pieces)
     pieces = [token_part] + over_outer(token_part)
     tokens = jnp.concatenate(pieces, axis=0)
@@ -332,11 +378,15 @@
     coarse_rows = coarse_query.shape[0]
     coarse_keys = received[:, coarse_rows:]
     others = over_blocks(coarse_keys)
-    far = swap(far_edge, late)
+    pair_value = to_pair(pair_value)
+    far_value = to_next_pair(far_value)
+    far_key = to_far(far_key)
+    halo = (pair_key, pair_value, far_key, far_value)
     cross_result = attend_cross(fine_query, all_tokens, token_part.shape[0])
     attended = attend_coarse(received, others)
     returned = exchange(attended)
-    window = attend_window(head_reach, fine_query, fine_key, fine_value, pair, far, tiles_across)
+    head_reach, cross_result = lax.optimization_barrier((head_reach, cross_result))
+    window = attend_window(head_reach, fine_query, fine_key, fine_value, halo, tiles_across)
     fine_result = finish(window, returned)
     return (fine_result, cross_result)
 

time: 79.8 us -> 74.7 us (0.936)
  the two profiles are of different devices: /device:TPU:1 before, /device:TPU:0 now
where the time goes in v3:
time: 74.7 us; the launch traced here: 74.3 us
  waiting for transfers between devices  30.3 us (41%)
  starting transfers between devices  28 us (37%)
  Pallas kernels  13.5 us (18%)
  local copies, waits for them, and re-layouts  1.79 us (2%)
  between operations  0.75 us (1%)
    ppermute x6, waiting for transfers between devices, around(): moved.append(lax.ppermute(value, 'seq', links))  14 us
    ppermute x5, starting transfers between devices, between_tiles(): return lax.ppermute(value, 'seq', links)  10.4 us
    ppermute x5, waiting for transfers between devices, between_tiles(): return lax.ppermute(value, 'seq', links)  10.2 us
    all_to_all x2, starting transfers between devices, exchange(): lax.all_to_all(slots, 'seq', 0, 0, tiled=True, axis_index_groups=same_block)  9.89 us
    ppermute x6, starting transfers between devices, around(): moved.append(lax.ppermute(value, 'seq', links))  7.73 us
    all_to_all x2, waiting for transfers between devices, exchange(): lax.all_to_all(slots, 'seq', 0, 0, tiled=True, axis_index_groups=same_block)  6.11 us
    pallas_call x1, Pallas kernels, attend_window(): pl.pallas_call(functools.partial(window_kernel, tiles_across), out_shape=...  4.21 us
    pallas_call x1, Pallas kernels, attend_cross(): pl.pallas_call(functools.partial(cross_kernel, chunk), out_shape=jax.Shap...  3.69 us
  transfers between devices with their start and end apart: 13, of which 5 were waited for; matrix products, arithmetic and copies ran while one was open for 0% of the time, Pallas kernels for 13%

profile of v3, /device:TPU:0, one launch (start us, length us, event | category | flops | bytes accessed | tf_op | source)
XLA Modules:
  0.0 74.3 jit_solution(4097702321240717074)
XLA Ops:
  0.6 2.7 %pack.1 = (bf16[8,96,384]{2,1,0:T(8,128)(2,1)}, f32[8,3072]{1,0:T(8,128)S(1)}, bf16[64,3072]{1,0:T(8,128)(2,1)}, bf16[64,3072]{1,0:T(8,128)(2,1)}, bf16[64,3072]{1,0:T(8,128)(2,1)}, /*index=5*/bf16[64,3072]{1,0:T(8,128)(2,1)}) custom-call(bf16[32,3072]{1,0:T(8,128)(2,1)} %query_hbm.1, bf16[32,3072]{1,0:T(8,128)(2,1)} %key_hbm.1, bf16[32,3072]{1,0:T(8,128)(2,1)} %value_hbm.1, ...), custom_call_target="tpu_custom_call" | custom-call | tf_op jit(solution)/shard_map/pack/pallas_call | solution.py:130
  3.4 0.0 copy-start.3
  3.4 6.5 %all-to-all-start = ((bf16[8,96,384]{2,1,0:T(8,128)(2,1)}), bf16[8,96,384]{2,1,0:T(8,128)(2,1)S(1)}, u32[]{:S(2)}, u32[]{:S(2)}) async-start(bf16[8,96,384]{2,1,0:T(8,128)(2,1)} %get-tuple-element.16), calls=%async_computation | async-start | bytes 1179648 | tf_op jit(solution)/shard_map/all_to_all | solution.py:346
  9.9 1.5 %collective-permute-start = (f32[8,3072]{1,0:T(8,128)S(1)}, f32[8,3072]{1,0:T(8,128)S(1)}, u32[]{:S(2)}, u32[]{:S(2)}) collective-permute-start(f32[8,3072]{1,0:T(8,128)S(1)} %get-tuple-element.10.refs_0_), channel_id=1, source_target_pairs={{0,2},{1,3},{2,0},{3,1},{4,6},{5,7},{6,4},{7,5},{8,10},{9,11},{10,... | collective-permute-start | bytes 294920 | tf_op jit(solution)/shard_map/ppermute | solution.py:337
  11.4 3.7 %collective-permute-done.refs_1_ = f32[8,3072]{1,0:T(8,128)S(1)} collective-permute-done((f32[8,3072]{1,0:T(8,128)S(1)}, f32[8,3072]{1,0:T(8,128)S(1)}, u32[]{:S(2)}, u32[]{:S(2)}) %collective-permute-start) | collective-permute-done | bytes 98336 | tf_op jit(solution)/shard_map/ppermute | solution.py:337
  15.1 3.5 %collective-permute-start.3 = (bf16[24,3072]{1,0:T(8,128)(2,1)S(1)}, bf16[24,3072]{1,0:T(8,128)(2,1)S(1)}, u32[]{:S(2)}, u32[]{:S(2)}) collective-permute-start(bf16[24,3072]{1,0:T(8,128)(2,1)S(1)} %split_pooled.1), channel_id=1, source_target_pairs={{0,12},{1,13},{2,14},{3,15},{4,0},{5,1},{6,2},{7,3},{8,4},{9,5},{1... | collective-permute-start | bytes 442376 | tf_op jit(solution)/shard_map/ppermute | solution.py:337
  18.6 0.0 collective-permute-start.2
  18.6 1.1 %collective-permute-start.1 = (bf16[24,3072]{1,0:T(8,128)(2,1)S(1)}, bf16[24,3072]{1,0:T(8,128)(2,1)S(1)}, u32[]{:S(2)}, u32[]{:S(2)}) collective-permute-start(bf16[24,3072]{1,0:T(8,128)(2,1)S(1)} %split_pooled.1), channel_id=1, source_target_pairs={{0,4},{1,5},{2,6},{3,7},{4,8},{5,9},{6,10},{7,11},{8,12},{9,13},{1... | collective-permute-start | bytes 442376 | tf_op jit(solution)/shard_map/ppermute | solution.py:337
  19.7 0.0 copy-done.3
  19.7 1.5 %collective-permute-start.8 = (bf16[64,3072]{1,0:T(8,128)(2,1)S(1)}, bf16[64,3072]{1,0:T(8,128)(2,1)}, u32[]{:S(2)}, u32[]{:S(2)}) collective-permute-start(bf16[64,3072]{1,0:T(8,128)(2,1)S(1)} %copy-done.3), channel_id=1, source_target_pairs={{0,2},{1,3},{2,0},{3,1},{4,6},{5,7},{6,4},{7,5},{8,10},{9,11},{10,... | collective-permute-start | bytes 1179656 | tf_op jit(solution)/shard_map/ppermute | solution.py:356
  21.2 6.1 %all-to-all-done.own_ref = bf16[8,96,384]{2,1,0:T(8,128)(2,1)S(1)} async-done(((bf16[8,96,384]{2,1,0:T(8,128)(2,1)}), bf16[8,96,384]{2,1,0:T(8,128)(2,1)S(1)}, u32[]{:S(2)}, u32[]{:S(2)}) %all-to-all-start) | async-done | bytes 589856 | tf_op jit(solution)/shard_map/all_to_all | solution.py:346
  27.4 1.6 %collective-permute-start.10 = (bf16[8,64,384]{2,1,0:T(8,128)(2,1)S(1)}, bf16[8,64,384]{2,1,0:T(8,128)(2,1)S(1)}, u32[]{:S(2)}, u32[]{:S(2)}) collective-permute-start(bf16[8,64,384]{2,1,0:T(8,128)(2,1)S(1)} %slice.4), channel_id=1, source_target_pairs={{0,2},{1,3},{2,0},{3,1},{4,6},{5,7},{6,4},{7,5},{8,10},{9,11},{10,... | collective-permute-start | bytes 1179656 | tf_op jit(solution)/shard_map/ppermute | solution.py:337
  28.9 0.0 collective-permute-done.3
  28.9 10.3 %collective-permute-done.2 = bf16[24,3072]{1,0:T(8,128)(2,1)S(1)} collective-permute-done((bf16[24,3072]{1,0:T(8,128)(2,1)S(1)}, bf16[24,3072]{1,0:T(8,128)(2,1)S(1)}, u32[]{:S(2)}, u32[]{:S(2)}) %collective-permute-start.2) | collective-permute-done | bytes 147488 | tf_op jit(solution)/shard_map/ppermute | solution.py:337
  39.3 0.0 collective-permute-done.1
  39.3 0.1 collective-permute-start.4
  39.4 1.6 %collective-permute-start.5 = (bf16[64,3072]{1,0:T(8,128)(2,1)}, bf16[64,3072]{1,0:T(8,128)(2,1)S(1)}, u32[]{:S(2)}, u32[]{:S(2)}) collective-permute-start(bf16[64,3072]{1,0:T(8,128)(2,1)} %get-tuple-element.12), channel_id=1, source_target_pairs={{0,2},{1,3},{2,0},{3,1},{4,6},{5,7},{6,4},{7,5},{8,10},{9,11},{10,... | collective-permute-start | bytes 1179656 | tf_op jit(solution)/shard_map/ppermute | solution.py:356
  40.9 0.5 collective-permute-start.6
  41.5 0.0 collective-permute-done.8
  41.5 0.7 collective-permute-start.7
  42.2 0.0 collective-permute-done.10.refs_0_
  42.2 6.1 %collective-permute-start.9 = (bf16[64,3072]{1,0:T(8,128)(2,1)}, bf16[64,3072]{1,0:T(8,128)(2,1)S(1)}, u32[]{:S(2)}, u32[]{:S(2)}) collective-permute-start(bf16[64,3072]{1,0:T(8,128)(2,1)} %collective-permute-done.8), channel_id=1, source_target_pairs={{0,4},{1,5},{4,8},{5,9},{6,2},{7,3},{8,12},{9,13},{10,6},{11,7},{1... | collective-permute-start | bytes 1179656 | tf_op jit(solution)/shard_map/ppermute | solution.py:356
  48.3 1.5 %attend_coarse.1 = bf16[8,32,384]{2,1,0:T(8,128)(2,1)} custom-call(bf16[8,96,384]{2,1,0:T(8,128)(2,1)S(1)} %all-to-all-done.own_ref, bf16[8,64,384]{2,1,0:T(8,128)(2,1)S(1)} %collective-permute-done.10.refs_0_), custom_call_target="tpu_custom_call" | custom-call | tf_op jit(solution)/shard_map/attend_coarse/pallas_call | solution.py:193
  49.8 3.4 %all-to-all-start.1 = ((bf16[8,32,384]{2,1,0:T(8,128)(2,1)}), bf16[8,32,384]{2,1,0:T(8,128)(2,1)S(1)}, u32[]{:S(2)}, u32[]{:S(2)}) async-start(bf16[8,32,384]{2,1,0:T(8,128)(2,1)} %attend_coarse.1), calls=%async_computation.1 | async-start | bytes 393216 | tf_op jit(solution)/shard_map/all_to_all | solution.py:346
  53.2 0.0 copy-start.2
  53.2 0.0 collective-permute-done.4.refs_1_
  53.2 3.7 %attend_cross.1 = bf16[128,3072]{1,0:T(8,128)(2,1)} custom-call(bf16[128,3072]{1,0:T(8,128)(2,1)} %refs_0_.1, bf16[96,3072]{1,0:T(8,128)(2,1)S(1)} %pad_maximum_fusion.refs_0_, bf16[96,3072]{1,0:T(8,128)(2,1)S(1)} %collective-permute-done.4.refs_1_), custom_call_target="tpu_custom_call" | custom-call | tf_op jit(solution)/shard_map/attend_cross/pallas_call | solution.py:224
  56.9 2.3 %collective-permute-done.5.refs_3_ = bf16[64,3072]{1,0:T(8,128)(2,1)S(1)} collective-permute-done((bf16[64,3072]{1,0:T(8,128)(2,1)}, bf16[64,3072]{1,0:T(8,128)(2,1)S(1)}, u32[]{:S(2)}, u32[]{:S(2)}) %collective-permute-start.5) | collective-permute-done | bytes 393248 | tf_op jit(solution)/shard_map/ppermute | solution.py:356
  59.2 7.9 %collective-permute-done.6.refs_4_ = bf16[64,3072]{1,0:T(8,128)(2,1)S(1)} collective-permute-done((bf16[64,3072]{1,0:T(8,128)(2,1)}, bf16[64,3072]{1,0:T(8,128)(2,1)S(1)}, u32[]{:S(2)}, u32[]{:S(2)}) %collective-permute-start.6) | collective-permute-done | bytes 393248 | tf_op jit(solution)/shard_map/ppermute | solution.py:356
  67.1 0.0 collective-permute-done.7.refs_5_
  67.1 0.0 collective-permute-done.9.refs_6_
  67.1 0.0 copy-start
  67.1 0.7 %copy-done = bf16[64,3072]{1,0:T(8,128)(2,1)} copy-done((bf16[64,3072]{1,0:T(8,128)(2,1)}, bf16[64,3072]{1,0:T(8,128)(2,1)S(1)}, u32[]{:S(2)}) %copy-start) | copy-done | bytes 393240
  67.8 0.0 copy-done.2
  67.8 0.0 copy-start.1
  67.8 1.0 %copy-done.1 = bf16[64,3072]{1,0:T(8,128)(2,1)S(1)} copy-done((bf16[64,3072]{1,0:T(8,128)(2,1)S(1)}, bf16[64,3072]{1,0:T(8,128)(2,1)}, u32[]{:S(2)}) %copy-start.1) | copy-done | bytes 393240
  68.8 4.2 %attend_window.1.window_ref = f32[128,3072]{1,0:T(8,128)S(1)} custom-call(s32[24]{0:T(128)S(1)} %copy-done.2, bf16[128,3072]{1,0:T(8,128)(2,1)} %refs_0_.1, bf16[128,3072]{1,0:T(8,128)(2,1)} %refs_1_.1, bf16[128,3072]{1,0:T(8,128)(2,1)} %refs_2_.1, bf16[64,3072]{1,0:T(8,128)(2,1)S(1)} %collective-permute-done.5.refs_3_, ...), custom_call_target="tpu_custom_call" | custom-call | tf_op jit(solution)/shard_map/attend_window/pallas_call | solution.py:276
  73.0 0.0 all-to-all-done.1.coarse_ref
  73.1 1.2 %finish.1 = bf16[128,3072]{1,0:T(8,128)(2,1)} custom-call(f32[128,3072]{1,0:T(8,128)S(1)} %attend_window.1.window_ref, bf16[8,32,384]{2,1,0:T(8,128)(2,1)S(1)} %all-to-all-done.1.coarse_ref), custom_call_target="tpu_custom_call" | custom-call | tf_op jit(solution)/shard_map/finish/pallas_call | solution.py:306
  (3 shorter events, 0.1 us)
Async XLA Ops:
  3.4 16.4 %copy-start.3 = (bf16[64,3072]{1,0:T(8,128)(2,1)S(1)}, bf16[64,3072]{1,0:T(8,128)(2,1)}, u32[]{:S(2)}) copy-start(bf16[64,3072]{1,0:T(8,128)(2,1)} %get-tuple-element.15) | copy-start | bytes 1179652
  3.4 23.9 %all-to-all-start = ((bf16[8,96,384]{2,1,0:T(8,128)(2,1)}), bf16[8,96,384]{2,1,0:T(8,128)(2,1)S(1)}, u32[]{:S(2)}, u32[]{:S(2)}) async-start(bf16[8,96,384]{2,1,0:T(8,128)(2,1)} %get-tuple-element.16), calls=%async_computation | async-start | bytes 1179648 | tf_op jit(solution)/shard_map/all_to_all | solution.py:346
  9.9 5.2 %collective-permute-start = (f32[8,3072]{1,0:T(8,128)S(1)}, f32[8,3072]{1,0:T(8,128)S(1)}, u32[]{:S(2)}, u32[]{:S(2)}) collective-permute-start(f32[8,3072]{1,0:T(8,128)S(1)} %get-tuple-element.10.refs_0_), channel_id=1, source_target_pairs={{0,2},{1,3},{2,0},{3,1},{4,6},{5,7},{6,4},{7,5},{8,10},{9,11},{10,... | collective-permute-start | bytes 294920 | tf_op jit(solution)/shard_map/ppermute | solution.py:337
  15.1 13.8 %collective-permute-start.3 = (bf16[24,3072]{1,0:T(8,128)(2,1)S(1)}, bf16[24,3072]{1,0:T(8,128)(2,1)S(1)}, u32[]{:S(2)}, u32[]{:S(2)}) collective-permute-start(bf16[24,3072]{1,0:T(8,128)(2,1)S(1)} %split_pooled.1), channel_id=1, source_target_pairs={{0,12},{1,13},{2,14},{3,15},{4,0},{5,1},{6,2},{7,3},{8,4},{9,5},{1... | collective-permute-start | bytes 442376 | tf_op jit(solution)/shard_map/ppermute | solution.py:337
  18.6 20.6 %collective-permute-start.2 = (bf16[24,3072]{1,0:T(8,128)(2,1)S(1)}, bf16[24,3072]{1,0:T(8,128)(2,1)S(1)}, u32[]{:S(2)}, u32[]{:S(2)}) collective-permute-start(bf16[24,3072]{1,0:T(8,128)(2,1)S(1)} %split_pooled.1), channel_id=1, source_target_pairs={{0,8},{1,9},{2,10},{3,11},{4,12},{5,13},{6,14},{7,15},{8,0},{9,1},... | collective-permute-start | bytes 442376 | tf_op jit(solution)/shard_map/ppermute | solution.py:337
  18.6 20.6 %collective-permute-start.1 = (bf16[24,3072]{1,0:T(8,128)(2,1)S(1)}, bf16[24,3072]{1,0:T(8,128)(2,1)S(1)}, u32[]{:S(2)}, u32[]{:S(2)}) collective-permute-start(bf16[24,3072]{1,0:T(8,128)(2,1)S(1)} %split_pooled.1), channel_id=1, source_target_pairs={{0,4},{1,5},{2,6},{3,7},{4,8},{5,9},{6,10},{7,11},{8,12},{9,13},{1... | collective-permute-start | bytes 442376 | tf_op jit(solution)/shard_map/ppermute | solution.py:337
  19.7 21.7 %collective-permute-start.8 = (bf16[64,3072]{1,0:T(8,128)(2,1)S(1)}, bf16[64,3072]{1,0:T(8,128)(2,1)}, u32[]{:S(2)}, u32[]{:S(2)}) collective-permute-start(bf16[64,3072]{1,0:T(8,128)(2,1)S(1)} %copy-done.3), channel_id=1, source_target_pairs={{0,2},{1,3},{2,0},{3,1},{4,6},{5,7},{6,4},{7,5},{8,10},{9,11},{10,... | collective-permute-start | bytes 1179656 | tf_op jit(solution)/shard_map/ppermute | solution.py:356
  27.4 14.8 %collective-permute-start.10 = (bf16[8,64,384]{2,1,0:T(8,128)(2,1)S(1)}, bf16[8,64,384]{2,1,0:T(8,128)(2,1)S(1)}, u32[]{:S(2)}, u32[]{:S(2)}) collective-permute-start(bf16[8,64,384]{2,1,0:T(8,128)(2,1)S(1)} %slice.4), channel_id=1, source_target_pairs={{0,2},{1,3},{2,0},{3,1},{4,6},{5,7},{6,4},{7,5},{8,10},{9,11},{10,... | collective-permute-start | bytes 1179656 | tf_op jit(solution)/shard_map/ppermute | solution.py:337
  39.3 13.9 %collective-permute-start.4 = (bf16[96,3072]{1,0:T(8,128)(2,1)S(1)}, bf16[96,3072]{1,0:T(8,128)(2,1)S(1)}, u32[]{:S(2)}, u32[]{:S(2)}) collective-permute-start(bf16[96,3072]{1,0:T(8,128)(2,1)S(1)} %pad_maximum_fusion.refs_0_), channel_id=1, source_target_pairs={{0,1},{1,0},{2,3},{3,2},{4,5},{5,4},{6,7},{7,6},{8,9},{9,8},{10,11... | collective-permute-start | bytes 1769480 | tf_op jit(solution)/shard_map/ppermute | solution.py:337
  39.4 19.8 %collective-permute-start.5 = (bf16[64,3072]{1,0:T(8,128)(2,1)}, bf16[64,3072]{1,0:T(8,128)(2,1)S(1)}, u32[]{:S(2)}, u32[]{:S(2)}) collective-permute-start(bf16[64,3072]{1,0:T(8,128)(2,1)} %get-tuple-element.12), channel_id=1, source_target_pairs={{0,2},{1,3},{2,0},{3,1},{4,6},{5,7},{6,4},{7,5},{8,10},{9,11},{10,... | collective-permute-start | bytes 1179656 | tf_op jit(solution)/shard_map/ppermute | solution.py:356
  40.9 26.1 %collective-permute-start.6 = (bf16[64,3072]{1,0:T(8,128)(2,1)}, bf16[64,3072]{1,0:T(8,128)(2,1)S(1)}, u32[]{:S(2)}, u32[]{:S(2)}) collective-permute-start(bf16[64,3072]{1,0:T(8,128)(2,1)} %get-tuple-element.13), channel_id=1, source_target_pairs={{0,2},{1,3},{2,0},{3,1},{4,6},{5,7},{6,4},{7,5},{8,10},{9,11},{10,... | collective-permute-start | bytes 1179656 | tf_op jit(solution)/shard_map/ppermute | solution.py:356
  41.5 25.6 %collective-permute-start.7 = (bf16[64,3072]{1,0:T(8,128)(2,1)}, bf16[64,3072]{1,0:T(8,128)(2,1)S(1)}, u32[]{:S(2)}, u32[]{:S(2)}) collective-permute-start(bf16[64,3072]{1,0:T(8,128)(2,1)} %get-tuple-element.14), channel_id=1, source_target_pairs={{2,4},{3,5},{4,2},{5,3},{6,8},{7,9},{8,6},{9,7},{10,12},{11,13},{1... | collective-permute-start | bytes 1179656 | tf_op jit(solution)/shard_map/ppermute | solution.py:356
  42.2 24.9 %collective-permute-start.9 = (bf16[64,3072]{1,0:T(8,128)(2,1)}, bf16[64,3072]{1,0:T(8,128)(2,1)S(1)}, u32[]{:S(2)}, u32[]{:S(2)}) collective-permute-start(bf16[64,3072]{1,0:T(8,128)(2,1)} %collective-permute-done.8), channel_id=1, source_target_pairs={{0,4},{1,5},{4,8},{5,9},{6,2},{7,3},{8,12},{9,13},{10,6},{11,7},{1... | collective-permute-start | bytes 1179656 | tf_op jit(solution)/shard_map/ppermute | solution.py:356
  49.8 23.2 %all-to-all-start.1 = ((bf16[8,32,384]{2,1,0:T(8,128)(2,1)}), bf16[8,32,384]{2,1,0:T(8,128)(2,1)S(1)}, u32[]{:S(2)}, u32[]{:S(2)}) async-start(bf16[8,32,384]{2,1,0:T(8,128)(2,1)} %attend_coarse.1), calls=%async_computation.1 | async-start | bytes 393216 | tf_op jit(solution)/shard_map/all_to_all | solution.py:346
  53.2 14.6 %copy-start.2 = (s32[24]{0:T(128)S(1)}, s32[24]{0:T(128)}, u32[]{:S(2)}) copy-start(s32[24]{0:T(128)} %reach) | copy-start | bytes 292
  67.1 0.7 %copy-start = (bf16[64,3072]{1,0:T(8,128)(2,1)}, bf16[64,3072]{1,0:T(8,128)(2,1)S(1)}, u32[]{:S(2)}) copy-start(bf16[64,3072]{1,0:T(8,128)(2,1)S(1)} %collective-permute-done.9.refs_6_) | copy-start | bytes 1179652
  67.8 1.0 %copy-start.1 = (bf16[64,3072]{1,0:T(8,128)(2,1)S(1)}, bf16[64,3072]{1,0:T(8,128)(2,1)}, u32[]{:S(2)}) copy-start(bf16[64,3072]{1,0:T(8,128)(2,1)} %copy-done) | copy-start | bytes 1179652

commit v4 on v3

--- a/solution.py
+++ b/solution.py
@@ -62,8 +62,24 @@
     return jnp.sum(cells, axis=1) * CELLS**-0.5
 
 
+def outer_slots(reach, heads):
+    near, wide = jnp.int32(0), jnp.int32(0)
+    slots = []
+    for head in range(heads):
+        is_wide = (reach[head] > 1).astype(jnp.int32)
+        slots.append(pl.multiple_of(jnp.where(is_wide == 1, wide, heads - 1 - near) * HD, HD))
+        wide += is_wide
+        near += 1 - is_wide
+    return slots
+
+
+def sent_wide(heads):
+    return max(1, heads * 2 // 3)
+
+
 def pack_kernel(
     tiles_across,
+    reach_hbm,
     query_hbm,
     key_hbm,
     value_hbm,
@@ -72,11 +88,15 @@
     slots_hbm,
     pooled_ref,
     pair_key_hbm,
+    far_key_hbm,
     pair_value_hbm,
-    far_key_hbm,
     far_value_hbm,
+    pair_rest_hbm,
+    far_rest_hbm,
     coarse_buf,
     fine_buf,
+    outer_buf,
+    reach,
     in_sem,
     slot_sem,
     edge_sem,
@@ -85,27 +105,52 @@
     rows, width = query_hbm.shape
     fine_rows = fine_key_hbm.shape[0]
     group_width = width // groups
-    edge = HALO_F * PLANE
+    heads = width // HD
+    kept = sent_wide(heads) * HD
     odd = (lax.axis_index("seq") // tiles_across) % 2
     loads = []
     for index, source in enumerate((fine_key_hbm, fine_value_hbm)):
         loads.append(pltpu.make_async_copy(source, fine_buf.at[index], in_sem.at[index]))
     for index, source in enumerate((query_hbm, key_hbm, value_hbm)):
         loads.append(pltpu.make_async_copy(source, coarse_buf.at[index], in_sem.at[2 + index]))
+    reach_load = pltpu.make_async_copy(reach_hbm, reach, in_sem.at[5])
+    reach_load.start()
     for load in loads:
         load.start()
+    reach_load.wait()
     stores = []
+
+    def send(source, target, sem):
+        stores.append(pltpu.make_async_copy(source, target, sem))
+        stores[-1].start()
+
+    slots = outer_slots(reach, heads)
+    sides = ((pair_key_hbm, far_key_hbm), (pair_value_hbm, far_value_hbm))
     for index in range(2):
         loads[index].wait()
-        pair_hbm, far_hbm = ((pair_key_hbm, far_key_hbm), (pair_value_hbm, far_value_hbm))[index]
-        for side, (target, last) in enumerate(((pair_hbm, 1 - odd), (far_hbm, odd))):
-            start = pl.multiple_of(last * (fine_rows - edge), edge)
-            stores.append(
-                pltpu.make_async_copy(
-                    fine_buf.at[index, pl.ds(start, edge)], target, edge_sem.at[index, side]
-                )
+        for side, last in enumerate((1 - odd, odd)):
+            start = pl.multiple_of(last * (fine_rows - PLANE), PLANE)
+            send(
+                fine_buf.at[index, pl.ds(start, PLANE)],
+                sides[index][side].at[:, pl.ds(0, width)],
+                edge_sem.at[index, side, 0],
             )
-            stores[-1].start()
+        for head in range(heads):
+            cut = head_cut(head)
+            span = pl.ds(slots[head], HD)
+            outer_buf[index, 1 - odd, :, span] = fine_buf[index, PLANE : 2 * PLANE, cut]
+            outer_buf[index, odd, :, span] = fine_buf[index, fine_rows - 2 * PLANE : fine_rows - PLANE, cut]
+        for side, rest in enumerate((pair_rest_hbm, far_rest_hbm)):
+            send(
+                outer_buf.at[index, side, :, pl.ds(0, kept)],
+                sides[index][side].at[:, pl.ds(width, kept)],
+                edge_sem.at[index, side, 1],
+            )
+            send(
+                outer_buf.at[index, side, :, pl.ds(kept, width - kept)],
+                rest.at[:, pl.ds(index * (width - kept), width - kept)],
+                edge_sem.at[index, side, 2],
+            )
     for index in range(3):
         loads[2 + index].wait()
         for group in range(groups):
@@ -123,10 +168,12 @@
         store.wait()
 
 
-def pack(coarse_query, coarse_key, coarse_value, fine_key, fine_value, groups, tiles_across):
+def pack(head_reach, coarse_query, coarse_key, coarse_value, fine_key, fine_value, groups, tiles_across):
     rows, width = coarse_query.shape
     kind = coarse_query.dtype
-    halo = pltpu.HBM((HALO_F * PLANE, width), kind)
+    kept = sent_wide(width // HD) * HD
+    halo = pltpu.HBM((PLANE, width + kept), kind)
+    rest = pltpu.HBM((PLANE, 2 * (width - kept)), kind)
     return pl.pallas_call(
         functools.partial(pack_kernel, tiles_across),
         out_shape=(
@@ -136,19 +183,23 @@
             halo,
             halo,
             halo,
+            rest,
+            rest,
         ),
-        in_specs=[HBM] * 5,
-        out_specs=(HBM, VMEM, HBM, HBM, HBM, HBM),
+        in_specs=[HBM] * 6,
+        out_specs=(HBM, VMEM) + (HBM,) * 6,
         scratch_shapes=[
             pltpu.VMEM((3, rows, width), kind),
             pltpu.VMEM((2,) + fine_key.shape, kind),
-            pltpu.SemaphoreType.DMA((5,)),
+            pltpu.VMEM((2, 2, PLANE, width), kind),
+            pltpu.SMEM(head_reach.shape, head_reach.dtype),
+            pltpu.SemaphoreType.DMA((6,)),
             pltpu.SemaphoreType.DMA((3, groups)),
-            pltpu.SemaphoreType.DMA((2, 2)),
+            pltpu.SemaphoreType.DMA((2, 2, 3)),
         ],
         compiler_params=GRANT,
         name="pack",
-    )(*map(streamed, (coarse_query, coarse_key, coarse_value, fine_key, fine_value)))
+    )(*map(streamed, (head_reach, coarse_query, coarse_key, coarse_value, fine_key, fine_value)))
 
 
 def split_pooled_kernel(*refs):
@@ -200,29 +251,25 @@
     )(own, *others)
 
 
-def cross_kernel(chunk, query_ref, *refs):
+def cross_kernel(query_ref, *refs):
     *token_refs, out_ref = refs
-    third = chunk // 3
+    third = token_refs[0].shape[0] // 3
     for head in range(query_ref.shape[1] // HD):
         cut = head_cut(head)
-        high, low, values = [], [], []
-        for ref in token_refs:
-            rows = ref[:, cut].astype(jnp.float32)
-            for start in range(0, rows.shape[0], chunk):
-                high.append(rows[start : start + third])
-                low.append(rows[start + third : start + 2 * third])
-                values.append(rows[start + 2 * third : start + chunk])
-        high, low, values = (jnp.concatenate(p, axis=0).astype(jnp.bfloat16) for p in (high, low, values))
+        high, low, values = (
+            jnp.concatenate([ref[part * third : (part + 1) * third, cut] for ref in token_refs], axis=0)
+            for part in range(3)
+        )
         query = query_ref[:, cut]
         scores = dot_rows(jnp.concatenate([query, query], axis=1), jnp.concatenate([high, low], axis=1))
         out_ref[:, cut] = blend(scores * SCALE, values).astype(out_ref.dtype)
 
 
-def attend_cross(fine_query, tokens, chunk):
+def attend_cross(fine_query, tokens):
     rows, width = fine_query.shape
     columns = width // 2 if width % (2 * HD) == 0 else width
     return pl.pallas_call(
-        functools.partial(cross_kernel, chunk),
+        cross_kernel,
         out_shape=jax.ShapeDtypeStruct(fine_query.shape, jnp.bfloat16),
         grid=(width // columns,),
         in_specs=[pl.BlockSpec((t.shape[0], columns), lambda c: (0, c)) for t in (fine_query, *tokens)],
@@ -233,60 +280,86 @@
 
 
 def window_kernel(tiles_across, reach, *refs):
-    *sources, out_ref, held, edges, bias, sem = refs
+    query_hbm, key_hbm, value_hbm, *halo, pair_rest, far_rest, out_ref, held, inner, outer, bias, sem, outer_sem = refs
     rows, width = out_ref.shape
-    parts, columns = sem.shape[1], width // sem.shape[1]
-    edge = edges.shape[1]
+    heads = width // HD
+    kept = sent_wide(heads) * HD
+    parts = sem.shape[1]
+    columns = width // parts
+    outers = []
+    for index in range(4):
+        rest = (pair_rest, far_rest)[index % 2].at[:, pl.ds(index // 2 * (width - kept), width - kept)]
+        outers.append(
+            pltpu.make_async_copy(
+                halo[index].at[:, pl.ds(width, kept)], outer.at[index, :, pl.ds(0, kept)], outer_sem.at[index, 0]
+            )
+        )
+        outers.append(
+            pltpu.make_async_copy(rest, outer.at[index, :, pl.ds(kept, width - kept)], outer_sem.at[index, 1])
+        )
+    for load in outers:
+        load.start()
     loads = []
     for part in range(parts):
         span = pl.ds(part * columns, columns)
-        for index, source in enumerate(sources):
-            target = held.at[index] if index < 3 else edges.at[index - 3]
+        for index, source in enumerate((query_hbm, key_hbm, value_hbm, *halo)):
+            target = held.at[index] if index < 3 else inner.at[index - 3]
             loads.append(pltpu.make_async_copy(source.at[:, span], target.at[:, span], sem.at[index, part]))
             loads[-1].start()
-    total = rows + 2 * edge
+    slots = outer_slots(reach, heads)
+    total = 2 * rows
     time_tile = lax.axis_index("seq") // tiles_across
     later = time_tile % 2 == 0
     row_frame = lax.broadcasted_iota(jnp.int32, (rows, total), 0) // PLANE
     column = lax.broadcasted_iota(jnp.int32, (rows, total), 1)
-    pair_frame = (column - rows) // PLANE + jnp.where(later, TT, -HALO_F)
-    far_frame = (column - rows - edge) // PLANE + jnp.where(later, -HALO_F, TT)
-    key_frame = jnp.where(column < rows, column // PLANE, jnp.where(column < rows + edge, pair_frame, far_frame))
+    beyond = jnp.maximum(column - rows, 0) // PLANE
+    depth = beyond % HALO_F
+    after = (beyond < HALO_F) == later
+    key_frame = jnp.where(column < rows, column // PLANE, jnp.where(after, TT + depth, -1 - depth))
     absolute = key_frame + time_tile * TT
     distance = jnp.where((absolute >= 0) & (absolute < NT * TT), jnp.abs(row_frame - key_frame), FAR)
     for limit in range(HALO_F):
         bias[limit] = jnp.where(distance <= limit + 1, 0.0, MASKED)
-    heads = columns // HD
-    for head in range(width // HD):
-        if head % heads == 0:
-            for load in loads[head // heads * len(sources) : (head // heads + 1) * len(sources)]:
+    for load in outers:
+        load.wait()
+    chunk = columns // HD
+    for head in range(heads):
+        if head % chunk == 0:
+            for load in loads[head // chunk * 7 : (head // chunk + 1) * 7]:
                 load.wait()
         cut = head_cut(head)
-        keys = jnp.concatenate([held[1, :, cut], edges[0, :, cut], edges[2, :, cut]], axis=0)
-        values = jnp.concatenate([held[2, :, cut], edges[1, :, cut], edges[3, :, cut]], axis=0)
-        scores = dot_rows(held[0, :, cut], keys) * SCALE + bias[reach[head] - 1]
-        out_ref[:, cut] = blend(scores, values)
-
-
-def attend_window(head_reach, fine_query, fine_key, fine_value, halo, tiles_across):
+        span = pl.ds(slots[head], HD)
+
+        def gathered(own, kind):
+            pieces = [held[own, :, cut]]
+            for side in (kind, kind + 1):
+                pieces += [inner[side, :, cut], outer[side, :, span]]
+            return jnp.concatenate(pieces, axis=0)
+
+        scores = dot_rows(held[0, :, cut], gathered(1, 0)) * SCALE + bias[reach[head] - 1]
+        out_ref[:, cut] = blend(scores, gathered(2, 2))
+
+
+def attend_window(head_reach, fine_query, fine_key, fine_value, halo, rest, tiles_across):
     rows, width = fine_query.shape
     kind = fine_query.dtype
-    sources = (fine_query, fine_key, fine_value, *halo)
     parts = 4 if width % (4 * HD) == 0 else 1
     return pl.pallas_call(
         functools.partial(window_kernel, tiles_across),
         out_shape=jax.ShapeDtypeStruct((rows, width), jnp.float32),
-        in_specs=[SMEM] + [HBM] * 3 + [ANY] * len(halo),
+        in_specs=[SMEM] + [HBM] * 3 + [ANY] * 6,
         out_specs=VMEM,
         scratch_shapes=[
             pltpu.VMEM((3, rows, width), kind),
-            pltpu.VMEM((4,) + halo[0].shape, kind),
+            pltpu.VMEM((4, PLANE, width), kind),
+            pltpu.VMEM((4, PLANE, width), kind),
             pltpu.VMEM((HALO_F, rows, 2 * rows), jnp.float32),
-            pltpu.SemaphoreType.DMA((len(sources), parts)),
+            pltpu.SemaphoreType.DMA((7, parts)),
+            pltpu.SemaphoreType.DMA((4, 2)),
         ],
         compiler_params=GRANT,
         name="attend_window",
-    )(head_reach, *map(streamed, sources[:3]), *halo)
+    )(head_reach, *map(streamed, (fine_query, fine_key, fine_value)), *halo, *rest)
 
 
 def finish_kernel(window_ref, coarse_ref, out_ref):
@@ -364,8 +437,8 @@
     def to_next_pair(value):
         return between_tiles(value, lambda t: 2 - 4 * (t % 2))
 
-    slots, pooled, pair_key, pair_value, far_key, far_value = pack(
-        coarse_query, coarse_key, coarse_value, fine_key, fine_value, groups, tiles_across
+    slots, pooled, pair_key, far_key, pair_value, far_value, *rest = pack(
+        head_reach, coarse_query, coarse_key, coarse_value, fine_key, fine_value, groups, tiles_across
     )
     pieces = [pooled] + over_blocks(pooled)
     far_value = to_pair(far_value)
@@ -373,7 +446,8 @@
     received = exchange(slots)
     token_part = split_pooled(pieces)
     pieces = [token_part] + over_outer(token_part)
-    tokens = jnp.concatenate(pieces, axis=0)
+    third = token_part.shape[0] // 3
+    tokens = jnp.concatenate([p[k * third : (k + 1) * third] for k in range(3) for p in pieces], axis=0)
     all_tokens = [tokens] + over_inner(tokens)
     coarse_rows = coarse_query.shape[0]
     coarse_keys = received[:, coarse_rows:]
@@ -381,12 +455,18 @@
     pair_value = to_pair(pair_value)
     far_value = to_next_pair(far_value)
     far_key = to_far(far_key)
-    halo = (pair_key, pair_value, far_key, far_value)
-    cross_result = attend_cross(fine_query, all_tokens, token_part.shape[0])
+    rest = lax.cond(
+        jnp.sum((head_reach > 1).astype(jnp.int32)) > sent_wide(head_count),
+        lambda pair, far: (to_pair(pair), to_far(far)),
+        lambda pair, far: (pair, far),
+        *rest,
+    )
+    halo = (pair_key, far_key, pair_value, far_value)
+    cross_result = attend_cross(fine_query, all_tokens)
     attended = attend_coarse(received, others)
     returned = exchange(attended)
     head_reach, cross_result = lax.optimization_barrier((head_reach, cross_result))
-    window = attend_window(head_reach, fine_query, fine_key, fine_value, halo, tiles_across)
+    window = attend_window(head_reach, fine_query, fine_key, fine_value, halo, rest, tiles_across)
     fine_result = finish(window, returned)
     return (fine_result, cross_result)
 

time: 74.7 us -> 84.6 us (1.13)
  the two profiles are of different devices: /device:TPU:0 before, /device:TPU:11 now
where the time goes in v4:
time: 84.6 us; the launch traced here: 83.8 us
  waiting for transfers between devices  38.4 us (45%)
  starting transfers between devices  29.2 us (35%)
  Pallas kernels  14 us (17%)
  between operations  1.53 us (2%)
    ppermute x6, waiting for transfers between devices, around(): moved.append(lax.ppermute(value, 'seq', links))  28 us
    all_to_all x2, starting transfers between devices, exchange(): lax.all_to_all(slots, 'seq', 0, 0, tiled=True, axis_index_groups=same_block)  14.6 us
    ppermute x5, waiting for transfers between devices, between_tiles(): return lax.ppermute(value, 'seq', links)  10.4 us
    ppermute x5, starting transfers between devices, between_tiles(): return lax.ppermute(value, 'seq', links)  7.75 us
    ppermute x6, starting transfers between devices, around(): moved.append(lax.ppermute(value, 'seq', links))  6.86 us
    pallas_call x1, Pallas kernels, attend_window(): pl.pallas_call(functools.partial(window_kernel, tiles_across), out_shape=...  4.59 us
    pallas_call x1, Pallas kernels, attend_cross(): pl.pallas_call(cross_kernel, out_shape=jax.ShapeDtypeStruct(fine_query.sh...  3.69 us
    pallas_call x1, Pallas kernels, pack(): pl.pallas_call(functools.partial(pack_kernel, tiles_across), out_shape=(p...  2.87 us
  transfers between devices with their start and end apart: 13, of which 4 were waited for; matrix products, arithmetic and copies ran while one was open for 1% of the time, Pallas kernels for 12%

profile of v4, /device:TPU:11, one launch (start us, length us, event | category | flops | bytes accessed | tf_op | source)
XLA Modules:
  0.0 83.8 jit_solution(7859490362256222683)
XLA Ops:
  0.6 2.9 %pack.1 = (bf16[8,96,384]{2,1,0:T(8,128)(2,1)}, f32[8,3072]{1,0:T(8,128)S(1)}, bf16[32,5120]{1,0:T(8,128)(2,1)}, bf16[32,5120]{1,0:T(8,128)(2,1)}, bf16[32,5120]...) custom-call(s32[24]{0:T(128)} %reach, ...), custom_call_target="tpu_custom_call" | custom-call | tf_op jit(solution)/shard_map/pack/pallas_call | solution.py:177
  3.5 0.3 collective-permute-start.2
  3.8 5.9 %all-to-all-start = ((bf16[8,96,384]{2,1,0:T(8,128)(2,1)}), bf16[8,96,384]{2,1,0:T(8,128)(2,1)S(1)}, u32[]{:S(2)}, u32[]{:S(2)}) async-start(bf16[8,96,384]{2,1,0:T(8,128)(2,1)} %get-tuple-element.34), calls=%async_computation | async-start | bytes 1179648 | tf_op jit(solution)/shard_map/all_to_all | solution.py:419
  9.7 1.2 %collective-permute-start.10 = (bf16[32,5120]{1,0:T(8,128)(2,1)}, bf16[32,5120]{1,0:T(8,128)(2,1)}, u32[]{:S(2)}, u32[]{:S(2)}) collective-permute-start(bf16[32,5120]{1,0:T(8,128)(2,1)} %get-tuple-element.29), channel_id=1, source_target_pairs={{0,2},{1,3},{2,0},{3,1},{4,6},{5,7},{6,4},{7,5},{8,10},{9,11},{10,... | collective-permute-start | bytes 983048 | tf_op jit(solution)/shard_map/ppermute | solution.py:429
  10.9 0.0 collective-permute-done.2.refs_1_
  11.0 0.2 collective-permute-start.5
  11.1 2.3 %collective-permute-start.4 = (bf16[24,3072]{1,0:T(8,128)(2,1)S(1)}, bf16[24,3072]{1,0:T(8,128)(2,1)S(1)}, u32[]{:S(2)}, u32[]{:S(2)}) collective-permute-start(bf16[24,3072]{1,0:T(8,128)(2,1)S(1)} %split_pooled.1), channel_id=1, source_target_pairs={{0,8},{1,9},{2,10},{3,11},{4,12},{5,13},{6,14},{7,15},{8,0},{9,1},... | collective-permute-start | bytes 442376 | tf_op jit(solution)/shard_map/ppermute | solution.py:410
  13.4 2.1 %collective-permute-start.3 = (bf16[24,3072]{1,0:T(8,128)(2,1)S(1)}, bf16[24,3072]{1,0:T(8,128)(2,1)S(1)}, u32[]{:S(2)}, u32[]{:S(2)}) collective-permute-start(bf16[24,3072]{1,0:T(8,128)(2,1)S(1)} %split_pooled.1), channel_id=1, source_target_pairs={{0,4},{1,5},{2,6},{3,7},{4,8},{5,9},{6,10},{7,11},{8,12},{9,13},{1... | collective-permute-start | bytes 442376 | tf_op jit(solution)/shard_map/ppermute | solution.py:410
  15.5 20.0 %collective-permute-done.3 = bf16[24,3072]{1,0:T(8,128)(2,1)S(1)} collective-permute-done((bf16[24,3072]{1,0:T(8,128)(2,1)S(1)}, bf16[24,3072]{1,0:T(8,128)(2,1)S(1)}, u32[]{:S(2)}, u32[]{:S(2)}) %collective-permute-start.3) | collective-permute-done | bytes 147488 | tf_op jit(solution)/shard_map/ppermute | solution.py:410
  35.5 0.0 collective-permute-done.4
  35.5 0.0 collective-permute-done.5
  35.5 0.0 copy-start
  35.5 0.0 copy-start.1
  35.5 0.0 copy-start.2
  35.6 0.0 copy-start.4
  35.6 0.0 copy-start.3
  35.7 0.0 all-to-all-done.own_ref
  35.7 1.3 %collective-permute-start.12 = (bf16[8,64,384]{2,1,0:T(8,128)(2,1)S(1)}, bf16[8,64,384]{2,1,0:T(8,128)(2,1)S(1)}, u32[]{:S(2)}, u32[]{:S(2)}) collective-permute-start(bf16[8,64,384]{2,1,0:T(8,128)(2,1)S(1)} %slice.64), channel_id=1, source_target_pairs={{0,2},{1,3},{2,0},{3,1},{4,6},{5,7},{6,4},{7,5},{8,10},{9,11},{10,... | collective-permute-start | bytes 1179656 | tf_op jit(solution)/shard_map/ppermute | solution.py:410
  37.0 0.8 collective-permute-start.6
  37.8 0.3 collective-permute-start.7
  38.0 8.0 %collective-permute-done.12.refs_0_ = bf16[8,64,384]{2,1,0:T(8,128)(2,1)S(1)} collective-permute-done((bf16[8,64,384]{2,1,0:T(8,128)(2,1)S(1)}, bf16[8,64,384]{2,1,0:T(8,128)(2,1)S(1)}, u32[]{:S(2)}, u32[]{:S(2)}) %collective-permute-start.12) | collective-permute-done | bytes 393248 | tf_op jit(solution)/shard_map/ppermute | solution.py:410
  46.0 1.6 %attend_coarse.1 = bf16[8,32,384]{2,1,0:T(8,128)(2,1)} custom-call(bf16[8,96,384]{2,1,0:T(8,128)(2,1)S(1)} %all-to-all-done.own_ref, bf16[8,64,384]{2,1,0:T(8,128)(2,1)S(1)} %collective-permute-done.12.refs_0_), custom_call_target="tpu_custom_call" | custom-call | tf_op jit(solution)/shard_map/attend_coarse/pallas_call | solution.py:244
  47.6 8.7 %all-to-all-start.1 = ((bf16[8,32,384]{2,1,0:T(8,128)(2,1)}), bf16[8,32,384]{2,1,0:T(8,128)(2,1)S(1)}, u32[]{:S(2)}, u32[]{:S(2)}) async-start(bf16[8,32,384]{2,1,0:T(8,128)(2,1)} %attend_coarse.1), calls=%async_computation.1 | async-start | bytes 393216 | tf_op jit(solution)/shard_map/all_to_all | solution.py:419
  56.2 0.0 copy-done
  56.3 0.6 fusion
  57.5 0.0 copy-done.1
  57.5 0.0 copy-done.2
  57.6 0.0 copy-done.4
  57.6 4.0 %collective-permute-start.8 = (bf16[32,5120]{1,0:T(8,128)(2,1)S(1)}, bf16[32,5120]{1,0:T(8,128)(2,1)S(1)}, u32[]{:S(2)}, u32[]{:S(2)}) collective-permute-start(bf16[32,5120]{1,0:T(8,128)(2,1)S(1)} %copy-done.4), channel_id=1, source_target_pairs={{2,4},{3,5},{4,2},{5,3},{6,8},{7,9},{8,6},{9,7},{10,12},{11,13},{1... | collective-permute-start | bytes 983048 | tf_op jit(solution)/shard_map/ppermute | solution.py:429
  61.6 0.0 copy-done.3
  61.6 0.1 collective-permute-start.9
  61.7 0.0 collective-permute-done.10
  61.7 2.2 %collective-permute-start.11 = (bf16[32,5120]{1,0:T(8,128)(2,1)}, bf16[32,5120]{1,0:T(8,128)(2,1)S(1)}, u32[]{:S(2)}, u32[]{:S(2)}) collective-permute-start(bf16[32,5120]{1,0:T(8,128)(2,1)} %collective-permute-done.10), channel_id=1, source_target_pairs={{0,4},{1,5},{4,8},{5,9},{6,2},{7,3},{8,12},{9,13},{10,6},{11,7},{1... | collective-permute-start | bytes 983048 | tf_op jit(solution)/shard_map/ppermute | solution.py:429
  63.9 0.0 collective-permute-done.6.refs_1_
  63.9 3.7 %attend_cross.1 = bf16[128,3072]{1,0:T(8,128)(2,1)} custom-call(bf16[128,3072]{1,0:T(8,128)(2,1)} %refs_0_.1, bf16[96,3072]{1,0:T(8,128)(2,1)S(1)} %slice_dynamic-update-slice_fusion.refs_0_, bf16[96,3072]{1,0:T(8,128)(2,1)S(1)} %collective-permute-done.6.refs_1_), custom_call_target="tpu_custom_call" | custom-call | tf_op jit(solution)/shard_map/attend_cross/pallas_call | solution.py:271
  67.6 0.0 collective-permute-done.7.refs_3_
  67.6 3.4 %collective-permute-done.8.refs_4_ = bf16[32,5120]{1,0:T(8,128)(2,1)S(1)} collective-permute-done((bf16[32,5120]{1,0:T(8,128)(2,1)S(1)}, bf16[32,5120]{1,0:T(8,128)(2,1)S(1)}, u32[]{:S(2)}, u32[]{:S(2)}) %collective-permute-start.8) | collective-permute-done | bytes 327712 | tf_op jit(solution)/shard_map/ppermute | solution.py:429
  71.0 7.0 %collective-permute-done.9.refs_5_ = bf16[32,5120]{1,0:T(8,128)(2,1)S(1)} collective-permute-done((bf16[32,5120]{1,0:T(8,128)(2,1)S(1)}, bf16[32,5120]{1,0:T(8,128)(2,1)S(1)}, u32[]{:S(2)}, u32[]{:S(2)}) %collective-permute-start.9) | collective-permute-done | bytes 327712 | tf_op jit(solution)/shard_map/ppermute | solution.py:429
  78.0 0.0 collective-permute-done.11.refs_6_
  78.0 4.6 %attend_window.1.window_ref = f32[128,3072]{1,0:T(8,128)S(1)} custom-call(s32[24]{0:T(128)S(1)} %copy-done, bf16[128,3072]{1,0:T(8,128)(2,1)} %refs_0_.1, bf16[128,3072]{1,0:T(8,128)(2,1)} %refs_1_.1, bf16[128,3072]{1,0:T(8,128)(2,1)} %refs_2_.1, bf16[32,5120]{1,0:T(8,128)(2,1)S(1)} %collective-permute-done.7.refs_3_, ...), custom_call_target="tpu_custom_call" | custom-call | tf_op jit(solution)/shard_map/attend_window/pallas_call | solution.py:347
  82.6 0.0 all-to-all-done.1.coarse_ref
  82.6 1.2 %finish.1 = bf16[128,3072]{1,0:T(8,128)(2,1)} custom-call(f32[128,3072]{1,0:T(8,128)S(1)} %attend_window.1.window_ref, bf16[8,32,384]{2,1,0:T(8,128)(2,1)S(1)} %all-to-all-done.1.coarse_ref), custom_call_target="tpu_custom_call" | custom-call | tf_op jit(solution)/shard_map/finish/pallas_call | solution.py:379
  (15 shorter events, 0.1 us)
Async XLA Ops:
  3.5 7.4 %collective-permute-start.2 = (f32[8,3072]{1,0:T(8,128)S(1)}, f32[8,3072]{1,0:T(8,128)S(1)}, u32[]{:S(2)}, u32[]{:S(2)}) collective-permute-start(f32[8,3072]{1,0:T(8,128)S(1)} %get-tuple-element.24.refs_0_), channel_id=1, source_target_pairs={{0,2},{1,3},{2,0},{3,1},{4,6},{5,7},{6,4},{7,5},{8,10},{9,11},{10,... | collective-permute-start | bytes 294920 | tf_op jit(solution)/shard_map/ppermute | solution.py:410
  3.8 31.8 %all-to-all-start = ((bf16[8,96,384]{2,1,0:T(8,128)(2,1)}), bf16[8,96,384]{2,1,0:T(8,128)(2,1)S(1)}, u32[]{:S(2)}, u32[]{:S(2)}) async-start(bf16[8,96,384]{2,1,0:T(8,128)(2,1)} %get-tuple-element.34), calls=%async_computation | async-start | bytes 1179648 | tf_op jit(solution)/shard_map/all_to_all | solution.py:419
  9.7 52.0 %collective-permute-start.10 = (bf16[32,5120]{1,0:T(8,128)(2,1)}, bf16[32,5120]{1,0:T(8,128)(2,1)}, u32[]{:S(2)}, u32[]{:S(2)}) collective-permute-start(bf16[32,5120]{1,0:T(8,128)(2,1)} %get-tuple-element.29), channel_id=1, source_target_pairs={{0,2},{1,3},{2,0},{3,1},{4,6},{5,7},{6,4},{7,5},{8,10},{9,11},{10,... | collective-permute-start | bytes 983048 | tf_op jit(solution)/shard_map/ppermute | solution.py:429
  11.0 24.5 %collective-permute-start.5 = (bf16[24,3072]{1,0:T(8,128)(2,1)S(1)}, bf16[24,3072]{1,0:T(8,128)(2,1)S(1)}, u32[]{:S(2)}, u32[]{:S(2)}) collective-permute-start(bf16[24,3072]{1,0:T(8,128)(2,1)S(1)} %split_pooled.1), channel_id=1, source_target_pairs={{0,12},{1,13},{2,14},{3,15},{4,0},{5,1},{6,2},{7,3},{8,4},{9,5},{1... | collective-permute-start | bytes 442376 | tf_op jit(solution)/shard_map/ppermute | solution.py:410
  11.1 24.4 %collective-permute-start.4 = (bf16[24,3072]{1,0:T(8,128)(2,1)S(1)}, bf16[24,3072]{1,0:T(8,128)(2,1)S(1)}, u32[]{:S(2)}, u32[]{:S(2)}) collective-permute-start(bf16[24,3072]{1,0:T(8,128)(2,1)S(1)} %split_pooled.1), channel_id=1, source_target_pairs={{0,8},{1,9},{2,10},{3,11},{4,12},{5,13},{6,14},{7,15},{8,0},{9,1},... | collective-permute-start | bytes 442376 | tf_op jit(solution)/shard_map/ppermute | solution.py:410
  13.4 22.1 %collective-permute-start.3 = (bf16[24,3072]{1,0:T(8,128)(2,1)S(1)}, bf16[24,3072]{1,0:T(8,128)(2,1)S(1)}, u32[]{:S(2)}, u32[]{:S(2)}) collective-permute-start(bf16[24,3072]{1,0:T(8,128)(2,1)S(1)} %split_pooled.1), channel_id=1, source_target_pairs={{0,4},{1,5},{2,6},{3,7},{4,8},{5,9},{6,10},{7,11},{8,12},{9,13},{1... | collective-permute-start | bytes 442376 | tf_op jit(solution)/shard_map/ppermute | solution.py:410
  35.5 20.7 %copy-start = (s32[24]{0:T(128)S(1)}, s32[24]{0:T(128)}, u32[]{:S(2)}) copy-start(s32[24]{0:T(128)} %reach) | copy-start | bytes 292
  35.5 22.0 %copy-start.1 = (bf16[32,2048]{1,0:T(8,128)(2,1)S(1)}, bf16[32,2048]{1,0:T(8,128)(2,1)}, u32[]{:S(2)}) copy-start(bf16[32,2048]{1,0:T(8,128)(2,1)} %get-tuple-element.31) | copy-start | bytes 393220
  35.5 22.0 %copy-start.2 = (bf16[32,2048]{1,0:T(8,128)(2,1)S(1)}, bf16[32,2048]{1,0:T(8,128)(2,1)}, u32[]{:S(2)}) copy-start(bf16[32,2048]{1,0:T(8,128)(2,1)} %get-tuple-element.30) | copy-start | bytes 393220
  35.6 21.9 %copy-start.4 = (bf16[32,5120]{1,0:T(8,128)(2,1)S(1)}, bf16[32,5120]{1,0:T(8,128)(2,1)}, u32[]{:S(2)}) copy-start(bf16[32,5120]{1,0:T(8,128)(2,1)} %get-tuple-element.27) | copy-start | bytes 983044
  35.6 26.0 %copy-start.3 = (bf16[32,5120]{1,0:T(8,128)(2,1)S(1)}, bf16[32,5120]{1,0:T(8,128)(2,1)}, u32[]{:S(2)}) copy-start(bf16[32,5120]{1,0:T(8,128)(2,1)} %get-tuple-element.28) | copy-start | bytes 983044
  35.7 10.3 %collective-permute-start.12 = (bf16[8,64,384]{2,1,0:T(8,128)(2,1)S(1)}, bf16[8,64,384]{2,1,0:T(8,128)(2,1)S(1)}, u32[]{:S(2)}, u32[]{:S(2)}) collective-permute-start(bf16[8,64,384]{2,1,0:T(8,128)(2,1)S(1)} %slice.64), channel_id=1, source_target_pairs={{0,2},{1,3},{2,0},{3,1},{4,6},{5,7},{6,4},{7,5},{8,10},{9,11},{10,... | collective-permute-start | bytes 1179656 | tf_op jit(solution)/shard_map/ppermute | solution.py:410
  37.0 26.9 %collective-permute-start.6 = (bf16[96,3072]{1,0:T(8,128)(2,1)S(1)}, bf16[96,3072]{1,0:T(8,128)(2,1)S(1)}, u32[]{:S(2)}, u32[]{:S(2)}) collective-permute-start(bf16[96,3072]{1,0:T(8,128)(2,1)S(1)} %slice_dynamic-update-slice_fusion.refs_0_), channel_id=1, source_target_pairs={{0,1},{1,0},{2,3},{3,2},{4,5},{5,4},{6,7},{7,6},{8,9},{9,8},{10,11... | collective-permute-start | bytes 1769480 | tf_op jit(solution)/shard_map/ppermute | solution.py:410
  37.8 29.8 %collective-permute-start.7 = (bf16[32,5120]{1,0:T(8,128)(2,1)}, bf16[32,5120]{1,0:T(8,128)(2,1)S(1)}, u32[]{:S(2)}, u32[]{:S(2)}) collective-permute-start(bf16[32,5120]{1,0:T(8,128)(2,1)} %get-tuple-element.26), channel_id=1, source_target_pairs={{0,2},{1,3},{2,0},{3,1},{4,6},{5,7},{6,4},{7,5},{8,10},{9,11},{10,... | collective-permute-start | bytes 983048 | tf_op jit(solution)/shard_map/ppermute | solution.py:429
  47.6 35.0 %all-to-all-start.1 = ((bf16[8,32,384]{2,1,0:T(8,128)(2,1)}), bf16[8,32,384]{2,1,0:T(8,128)(2,1)S(1)}, u32[]{:S(2)}, u32[]{:S(2)}) async-start(bf16[8,32,384]{2,1,0:T(8,128)(2,1)} %attend_coarse.1), calls=%async_computation.1 | async-start | bytes 393216 | tf_op jit(solution)/shard_map/all_to_all | solution.py:419
  57.6 13.4 %collective-permute-start.8 = (bf16[32,5120]{1,0:T(8,128)(2,1)S(1)}, bf16[32,5120]{1,0:T(8,128)(2,1)S(1)}, u32[]{:S(2)}, u32[]{:S(2)}) collective-permute-start(bf16[32,5120]{1,0:T(8,128)(2,1)S(1)} %copy-done.4), channel_id=1, source_target_pairs={{2,4},{3,5},{4,2},{5,3},{6,8},{7,9},{8,6},{9,7},{10,12},{11,13},{1... | collective-permute-start | bytes 983048 | tf_op jit(solution)/shard_map/ppermute | solution.py:429
  61.6 16.4 %collective-permute-start.9 = (bf16[32,5120]{1,0:T(8,128)(2,1)S(1)}, bf16[32,5120]{1,0:T(8,128)(2,1)S(1)}, u32[]{:S(2)}, u32[]{:S(2)}) collective-permute-start(bf16[32,5120]{1,0:T(8,128)(2,1)S(1)} %copy-done.3), channel_id=1, source_target_pairs={{0,2},{1,3},{2,0},{3,1},{4,6},{5,7},{6,4},{7,5},{8,10},{9,11},{10,... | collective-permute-start | bytes 983048 | tf_op jit(solution)/shard_map/ppermute | solution.py:429
  61.7 16.3 %collective-permute-start.11 = (bf16[32,5120]{1,0:T(8,128)(2,1)}, bf16[32,5120]{1,0:T(8,128)(2,1)S(1)}, u32[]{:S(2)}, u32[]{:S(2)}) collective-permute-start(bf16[32,5120]{1,0:T(8,128)(2,1)} %collective-permute-done.10), channel_id=1, source_target_pairs={{0,4},{1,5},{4,8},{5,9},{6,2},{7,3},{8,12},{9,13},{10,6},{11,7},{1... | collective-permute-start | bytes 983048 | tf_op jit(solution)/shard_map/ppermute | solution.py:429

commit v5 on v4

--- a/solution.py
+++ b/solution.py
@@ -27,7 +27,6 @@
 VMEM = pl.BlockSpec(memory_space=pltpu.VMEM)
 SMEM = pl.BlockSpec(memory_space=pltpu.SMEM)
 HBM = pl.BlockSpec(memory_space=pltpu.HBM)
-ANY = pl.BlockSpec(memory_space=pl.ANY)
 
 
 def streamed(value):
@@ -251,6 +250,26 @@
     )(own, *others)
 
 
+def merge_kernel(*refs):
+    *in_refs, out_ref = refs
+    third = in_refs[0].shape[0] // 3
+    parts = [ref[...].astype(jnp.float32) for ref in in_refs]
+    rows = [p[k * third : (k + 1) * third] for k in range(3) for p in parts]
+    out_ref[...] = jnp.concatenate(rows, axis=0).astype(out_ref.dtype)
+
+
+def merge_tokens(pieces):
+    rows, width = pieces[0].shape
+    return pl.pallas_call(
+        merge_kernel,
+        out_shape=jax.ShapeDtypeStruct((rows * len(pieces), width), pieces[0].dtype),
+        in_specs=[VMEM] * len(pieces),
+        out_specs=VMEM,
+        compiler_params=GRANT,
+        name="merge_tokens",
+    )(*pieces)
+
+
 def cross_kernel(query_ref, *refs):
     *token_refs, out_ref = refs
     third = token_refs[0].shape[0] // 3
@@ -266,46 +285,48 @@
 
 
 def attend_cross(fine_query, tokens):
-    rows, width = fine_query.shape
-    columns = width // 2 if width % (2 * HD) == 0 else width
     return pl.pallas_call(
         cross_kernel,
         out_shape=jax.ShapeDtypeStruct(fine_query.shape, jnp.bfloat16),
-        grid=(width // columns,),
-        in_specs=[pl.BlockSpec((t.shape[0], columns), lambda c: (0, c)) for t in (fine_query, *tokens)],
-        out_specs=pl.BlockSpec((rows, columns), lambda c: (0, c)),
+        in_specs=[VMEM] * (1 + len(tokens)),
+        out_specs=VMEM,
         compiler_params=GRANT,
         name="attend_cross",
-    )(streamed(fine_query), *tokens)
-
-
-def window_kernel(tiles_across, reach, *refs):
-    query_hbm, key_hbm, value_hbm, *halo, pair_rest, far_rest, out_ref, held, inner, outer, bias, sem, outer_sem = refs
+    )(*map(resident, (fine_query, *tokens)))
+
+
+def hold_kernel(*refs):
+    count = len(refs) // 2
+    *refs, sem = refs
+    loads = [pltpu.make_async_copy(refs[i], refs[count + i], sem.at[i]) for i in range(count)]
+    for load in loads:
+        load.start()
+    for load in loads:
+        load.wait()
+
+
+def hold(*values):
+    return pl.pallas_call(
+        hold_kernel,
+        out_shape=tuple(pltpu.VMEM(v.shape, v.dtype) for v in values),
+        in_specs=[HBM] * len(values),
+        out_specs=(VMEM,) * len(values),
+        scratch_shapes=[pltpu.SemaphoreType.DMA((len(values),))],
+        compiler_params=GRANT,
+        name="hold",
+    )(*map(streamed, values))
+
+
+def window_kernel(tiles_across, reach, query_ref, key_ref, value_ref, *refs):
+    *halo, pair_rest, far_rest, out_ref, outer, bias = refs
     rows, width = out_ref.shape
     heads = width // HD
     kept = sent_wide(heads) * HD
-    parts = sem.shape[1]
-    columns = width // parts
-    outers = []
     for index in range(4):
-        rest = (pair_rest, far_rest)[index % 2].at[:, pl.ds(index // 2 * (width - kept), width - kept)]
-        outers.append(
-            pltpu.make_async_copy(
-                halo[index].at[:, pl.ds(width, kept)], outer.at[index, :, pl.ds(0, kept)], outer_sem.at[index, 0]
-            )
-        )
-        outers.append(
-            pltpu.make_async_copy(rest, outer.at[index, :, pl.ds(kept, width - kept)], outer_sem.at[index, 1])
-        )
-    for load in outers:
-        load.start()
-    loads = []
-    for part in range(parts):
-        span = pl.ds(part * columns, columns)
-        for index, source in enumerate((query_hbm, key_hbm, value_hbm, *halo)):
-            target = held.at[index] if index < 3 else inner.at[index - 3]
-            loads.append(pltpu.make_async_copy(source.at[:, span], target.at[:, span], sem.at[index, part]))
-            loads[-1].start()
+        rest = (pair_rest, far_rest)[index % 2]
+        start = index // 2 * (width - kept)
+        outer[index, :, :kept] = halo[index][:, width:]
+        outer[index, :, kept:] = rest[:, start : start + width - kept]
     slots = outer_slots(reach, heads)
     total = 2 * rows
     time_tile = lax.axis_index("seq") // tiles_across
@@ -320,46 +341,34 @@
     distance = jnp.where((absolute >= 0) & (absolute < NT * TT), jnp.abs(row_frame - key_frame), FAR)
     for limit in range(HALO_F):
         bias[limit] = jnp.where(distance <= limit + 1, 0.0, MASKED)
-    for load in outers:
-        load.wait()
-    chunk = columns // HD
     for head in range(heads):
-        if head % chunk == 0:
-            for load in loads[head // chunk * 7 : (head // chunk + 1) * 7]:
-                load.wait()
         cut = head_cut(head)
         span = pl.ds(slots[head], HD)
 
         def gathered(own, kind):
-            pieces = [held[own, :, cut]]
+            pieces = [own[:, cut]]
             for side in (kind, kind + 1):
-                pieces += [inner[side, :, cut], outer[side, :, span]]
+                pieces += [halo[side][:, cut], outer[side, :, span]]
             return jnp.concatenate(pieces, axis=0)
 
-        scores = dot_rows(held[0, :, cut], gathered(1, 0)) * SCALE + bias[reach[head] - 1]
-        out_ref[:, cut] = blend(scores, gathered(2, 2))
+        scores = dot_rows(query_ref[:, cut], gathered(key_ref, 0)) * SCALE + bias[reach[head] - 1]
+        out_ref[:, cut] = blend(scores, gathered(value_ref, 2))
 
 
 def attend_window(head_reach, fine_query, fine_key, fine_value, halo, rest, tiles_across):
     rows, width = fine_query.shape
-    kind = fine_query.dtype
-    parts = 4 if width % (4 * HD) == 0 else 1
     return pl.pallas_call(
         functools.partial(window_kernel, tiles_across),
         out_shape=jax.ShapeDtypeStruct((rows, width), jnp.float32),
-        in_specs=[SMEM] + [HBM] * 3 + [ANY] * 6,
+        in_specs=[SMEM] + [VMEM] * 9,
         out_specs=VMEM,
         scratch_shapes=[
-            pltpu.VMEM((3, rows, width), kind),
-            pltpu.VMEM((4, PLANE, width), kind),
-            pltpu.VMEM((4, PLANE, width), kind),
+            pltpu.VMEM((4, PLANE, width), fine_query.dtype),
             pltpu.VMEM((HALO_F, rows, 2 * rows), jnp.float32),
-            pltpu.SemaphoreType.DMA((7, parts)),
-            pltpu.SemaphoreType.DMA((4, 2)),
         ],
         compiler_params=GRANT,
         name="attend_window",
-    )(head_reach, *map(streamed, (fine_query, fine_key, fine_value)), *halo, *rest)
+    )(head_reach, *map(resident, (fine_query, fine_key, fine_value, *halo)), *rest)
 
 
 def finish_kernel(window_ref, coarse_ref, out_ref):
@@ -440,14 +449,14 @@
     slots, pooled, pair_key, far_key, pair_value, far_value, *rest = pack(
         head_reach, coarse_query, coarse_key, coarse_value, fine_key, fine_value, groups, tiles_across
     )
+    fine_query, fine_key, fine_value = hold(fine_query, fine_key, fine_value)
     pieces = [pooled] + over_blocks(pooled)
     far_value = to_pair(far_value)
     pair_key = to_pair(pair_key)
     received = exchange(slots)
     token_part = split_pooled(pieces)
     pieces = [token_part] + over_outer(token_part)
-    third = token_part.shape[0] // 3
-    tokens = jnp.concatenate([p[k * third : (k + 1) * third] for k in range(3) for p in pieces], axis=0)
+    tokens = merge_tokens(pieces)
     all_tokens = [tokens] + over_inner(tokens)
     coarse_rows = coarse_query.shape[0]
     coarse_keys = received[:, coarse_rows:]

time: 84.6 us -> 72.7 us (0.86)
  waiting for transfers between devices: 38.4 us -> 31.9 us
  starting transfers between devices: 29.2 us -> 26.1 us
  Pallas kernels: 14 us -> 11.7 us
    ppermute x6, waiting for transfers between devices: 28 us -> 8.77 us  [around(): moved.append(lax.ppermute(value, 'seq', links))]
    all_to_all x2, waiting for transfers between devices: 0.01 us -> 13 us  [exchange(): lax.all_to_all(slots, 'seq', 0, 0, tiled=True, axis_index_groups=same_block)]
    all_to_all x2, starting transfers between devices: 14.6 us -> 10.9 us  [exchange(): lax.all_to_all(slots, 'seq', 0, 0, tiled=True, axis_index_groups=same_block)]
    pallas_call x1, Pallas kernels: 4.59 us -> 2.03 us  [attend_window(): pl.pallas_call(functools.partial(window_kernel, tiles_across), out_shape=...]
    pallas_call x0 -> x2, Pallas kernels: none -> 1.68 us  [the longest x1 1.64 us: hold(): pl.pallas_call(hold_kernel, out_shape=tuple((pltpu.VMEM(v.shape, v.dtype)...]
    pallas_call x1, Pallas kernels: 3.69 us -> 2.25 us  [attend_cross(): pl.pallas_call(cross_kernel, out_shape=jax.ShapeDtypeStruct(fine_query.sh...]
  transfers between devices with their start and end apart: 13 -> 13, of which waited for: 4 -> 5; matrix products, arithmetic and copies ran while one was open for 1% -> 1% of each run, Pallas kernels for 12% -> 11%
where the time goes in v5:
time: 72.7 us; the launch traced here: 71.8 us
  waiting for transfers between devices  31.9 us (44%)
  starting transfers between devices  26.1 us (36%)
  Pallas kernels  11.7 us (16%)
  between operations  1.44 us (2%)
    all_to_all x2, waiting for transfers between devices, exchange(): lax.all_to_all(slots, 'seq', 0, 0, tiled=True, axis_index_groups=same_block)  13 us
    all_to_all x2, starting transfers between devices, exchange(): lax.all_to_all(slots, 'seq', 0, 0, tiled=True, axis_index_groups=same_block)  10.9 us
    ppermute x5, waiting for transfers between devices, between_tiles(): return lax.ppermute(value, 'seq', links)  10.2 us
    ppermute x6, waiting for transfers between devices, around(): moved.append(lax.ppermute(value, 'seq', links))  8.77 us
    ppermute x5, starting transfers between devices, between_tiles(): return lax.ppermute(value, 'seq', links)  7.76 us
    ppermute x6, starting transfers between devices, around(): moved.append(lax.ppermute(value, 'seq', links))  7.37 us
    pallas_call x1, Pallas kernels, pack(): pl.pallas_call(functools.partial(pack_kernel, tiles_across), out_shape=(p...  2.87 us
    pallas_call x1, Pallas kernels, attend_cross(): pl.pallas_call(cross_kernel, out_shape=jax.ShapeDtypeStruct(fine_query.sh...  2.25 us
  transfers between devices with their start and end apart: 13, of which 5 were waited for; matrix products, arithmetic and copies ran while one was open for 1% of the time, Pallas kernels for 11%

profile of v5, /device:TPU:11, one launch (start us, length us, event | category | flops | bytes accessed | tf_op | source)
XLA Modules:
  0.0 71.8 jit_solution(3633793595529499348)
XLA Ops:
  0.6 2.9 %pack.1 = (bf16[8,96,384]{2,1,0:T(8,128)(2,1)}, f32[8,3072]{1,0:T(8,128)S(1)}, bf16[32,5120]{1,0:T(8,128)(2,1)}, bf16[32,5120]{1,0:T(8,128)(2,1)}, bf16[32,5120]...) custom-call(s32[24]{0:T(128)} %reach, ...), custom_call_target="tpu_custom_call" | custom-call | tf_op jit(solution)/shard_map/pack/pallas_call | solution.py:176
  3.5 0.0 copy-start.5
  3.5 5.7 %all-to-all-start = ((bf16[8,96,384]{2,1,0:T(8,128)(2,1)}), bf16[8,96,384]{2,1,0:T(8,128)(2,1)S(1)}, u32[]{:S(2)}, u32[]{:S(2)}) async-start(bf16[8,96,384]{2,1,0:T(8,128)(2,1)} %get-tuple-element.40), calls=%async_computation | async-start | bytes 1179648 | tf_op jit(solution)/shard_map/all_to_all | solution.py:428
  9.3 0.3 collective-permute-start.2
  9.5 13.0 %all-to-all-done.own_ref = bf16[8,96,384]{2,1,0:T(8,128)(2,1)S(1)} async-done(((bf16[8,96,384]{2,1,0:T(8,128)(2,1)}), bf16[8,96,384]{2,1,0:T(8,128)(2,1)S(1)}, u32[]{:S(2)}, u32[]{:S(2)}) %all-to-all-start) | async-done | bytes 589856 | tf_op jit(solution)/shard_map/all_to_all | solution.py:428
  22.6 0.0 copy-start
  22.6 0.0 copy-start.1
  22.6 0.0 copy-start.2
  22.6 0.3 collective-permute-start.12
  22.9 0.0 collective-permute-done.2.refs_1_
  22.9 2.7 %collective-permute-start.5 = (bf16[24,3072]{1,0:T(8,128)(2,1)S(1)}, bf16[24,3072]{1,0:T(8,128)(2,1)S(1)}, u32[]{:S(2)}, u32[]{:S(2)}) collective-permute-start(bf16[24,3072]{1,0:T(8,128)(2,1)S(1)} %split_pooled.1.refs_0_), channel_id=1, source_target_pairs={{0,12},{1,13},{2,14},{3,15},{4,0},{5,1},{6,2},{7,3},{8,4},{9,5},{1... | collective-permute-start | bytes 442376 | tf_op jit(solution)/shard_map/ppermute | solution.py:419
  25.6 0.4 collective-permute-start.4
  26.1 2.3 %collective-permute-start.3 = (bf16[24,3072]{1,0:T(8,128)(2,1)S(1)}, bf16[24,3072]{1,0:T(8,128)(2,1)S(1)}, u32[]{:S(2)}, u32[]{:S(2)}) collective-permute-start(bf16[24,3072]{1,0:T(8,128)(2,1)S(1)} %split_pooled.1.refs_0_), channel_id=1, source_target_pairs={{0,4},{1,5},{2,6},{3,7},{4,8},{5,9},{6,10},{7,11},{8,12},{9,13},{1... | collective-permute-start | bytes 442376 | tf_op jit(solution)/shard_map/ppermute | solution.py:419
  28.4 0.0 copy-start.4
  28.4 0.0 copy-start.3
  28.4 1.2 %collective-permute-start.10 = (bf16[32,5120]{1,0:T(8,128)(2,1)}, bf16[32,5120]{1,0:T(8,128)(2,1)}, u32[]{:S(2)}, u32[]{:S(2)}) collective-permute-start(bf16[32,5120]{1,0:T(8,128)(2,1)} %get-tuple-element.35), channel_id=1, source_target_pairs={{0,2},{1,3},{2,0},{3,1},{4,6},{5,7},{6,4},{7,5},{8,10},{9,11},{10,... | collective-permute-start | bytes 983048 | tf_op jit(solution)/shard_map/ppermute | solution.py:438
  29.6 0.0 collective-permute-done.5.refs_3_
  29.6 5.3 %collective-permute-done.4.refs_2_ = bf16[24,3072]{1,0:T(8,128)(2,1)S(1)} collective-permute-done((bf16[24,3072]{1,0:T(8,128)(2,1)S(1)}, bf16[24,3072]{1,0:T(8,128)(2,1)S(1)}, u32[]{:S(2)}, u32[]{:S(2)}) %collective-permute-start.4) | collective-permute-done | bytes 147488 | tf_op jit(solution)/shard_map/ppermute | solution.py:419
  34.9 3.4 %collective-permute-done.3.refs_1_ = bf16[24,3072]{1,0:T(8,128)(2,1)S(1)} collective-permute-done((bf16[24,3072]{1,0:T(8,128)(2,1)S(1)}, bf16[24,3072]{1,0:T(8,128)(2,1)S(1)}, u32[]{:S(2)}, u32[]{:S(2)}) %collective-permute-start.3) | collective-permute-done | bytes 147488 | tf_op jit(solution)/shard_map/ppermute | solution.py:419
  38.4 1.4 %collective-permute-start.6 = (bf16[96,3072]{1,0:T(8,128)(2,1)S(1)}, bf16[96,3072]{1,0:T(8,128)(2,1)S(1)}, u32[]{:S(2)}, u32[]{:S(2)}) collective-permute-start(bf16[96,3072]{1,0:T(8,128)(2,1)S(1)} %merge_tokens.1.refs_0_), channel_id=1, source_target_pairs={{0,1},{1,0},{2,3},{3,2},{4,5},{5,4},{6,7},{7,6},{8,9},{9,8},{10,11... | collective-permute-start | bytes 1769480 | tf_op jit(solution)/shard_map/ppermute | solution.py:419
  39.8 0.0 copy-done.5
  39.8 1.2 %collective-permute-start.7 = (bf16[32,5120]{1,0:T(8,128)(2,1)S(1)}, bf16[32,5120]{1,0:T(8,128)(2,1)S(1)}, u32[]{:S(2)}, u32[]{:S(2)}) collective-permute-start(bf16[32,5120]{1,0:T(8,128)(2,1)S(1)} %copy-done.5), channel_id=1, source_target_pairs={{0,2},{1,3},{2,0},{3,1},{4,6},{5,7},{6,4},{7,5},{8,10},{9,11},{10,... | collective-permute-start | bytes 983048 | tf_op jit(solution)/shard_map/ppermute | solution.py:438
  41.0 0.0 collective-permute-done.12.refs_0_
  41.0 1.6 %attend_coarse.1 = bf16[8,32,384]{2,1,0:T(8,128)(2,1)} custom-call(bf16[8,96,384]{2,1,0:T(8,128)(2,1)S(1)} %all-to-all-done.own_ref, bf16[8,64,384]{2,1,0:T(8,128)(2,1)S(1)} %collective-permute-done.12.refs_0_), custom_call_target="tpu_custom_call" | custom-call | tf_op jit(solution)/shard_map/attend_coarse/pallas_call | solution.py:243
  42.5 5.2 %all-to-all-start.1 = ((bf16[8,32,384]{2,1,0:T(8,128)(2,1)}), bf16[8,32,384]{2,1,0:T(8,128)(2,1)S(1)}, u32[]{:S(2)}, u32[]{:S(2)}) async-start(bf16[8,32,384]{2,1,0:T(8,128)(2,1)} %attend_coarse.1), calls=%async_computation.1 | async-start | bytes 393216 | tf_op jit(solution)/shard_map/all_to_all | solution.py:428
  47.7 0.0 copy-done
  47.7 0.6 fusion
  49.0 0.0 copy-done.1
  49.0 0.0 copy-done.2
  49.0 0.0 copy-done.4
  49.1 3.1 %collective-permute-start.8 = (bf16[32,5120]{1,0:T(8,128)(2,1)S(1)}, bf16[32,5120]{1,0:T(8,128)(2,1)S(1)}, u32[]{:S(2)}, u32[]{:S(2)}) collective-permute-start(bf16[32,5120]{1,0:T(8,128)(2,1)S(1)} %copy-done.4), channel_id=1, source_target_pairs={{2,4},{3,5},{4,2},{5,3},{6,8},{7,9},{8,6},{9,7},{10,12},{11,13},{1... | collective-permute-start | bytes 983048 | tf_op jit(solution)/shard_map/ppermute | solution.py:438
  52.1 0.0 copy-done.3
  52.1 0.2 collective-permute-start.9
  52.3 0.0 collective-permute-done.10
  52.3 2.1 %collective-permute-start.11 = (bf16[32,5120]{1,0:T(8,128)(2,1)}, bf16[32,5120]{1,0:T(8,128)(2,1)S(1)}, u32[]{:S(2)}, u32[]{:S(2)}) collective-permute-start(bf16[32,5120]{1,0:T(8,128)(2,1)} %collective-permute-done.10), channel_id=1, source_target_pairs={{0,4},{1,5},{4,8},{5,9},{6,2},{7,3},{8,12},{9,13},{10,6},{11,7},{1... | collective-permute-start | bytes 983048 | tf_op jit(solution)/shard_map/ppermute | solution.py:438
  54.4 1.6 %hold.1 = (bf16[128,3072]{1,0:T(8,128)(2,1)S(1)}, bf16[128,3072]{1,0:T(8,128)(2,1)S(1)}, bf16[128,3072]{1,0:T(8,128)(2,1)S(1)}) custom-call(bf16[128,3072]{1,0:T(8,128)(2,1)} %refs_0_.1, bf16[128,3072]{1,0:T(8,128)(2,1)} %fine_key_hbm.1, bf16[128,3072]{1,0:T(8,128)(2,1)} %fine_value_hbm.1), custom_call_target="tpu_custom_call" | custom-call | tf_op jit(solution)/shard_map/hold/pallas_call | solution.py:309
  56.1 0.0 collective-permute-done.6.refs_1_
  56.1 2.3 %attend_cross.1 = bf16[128,3072]{1,0:T(8,128)(2,1)} custom-call(bf16[128,3072]{1,0:T(8,128)(2,1)S(1)} %get-tuple-element.27.query_ref, bf16[96,3072]{1,0:T(8,128)(2,1)S(1)} %merge_tokens.1.refs_0_, bf16[96,3072]{1,0:T(8,128)(2,1)S(1)} %collective-permute-done.6.refs_1_), custom_call_target="tpu_custom_call" | custom-call | tf_op jit(solution)/shard_map/attend_cross/pallas_call | solution.py:288
  58.3 0.0 collective-permute-done.7.refs_0_
  58.3 2.4 %collective-permute-done.8.refs_1_ = bf16[32,5120]{1,0:T(8,128)(2,1)S(1)} collective-permute-done((bf16[32,5120]{1,0:T(8,128)(2,1)S(1)}, bf16[32,5120]{1,0:T(8,128)(2,1)S(1)}, u32[]{:S(2)}, u32[]{:S(2)}) %collective-permute-start.8) | collective-permute-done | bytes 327712 | tf_op jit(solution)/shard_map/ppermute | solution.py:438
  60.8 7.7 %collective-permute-done.9.refs_2_ = bf16[32,5120]{1,0:T(8,128)(2,1)S(1)} collective-permute-done((bf16[32,5120]{1,0:T(8,128)(2,1)S(1)}, bf16[32,5120]{1,0:T(8,128)(2,1)S(1)}, u32[]{:S(2)}, u32[]{:S(2)}) %collective-permute-start.9) | collective-permute-done | bytes 327712 | tf_op jit(solution)/shard_map/ppermute | solution.py:438
  68.5 0.0 collective-permute-done.11.refs_3_
  68.5 2.0 %attend_window.1.window_ref = f32[128,3072]{1,0:T(8,128)S(1)} custom-call(s32[24]{0:T(128)S(1)} %copy-done, bf16[128,3072]{1,0:T(8,128)(2,1)S(1)} %get-tuple-element.27.query_ref, bf16[128,3072]{1,0:T(8,128)(2,1)S(1)} %get-tuple-element.30.key_ref, bf16[128,3072]{1,0:T(8,128)(2,1)S(1)} %get-tuple-element.31.value_ref, ...), custom_call_target="tpu_custom_call" | custom-call | tf_op jit(solution)/shard_map/attend_window/pallas_call | solution.py:360
  70.5 0.0 all-to-all-done.1.coarse_ref
  70.6 1.2 %finish.1 = bf16[128,3072]{1,0:T(8,128)(2,1)} custom-call(f32[128,3072]{1,0:T(8,128)S(1)} %attend_window.1.window_ref, bf16[8,32,384]{2,1,0:T(8,128)(2,1)S(1)} %all-to-all-done.1.coarse_ref), custom_call_target="tpu_custom_call" | custom-call | tf_op jit(solution)/shard_map/finish/pallas_call | solution.py:388
  (4 shorter events, 0.1 us)
Async XLA Ops:
  3.5 36.3 %copy-start.5 = (bf16[32,5120]{1,0:T(8,128)(2,1)S(1)}, bf16[32,5120]{1,0:T(8,128)(2,1)}, u32[]{:S(2)}) copy-start(bf16[32,5120]{1,0:T(8,128)(2,1)} %get-tuple-element.32) | copy-start | bytes 983044
  3.5 19.0 %all-to-all-start = ((bf16[8,96,384]{2,1,0:T(8,128)(2,1)}), bf16[8,96,384]{2,1,0:T(8,128)(2,1)S(1)}, u32[]{:S(2)}, u32[]{:S(2)}) async-start(bf16[8,96,384]{2,1,0:T(8,128)(2,1)} %get-tuple-element.40), calls=%async_computation | async-start | bytes 1179648 | tf_op jit(solution)/shard_map/all_to_all | solution.py:428
  9.3 13.6 %collective-permute-start.2 = (f32[8,3072]{1,0:T(8,128)S(1)}, f32[8,3072]{1,0:T(8,128)S(1)}, u32[]{:S(2)}, u32[]{:S(2)}) collective-permute-start(f32[8,3072]{1,0:T(8,128)S(1)} %get-tuple-element.28.refs_0_), channel_id=1, source_target_pairs={{0,2},{1,3},{2,0},{3,1},{4,6},{5,7},{6,4},{7,5},{8,10},{9,11},{10,... | collective-permute-start | bytes 294920 | tf_op jit(solution)/shard_map/ppermute | solution.py:419
  22.6 25.2 %copy-start = (s32[24]{0:T(128)S(1)}, s32[24]{0:T(128)}, u32[]{:S(2)}) copy-start(s32[24]{0:T(128)} %reach) | copy-start | bytes 292
  22.6 26.5 %copy-start.1 = (bf16[32,2048]{1,0:T(8,128)(2,1)S(1)}, bf16[32,2048]{1,0:T(8,128)(2,1)}, u32[]{:S(2)}) copy-start(bf16[32,2048]{1,0:T(8,128)(2,1)} %get-tuple-element.37) | copy-start | bytes 393220
  22.6 26.5 %copy-start.2 = (bf16[32,2048]{1,0:T(8,128)(2,1)S(1)}, bf16[32,2048]{1,0:T(8,128)(2,1)}, u32[]{:S(2)}) copy-start(bf16[32,2048]{1,0:T(8,128)(2,1)} %get-tuple-element.36) | copy-start | bytes 393220
  22.6 18.4 %collective-permute-start.12 = (bf16[8,64,384]{2,1,0:T(8,128)(2,1)S(1)}, bf16[8,64,384]{2,1,0:T(8,128)(2,1)S(1)}, u32[]{:S(2)}, u32[]{:S(2)}) collective-permute-start(bf16[8,64,384]{2,1,0:T(8,128)(2,1)S(1)} %slice.4), channel_id=1, source_target_pairs={{0,2},{1,3},{2,0},{3,1},{4,6},{5,7},{6,4},{7,5},{8,10},{9,11},{10,... | collective-permute-start | bytes 1179656 | tf_op jit(solution)/shard_map/ppermute | solution.py:419
  22.9 6.6 %collective-permute-start.5 = (bf16[24,3072]{1,0:T(8,128)(2,1)S(1)}, bf16[24,3072]{1,0:T(8,128)(2,1)S(1)}, u32[]{:S(2)}, u32[]{:S(2)}) collective-permute-start(bf16[24,3072]{1,0:T(8,128)(2,1)S(1)} %split_pooled.1.refs_0_), channel_id=1, source_target_pairs={{0,12},{1,13},{2,14},{3,15},{4,0},{5,1},{6,2},{7,3},{8,4},{9,5},{1... | collective-permute-start | bytes 442376 | tf_op jit(solution)/shard_map/ppermute | solution.py:419
  25.6 9.3 %collective-permute-start.4 = (bf16[24,3072]{1,0:T(8,128)(2,1)S(1)}, bf16[24,3072]{1,0:T(8,128)(2,1)S(1)}, u32[]{:S(2)}, u32[]{:S(2)}) collective-permute-start(bf16[24,3072]{1,0:T(8,128)(2,1)S(1)} %split_pooled.1.refs_0_), channel_id=1, source_target_pairs={{0,8},{1,9},{2,10},{3,11},{4,12},{5,13},{6,14},{7,15},{8,0},{9,1},... | collective-permute-start | bytes 442376 | tf_op jit(solution)/shard_map/ppermute | solution.py:419
  26.1 12.3 %collective-permute-start.3 = (bf16[24,3072]{1,0:T(8,128)(2,1)S(1)}, bf16[24,3072]{1,0:T(8,128)(2,1)S(1)}, u32[]{:S(2)}, u32[]{:S(2)}) collective-permute-start(bf16[24,3072]{1,0:T(8,128)(2,1)S(1)} %split_pooled.1.refs_0_), channel_id=1, source_target_pairs={{0,4},{1,5},{2,6},{3,7},{4,8},{5,9},{6,10},{7,11},{8,12},{9,13},{1... | collective-permute-start | bytes 442376 | tf_op jit(solution)/shard_map/ppermute | solution.py:419
  28.4 20.7 %copy-start.4 = (bf16[32,5120]{1,0:T(8,128)(2,1)S(1)}, bf16[32,5120]{1,0:T(8,128)(2,1)}, u32[]{:S(2)}) copy-start(bf16[32,5120]{1,0:T(8,128)(2,1)} %get-tuple-element.33) | copy-start | bytes 983044
  28.4 23.8 %copy-start.3 = (bf16[32,5120]{1,0:T(8,128)(2,1)S(1)}, bf16[32,5120]{1,0:T(8,128)(2,1)}, u32[]{:S(2)}) copy-start(bf16[32,5120]{1,0:T(8,128)(2,1)} %get-tuple-element.34) | copy-start | bytes 983044
  28.4 24.0 %collective-permute-start.10 = (bf16[32,5120]{1,0:T(8,128)(2,1)}, bf16[32,5120]{1,0:T(8,128)(2,1)}, u32[]{:S(2)}, u32[]{:S(2)}) collective-permute-start(bf16[32,5120]{1,0:T(8,128)(2,1)} %get-tuple-element.35), channel_id=1, source_target_pairs={{0,2},{1,3},{2,0},{3,1},{4,6},{5,7},{6,4},{7,5},{8,10},{9,11},{10,... | collective-permute-start | bytes 983048 | tf_op jit(solution)/shard_map/ppermute | solution.py:438
  38.4 17.7 %collective-permute-start.6 = (bf16[96,3072]{1,0:T(8,128)(2,1)S(1)}, bf16[96,3072]{1,0:T(8,128)(2,1)S(1)}, u32[]{:S(2)}, u32[]{:S(2)}) collective-permute-start(bf16[96,3072]{1,0:T(8,128)(2,1)S(1)} %merge_tokens.1.refs_0_), channel_id=1, source_target_pairs={{0,1},{1,0},{2,3},{3,2},{4,5},{5,4},{6,7},{7,6},{8,9},{9,8},{10,11... | collective-permute-start | bytes 1769480 | tf_op jit(solution)/shard_map/ppermute | solution.py:419
  39.8 18.6 %collective-permute-start.7 = (bf16[32,5120]{1,0:T(8,128)(2,1)S(1)}, bf16[32,5120]{1,0:T(8,128)(2,1)S(1)}, u32[]{:S(2)}, u32[]{:S(2)}) collective-permute-start(bf16[32,5120]{1,0:T(8,128)(2,1)S(1)} %copy-done.5), channel_id=1, source_target_pairs={{0,2},{1,3},{2,0},{3,1},{4,6},{5,7},{6,4},{7,5},{8,10},{9,11},{10,... | collective-permute-start | bytes 983048 | tf_op jit(solution)/shard_map/ppermute | solution.py:438
  42.5 28.0 %all-to-all-start.1 = ((bf16[8,32,384]{2,1,0:T(8,128)(2,1)}), bf16[8,32,384]{2,1,0:T(8,128)(2,1)S(1)}, u32[]{:S(2)}, u32[]{:S(2)}) async-start(bf16[8,32,384]{2,1,0:T(8,128)(2,1)} %attend_coarse.1), calls=%async_computation.1 | async-start | bytes 393216 | tf_op jit(solution)/shard_map/all_to_all | solution.py:428
  49.1 11.7 %collective-permute-start.8 = (bf16[32,5120]{1,0:T(8,128)(2,1)S(1)}, bf16[32,5120]{1,0:T(8,128)(2,1)S(1)}, u32[]{:S(2)}, u32[]{:S(2)}) collective-permute-start(bf16[32,5120]{1,0:T(8,128)(2,1)S(1)} %copy-done.4), channel_id=1, source_target_pairs={{2,4},{3,5},{4,2},{5,3},{6,8},{7,9},{8,6},{9,7},{10,12},{11,13},{1... | collective-permute-start | bytes 983048 | tf_op jit(solution)/shard_map/ppermute | solution.py:438
  52.1 16.4 %collective-permute-start.9 = (bf16[32,5120]{1,0:T(8,128)(2,1)S(1)}, bf16[32,5120]{1,0:T(8,128)(2,1)S(1)}, u32[]{:S(2)}, u32[]{:S(2)}) collective-permute-start(bf16[32,5120]{1,0:T(8,128)(2,1)S(1)} %copy-done.3), channel_id=1, source_target_pairs={{0,2},{1,3},{2,0},{3,1},{4,6},{5,7},{6,4},{7,5},{8,10},{9,11},{10,... | collective-permute-start | bytes 983048 | tf_op jit(solution)/shard_map/ppermute | solution.py:438
  52.3 16.2 %collective-permute-start.11 = (bf16[32,5120]{1,0:T(8,128)(2,1)}, bf16[32,5120]{1,0:T(8,128)(2,1)S(1)}, u32[]{:S(2)}, u32[]{:S(2)}) collective-permute-start(bf16[32,5120]{1,0:T(8,128)(2,1)} %collective-permute-done.10), channel_id=1, source_target_pairs={{0,4},{1,5},{4,8},{5,9},{6,2},{7,3},{8,12},{9,13},{10,6},{11,7},{1... | collective-permute-start | bytes 983048 | tf_op jit(solution)/shard_map/ppermute | solution.py:438
